TPU v7x, 512 devices: a whole 4x8x8 slice. The times are simulated.
512 devices in a mesh: seq: 64 (over y, z_lo, core), head: 8 (over x, z_hi).
Axes of the slice: x: 4, y: 8, z: 8 (z_hi: 2, z_lo: 4; z = z_hi * 4 + z_lo), core: 2. Of those that a mesh axis runs over, the one named last changes fastest.
Arguments:
- mixer_query: bfloat16 [16384, 4096], P('seq', 'head'), may hold values from -13 to 13
- mixer_key: bfloat16 [16384, 4096], P('seq', 'head'), may hold values from -6 to 6
- mixer_value: bfloat16 [16384, 4096], P('seq', 'head'), may hold values from -6 to 6
- shift_taps: float32 [8, 4096], P(None, 'head'), may hold values from -2 to 2
- conv_kernel: float32 [4096, 16384], P(('head', 'seq')), may hold values from -2 to 2
- heads_query: bfloat16 [16384, 4096], P('seq', 'head'), may hold values from -6 to 6
- heads_key: bfloat16 [16384, 4096], P('seq', 'head'), may hold values from -6 to 6
- heads_value: bfloat16 [16384, 4096], P('seq', 'head'), may hold values from -6 to 6
- beta_attention: float32 [4096], P('head'), may hold values from 0.5 to 2
- beta_mixer: float32 [4096], P('head'), may hold values from 0.5 to 2
Outputs:
- block_output: bfloat16 [16384, 4096], P('seq', 'head')
All inputs are finite; a program needn't handle non-finite values.
Results may differ from a plain program's by a relative error of at most 0.0053.
Values may be sent and summed in bfloat16 or wider, within the bound.
No kernel may reach another device: no remote copies, remote signals or barrier semaphores. Data moves between devices by JAX's collectives and lax.ppermute only.
A program may use at most 64 MiB of HBM per device.

v0:
```python
import math

import jax
import jax.numpy as jnp
from jax import lax
from jax.sharding import PartitionSpec as P

D = 4096
HD = 128
TAPS = 8
SPAN = 3


exact_mode = lax.Precision.HIGHEST


def shifted_2(block, axis, distance):
    devices = range(lax.axis_size(axis))
    route = [(i - distance, i) for i in devices if i - distance in devices]
    return lax.ppermute(block, axis, route)


def shift_sum(extended, taps, count, axis):
    width = taps.shape[0]
    source = extended.astype(jnp.float32)
    total = jnp.zeros_like(lax.slice_in_dim(source, 0, count, axis=axis))
    for offset in range(width):
        window = lax.slice_in_dim(source, width - 1 - offset, width - 1 - offset + count, axis=axis)
        total = total + jnp.expand_dims(taps[offset], axis) * window
    return total


def angle_table(first_count, second_count, period):
    left = jnp.arange(first_count, dtype=jnp.int32)[:, None]
    right = jnp.arange(second_count, dtype=jnp.int32)[None, :]
    phase = (left * right % period).astype(jnp.float32) * (2.0 * math.pi / period)
    return (jnp.cos(phase), jnp.sin(phase))


def long_conv(signal, kernel):
    number, length = signal.shape
    radix = 128
    upper = length // radix
    outer = 2 * upper
    period = outer * radix
    cos_one, sin_one = angle_table(upper, outer, outer)
    cos_twist, sin_twist = angle_table(outer, radix, period)
    cos_two, sin_two = angle_table(radix, radix, radix)
    stacked = jnp.concatenate([signal, kernel], 0).reshape(2 * number, upper, radix)
    real_a = jnp.einsum("cab,ak->ckb", stacked, cos_one, precision=exact_mode)
    imag_a = -jnp.einsum("cab,ak->ckb", stacked, sin_one, precision=exact_mode)
    real_b = real_a * cos_twist + imag_a * sin_twist
    imag_b = imag_a * cos_twist - real_a * sin_twist
    real_c = jnp.einsum("ckb,bm->ckm", real_b, cos_two, precision=exact_mode) + jnp.einsum(
        "ckb,bm->ckm", imag_b, sin_two, precision=exact_mode
    )
    imag_c = jnp.einsum("ckb,bm->ckm", imag_b, cos_two, precision=exact_mode) - jnp.einsum(
        "ckb,bm->ckm", real_b, sin_two, precision=exact_mode
    )
    real_sig, real_ker = (real_c[:number], real_c[number:])
    imag_sig, imag_ker = (imag_c[:number], imag_c[number:])
    real_prod = real_sig * real_ker - imag_sig * imag_ker
    imag_prod = real_sig * imag_ker + imag_sig * real_ker
    real_z = jnp.einsum("ckm,mb->ckb", real_prod, cos_two, precision=exact_mode) - jnp.einsum(
        "ckm,mb->ckb", imag_prod, sin_two, precision=exact_mode
    )
    imag_z = jnp.einsum("ckm,mb->ckb", imag_prod, cos_two, precision=exact_mode) + jnp.einsum(
        "ckm,mb->ckb", real_prod, sin_two, precision=exact_mode
    )
    real_w = real_z * cos_twist - imag_z * sin_twist
    imag_w = imag_z * cos_twist + real_z * sin_twist
    result = jnp.einsum("ckb,ak->cab", real_w, cos_one, precision=exact_mode) - jnp.einsum(
        "ckb,ak->cab", imag_w, sin_one, precision=exact_mode
    )
    return (result / period).reshape(number, length)


def attend(query, keys, values, first):
    count, width = query.shape
    heads = width // HD
    scale = 1.0 / math.sqrt(HD)
    seen = keys.shape[0]
    query_heads = query.reshape(count, heads, HD)
    key_heads = keys.reshape(seen, heads, HD)
    value_heads = values.reshape(seen, heads, HD)
    scores = (
        jnp.einsum("qhd,khd->hqk", query_heads, key_heads, preferred_element_type=jnp.float32)
        * scale
    )
    query_pos = first + jnp.arange(count, dtype=jnp.int32)
    key_pos = first - (seen - count) + jnp.arange(seen, dtype=jnp.int32)
    visible = (key_pos[None, :] <= query_pos[:, None]) & (key_pos[None, :] >= 0)
    scores = jnp.where(visible[None], scores, -1e30)
    top = jnp.max(scores, axis=2, keepdims=True)
    probs = jnp.exp(scores - top)
    weights = probs.astype(jnp.bfloat16)
    numer = jnp.einsum("hqk,khd->qhd", weights, value_heads, preferred_element_type=jnp.float32)
    total = jnp.sum(probs, axis=2)
    return (numer / jnp.transpose(total)[:, :, None]).reshape(count, width)


def on_device(
    mixer_query,
    mixer_key,
    mixer_value,
    shift_taps,
    conv_kernel,
    heads_query,
    heads_key,
    heads_value,
    beta_attention,
    beta_mixer,
):
    count, width = mixer_key.shape
    edge = mixer_key[count - (TAPS - 1) :]
    before = shifted_2(edge, "seq", 1)
    extended = jnp.concatenate([before, mixer_key], 0)
    shifted = shift_sum(extended, shift_taps, count, 0)
    ssm_input = (shifted * mixer_value.astype(jnp.float32)).astype(jnp.bfloat16)
    signal = lax.all_to_all(
        jnp.transpose(ssm_input), "seq", split_axis=0, concat_axis=1, tiled=True
    )
    filtered = long_conv(signal.astype(jnp.float32), conv_kernel).astype(jnp.bfloat16)
    returned = lax.all_to_all(filtered, "seq", split_axis=1, concat_axis=0, tiled=True)
    mixer_branch = mixer_query.astype(jnp.float32) * jnp.transpose(returned).astype(jnp.float32)
    earlier = []
    carried = (heads_key, heads_value)
    for step in range(SPAN):
        carried = shifted_2((carried[0], carried[1]), "seq", 1)
        earlier.insert(0, carried)
    keys = jnp.concatenate([pair[0] for pair in earlier] + [heads_key], 0)
    values = jnp.concatenate([pair[1] for pair in earlier] + [heads_value], 0)
    first = lax.axis_index("seq") * count
    attention_branch = attend(heads_query, keys, values, first)
    attention_sums, mixer_sums = lax.psum(
        (
            jnp.sum(attention_branch * attention_branch, axis=1),
            jnp.sum(mixer_branch * mixer_branch, axis=1),
        ),
        "head",
    )
    attention_scale = lax.rsqrt(attention_sums / D + 1e-05)
    mixer_scale = lax.rsqrt(mixer_sums / D + 1e-05)
    joined = (
        beta_attention[None, :] * attention_branch * attention_scale[:, None]
        + beta_mixer[None, :] * mixer_branch * mixer_scale[:, None]
    )
    return (joined * 0.5).astype(jnp.bfloat16)


def solution(mesh):
    return jax.shard_map(
        on_device,
        mesh=mesh,
        in_specs=(
            P("seq", "head"),
            P("seq", "head"),
            P("seq", "head"),
            P(None, "head"),
            P(("head", "seq"), None),
            P("seq", "head"),
            P("seq", "head"),
            P("seq", "head"),
            P("head"),
            P("head"),
        ),
        out_specs=P("seq", "head"),
        check_vma=False,
    )
```

profile of v0, /device:TPU:56, one launch (start us, length us, event | category | flops | bytes accessed | tf_op | source)
XLA Modules:
  0.0 127.0 jit_solution(9681265963723368630)
XLA Ops:
  0.9 1.9 %collective-permute-start.6 = (bf16[7,512]{0,1:T(8,128)(2,1)S(1)}, bf16[7,512]{0,1:T(8,128)(2,1)S(1)}, u32[]{:S(2)}, u32[]{:S(2)}) collective-permute-start(bf16[7,512]{0,1:T(8,128)(2,1)S(1)} %copy.26), channel_id=1, source_target_pairs={{0,8},{8,16},{16,24},{24,32},{32,40},{40,48},{48,56},{56,64},{64,7... | collective-permute-start | bytes 21512 | tf_op jit(solution)/shard_map/ppermute | solution.py:20
  2.9 1.1 copy.20
  4.0 4.4 %collective-permute-start.3 = (bf16[256,512]{0,1:T(8,128)(2,1)S(1)}, bf16[256,512]{0,1:T(8,128)(2,1)S(1)}, u32[]{:S(2)}, u32[]{:S(2)}) collective-permute-start(bf16[256,512]{0,1:T(8,128)(2,1)S(1)} %copy.20), channel_id=1, source_target_pairs={{0,8},{8,16},{16,24},{24,32},{32,40},{40,48},{48,56},{56,64},{64,7... | collective-permute-start | bytes 786440 | tf_op jit(solution)/shard_map/ppermute | solution.py:20
  8.3 1.9 %collective-permute-start = (bf16[256,512]{1,0:T(8,128)(2,1)}, bf16[256,512]{1,0:T(8,128)(2,1)S(1)}, u32[]{:S(2)}, u32[]{:S(2)}) collective-permute-start(bf16[256,512]{1,0:T(8,128)(2,1)} %param.17), channel_id=1, source_target_pairs={{0,8},{8,16},{16,24},{24,32},{32,40},{40,48},{48,56},{56,64},{64,7... | collective-permute-start | bytes 786440 | tf_op jit(solution)/shard_map/ppermute | solution.py:20
  10.3 1.0 fusion.162
  11.3 1.1 copy.27
  12.4 1.1 copy.28
  13.7 2.4 %fusion.59 = bf16[64,8,256]{2,1,0:T(8,128)(2,1)} fusion(bf16[256,512]{0,1:T(8,128)(2,1)S(1)} %copy.28, f32[263,512]{0,1:T(8,128)S(1)} %maximum_convert_fusion, f32[512]{0:T(512)S(1)} %bitcast.134, f32[512]{0:T(512)S(1)} %bitcast.135, f32[512]{0:T(512)S(1)} %bitcast.129, f32[512]{0:T(512)S(1)} %bitcast.130, f32[512]{0:T(512)S(1)} %bitcast.131, ...), kind=kLoop, calls=%fused_computation.76 | loop fusion | flops 2359296 | bytes 4734976 | tf_op jit(solution)/shard_map/all_to_all | solution.py:120
  16.1 11.7 %all-to-all-start = ((bf16[64,8,256]{2,1,0:T(8,128)(2,1)}), bf16[64,8,256]{2,1,0:T(8,128)(2,1)S(1)}, u32[]{:S(2)}, u32[]{:S(2)}) async-start(bf16[64,8,256]{2,1,0:T(8,128)(2,1)} %fusion.59), calls=%async_computation | async-start | bytes 524288 | tf_op jit(solution)/shard_map/all_to_all | solution.py:120
  28.9 2.0 %collective-permute-start.4 = (bf16[256,512]{0,1:T(8,128)(2,1)S(1)}, bf16[256,512]{0,1:T(8,128)(2,1)}, u32[]{:S(2)}, u32[]{:S(2)}) collective-permute-start(bf16[256,512]{0,1:T(8,128)(2,1)S(1)} %collective-permute-done.3), channel_id=1, source_target_pairs={{0,8},{8,16},{16,24},{24,32},{32,40},{40,48},{48,56},{56,64},{64,7... | collective-permute-start | bytes 786440 | tf_op jit(solution)/shard_map/ppermute | solution.py:20
  30.9 3.6 %collective-permute-start.1 = (bf16[256,512]{1,0:T(8,128)(2,1)S(1)}, bf16[256,512]{1,0:T(8,128)(2,1)}, u32[]{:S(2)}, u32[]{:S(2)}) collective-permute-start(bf16[256,512]{1,0:T(8,128)(2,1)S(1)} %collective-permute-done), channel_id=1, source_target_pairs={{0,8},{8,16},{16,24},{24,32},{32,40},{40,48},{48,56},{56,64},{64,7... | collective-permute-start | bytes 786440 | tf_op jit(solution)/shard_map/ppermute | solution.py:20
  34.5 5.1 %all-to-all-done = bf16[64,8,256]{2,1,0:T(8,128)(2,1)S(1)} async-done(((bf16[64,8,256]{2,1,0:T(8,128)(2,1)}), bf16[64,8,256]{2,1,0:T(8,128)(2,1)S(1)}, u32[]{:S(2)}, u32[]{:S(2)}) %all-to-all-start) | async-done | bytes 262176 | tf_op jit(solution)/shard_map/all_to_all | solution.py:120
  39.9 2.3 %fusion.67 = f32[256,16,128]{2,0,1:T(8,128)S(1)} fusion(f32[16,128,128]{2,1,0:T(8,128)S(1)} %bitcast.123), kind=kOutput, calls=%fused_computation.90 | convolution fusion | flops 805765120 | bytes 3145728 | tf_op jit(solution)/shard_map/cab,ak->ckb/dot_general | solution.py:51
  42.2 2.3 %fusion.69 = f32[256,16,128]{2,0,1:T(8,128)S(1)} fusion(f32[16,128,128]{2,1,0:T(8,128)S(1)} %bitcast.124), kind=kOutput, calls=%fused_computation.92 | convolution fusion | flops 805765120 | bytes 3145728 | tf_op jit(solution)/shard_map/cab,ak->ckb/dot_general | solution.py:50
  44.5 2.3 %fusion.7 = f32[16,256,128]{2,1,0:T(8,128)S(1)} fusion(f32[256,16,128]{2,0,1:T(8,128)S(1)} %fusion.69, f32[256,16,128]{2,0,1:T(8,128)S(1)} %fusion.67, f32[256,128]{1,0:T(8,128)S(1)} %get-tuple-element.21, f32[256,128]{1,0:T(8,128)S(1)} %get-tuple-element.22), kind=kOutput, calls=%fused_computation.8 | convolution fusion | flops 807632896 | bytes 6553600 | tf_op jit(solution)/shard_map/ckb,bm->ckm/dot_general | solution.py:54
  46.9 2.3 %fusion.5 = f32[16,256,128]{2,1,0:T(8,128)S(1)} fusion(f32[256,16,128]{2,0,1:T(8,128)S(1)} %fusion.69, f32[256,16,128]{2,0,1:T(8,128)S(1)} %fusion.67, f32[256,128]{1,0:T(8,128)S(1)} %get-tuple-element.21, f32[256,128]{1,0:T(8,128)S(1)} %get-tuple-element.22), kind=kOutput, calls=%fused_computation.6 | convolution fusion | flops 807632896 | bytes 6553600 | tf_op jit(solution)/shard_map/ckb,bm->ckm/dot_general | solution.py:57
  49.2 2.2 %fusion.17 = f32[16,256,128]{2,1,0:T(8,128)S(1)} fusion(f32[16,256,128]{2,1,0:T(8,128)S(1)} %fusion.7, f32[256,16,128]{2,0,1:T(8,128)S(1)} %fusion.69, f32[256,16,128]{2,0,1:T(8,128)S(1)} %fusion.67, f32[256,128]{1,0:T(8,128)S(1)} %get-tuple-element.21, f32[256,128]{1,0:T(8,128)S(1)} %get-tuple-element.22), kind=kOutput, calls=%fused_computation.20 | convolution fusion | flops 808157184 | bytes 8650752 | tf_op jit(solution)/shard_map/ckb,bm->ckm/dot_general | solution.py:54
  51.4 2.5 %fusion.20 = f32[16,256,128]{2,1,0:T(8,128)S(1)} fusion(f32[16,256,128]{2,1,0:T(8,128)S(1)} %fusion.5, f32[256,16,128]{2,0,1:T(8,128)S(1)} %fusion.69, f32[256,16,128]{2,0,1:T(8,128)S(1)} %fusion.67, f32[256,128]{1,0:T(8,128)S(1)} %get-tuple-element.21, f32[256,128]{1,0:T(8,128)S(1)} %get-tuple-element.22), kind=kOutput, calls=%fused_computation.21 | convolution fusion | flops 808157184 | bytes 8650752 | tf_op jit(solution)/shard_map/ckb,bm->ckm/dot_general | solution.py:57
  54.2 1.2 fusion.87
  55.4 1.2 fusion.85
  56.6 1.2 convolution_subtract_fusion
  57.9 1.2 convolution_add_fusion
  59.1 1.3 %fusion.32 = f32[128,8,128]{2,0,1:T(8,128)S(1)} fusion(f32[8,256,128]{2,1,0:T(8,128)S(1)} %convolution_add_fusion, f32[8,256,128]{2,1,0:T(8,128)S(1)} %convolution_subtract_fusion, f32[256,128]{1,0:T(8,128)S(1)} %get-tuple-element.21, f32[256,128]{1,0:T(8,128)S(1)} %get-tuple-element.22), kind=kOutput, calls=%fused_computation.35 | convolution fusion | flops 403898368 | bytes 2883584 | tf_op jit(solution)/shard_map/ckb,ak->cab/dot_general | solution.py:72
  60.4 2.4 %collective-permute-start.5 = (bf16[256,512]{0,1:T(8,128)(2,1)}, bf16[256,512]{0,1:T(8,128)(2,1)S(1)}, u32[]{:S(2)}, u32[]{:S(2)}) collective-permute-start(bf16[256,512]{0,1:T(8,128)(2,1)} %collective-permute-done.4), channel_id=1, source_target_pairs={{0,8},{8,16},{16,24},{24,32},{32,40},{40,48},{48,56},{56,64},{64,7... | collective-permute-start | bytes 786440 | tf_op jit(solution)/shard_map/ppermute | solution.py:20
  62.8 1.3 %fusion.28 = bf16[8,128,128]{2,1,0:T(8,128)(2,1)S(1)} fusion(f32[128,8,128]{2,0,1:T(8,128)S(1)} %fusion.32, f32[8,256,128]{2,1,0:T(8,128)S(1)} %convolution_subtract_fusion, f32[8,256,128]{2,1,0:T(8,128)S(1)} %convolution_add_fusion, f32[256,128]{1,0:T(8,128)S(1)} %get-tuple-element.21, f32[256,128]{1,0:T(8,128)S(1)} %get-tuple-element.22), kind=kOutput, calls=%fused_computation.28 | convolution fusion | flops 404291584 | bytes 3145728 | tf_op jit(solution)/shard_map/ckb,ak->cab/dot_general | solution.py:72
  65.0 9.0 %all-to-all-start.1 = ((bf16[8,64,256]{2,0,1:T(8,128)(2,1)}), bf16[8,64,256]{2,0,1:T(8,128)(2,1)S(1)}, u32[]{:S(2)}, u32[]{:S(2)}) async-start(bf16[8,64,256]{2,0,1:T(8,128)(2,1)} %copy.31), calls=%async_computation.1 | async-start | bytes 524288 | tf_op jit(solution)/shard_map/all_to_all | solution.py:124
  74.1 2.3 %collective-permute-start.2 = (bf16[256,512]{1,0:T(8,128)(2,1)}, bf16[256,512]{1,0:T(8,128)(2,1)S(1)}, u32[]{:S(2)}, u32[]{:S(2)}) collective-permute-start(bf16[256,512]{1,0:T(8,128)(2,1)} %collective-permute-done.1), channel_id=1, source_target_pairs={{0,8},{8,16},{16,24},{24,32},{32,40},{40,48},{48,56},{56,64},{64,7... | collective-permute-start | bytes 786440 | tf_op jit(solution)/shard_map/ppermute | solution.py:20
  76.4 1.1 pad_maximum_fusion.1
  80.4 7.0 %collective-permute-done.2 = bf16[256,512]{1,0:T(8,128)(2,1)S(1)} collective-permute-done((bf16[256,512]{1,0:T(8,128)(2,1)}, bf16[256,512]{1,0:T(8,128)(2,1)S(1)}, u32[]{:S(2)}, u32[]{:S(2)}) %collective-permute-start.2) | collective-permute-done | bytes 262176 | tf_op jit(solution)/shard_map/ppermute | solution.py:20
  87.5 1.0 pad_maximum_fusion
  89.1 3.4 %multiply_reduce_fusion.1 = (f32[256]{0:T(256)S(1)}, f32[256,4,128]{0,2,1:T(8,128)S(1)}) fusion(f32[256,4]{0,1:T(4,128)S(1)} %bitcast.136, bf16[1024,4,128]{0,2,1:T(8,128)(2,1)S(1)} %bitcast.127, f32[4,1024,256]{2,1,0:T(8,128)} %copy-done.1, f32[4,256]{1,0:T(4,128)S(1)} %get-tuple-element.17, pred[256,1024]{0,1:T(8,128)(4,1)S(1)} %compare_and_fusion), kind=kOutput, calls=%fused_computation.71 | convolution fusion | flops 273022720 | bytes 6038528 | tf_op jit(solution)/shard_map/hqk,khd->qhd/dot_general | solution.py:97
  92.6 33.3 %all-reduce = (f32[256]{0:T(256)S(1)}, f32[256]{0:T(256)S(1)}) all-reduce(f32[256]{0:T(256)S(1)} %multiply_reduce_fusion, f32[256]{0:T(256)S(1)} %get-tuple-element.19), channel_id=1, replica_groups=mesh['seq'=64,'head'=8] {'head'}, use_global_device_ids=true, to_apply=%region_5.6 | all-reduce | flops 512 | bytes 4096 | tf_op jit(solution)/shard_map/psum | solution.py:135
  (44 shorter events, 8.3 us)
Async XLA Ops:
  0.0 77.5 %copy-start = (bf16[256,512]{1,0:T(8,128)(2,1)S(1)}, bf16[256,512]{1,0:T(8,128)(2,1)}, u32[]{:S(2)}) copy-start(bf16[256,512]{1,0:T(8,128)(2,1)} %param.15) | copy-start | bytes 786436
  0.9 12.6 %collective-permute-start.6 = (bf16[7,512]{0,1:T(8,128)(2,1)S(1)}, bf16[7,512]{0,1:T(8,128)(2,1)S(1)}, u32[]{:S(2)}, u32[]{:S(2)}) collective-permute-start(bf16[7,512]{0,1:T(8,128)(2,1)S(1)} %copy.26), channel_id=1, source_target_pairs={{0,8},{8,16},{16,24},{24,32},{32,40},{40,48},{48,56},{56,64},{64,7... | collective-permute-start | bytes 21512 | tf_op jit(solution)/shard_map/ppermute | solution.py:20
  4.0 24.9 %collective-permute-start.3 = (bf16[256,512]{0,1:T(8,128)(2,1)S(1)}, bf16[256,512]{0,1:T(8,128)(2,1)S(1)}, u32[]{:S(2)}, u32[]{:S(2)}) collective-permute-start(bf16[256,512]{0,1:T(8,128)(2,1)S(1)} %copy.20), channel_id=1, source_target_pairs={{0,8},{8,16},{16,24},{24,32},{32,40},{40,48},{48,56},{56,64},{64,7... | collective-permute-start | bytes 786440 | tf_op jit(solution)/shard_map/ppermute | solution.py:20
  8.3 22.6 %collective-permute-start = (bf16[256,512]{1,0:T(8,128)(2,1)}, bf16[256,512]{1,0:T(8,128)(2,1)S(1)}, u32[]{:S(2)}, u32[]{:S(2)}) collective-permute-start(bf16[256,512]{1,0:T(8,128)(2,1)} %param.17), channel_id=1, source_target_pairs={{0,8},{8,16},{16,24},{24,32},{32,40},{40,48},{48,56},{56,64},{64,7... | collective-permute-start | bytes 786440 | tf_op jit(solution)/shard_map/ppermute | solution.py:20
  13.7 14.6 %copy-start.3 = (bf16[256,512]{1,0:T(8,128)(2,1)S(1)}, bf16[256,512]{1,0:T(8,128)(2,1)}, u32[]{:S(2)}) copy-start(bf16[256,512]{1,0:T(8,128)(2,1)} %param.10) | copy-start | bytes 786436
  16.1 23.5 %copy-start.2 = (f32[8,16384]{1,0:T(8,128)S(1)}, f32[8,16384]{1,0:T(8,128)}, u32[]{:S(2)}) copy-start(f32[8,16384]{1,0:T(8,128)} %param.14) | copy-start | bytes 1572868
  16.1 23.5 %all-to-all-start = ((bf16[64,8,256]{2,1,0:T(8,128)(2,1)}), bf16[64,8,256]{2,1,0:T(8,128)(2,1)S(1)}, u32[]{:S(2)}, u32[]{:S(2)}) async-start(bf16[64,8,256]{2,1,0:T(8,128)(2,1)} %fusion.59), calls=%async_computation | async-start | bytes 524288 | tf_op jit(solution)/shard_map/all_to_all | solution.py:120
  28.9 31.5 %collective-permute-start.4 = (bf16[256,512]{0,1:T(8,128)(2,1)S(1)}, bf16[256,512]{0,1:T(8,128)(2,1)}, u32[]{:S(2)}, u32[]{:S(2)}) collective-permute-start(bf16[256,512]{0,1:T(8,128)(2,1)S(1)} %collective-permute-done.3), channel_id=1, source_target_pairs={{0,8},{8,16},{16,24},{24,32},{32,40},{40,48},{48,56},{56,64},{64,7... | collective-permute-start | bytes 786440 | tf_op jit(solution)/shard_map/ppermute | solution.py:20
  30.9 43.2 %collective-permute-start.1 = (bf16[256,512]{1,0:T(8,128)(2,1)S(1)}, bf16[256,512]{1,0:T(8,128)(2,1)}, u32[]{:S(2)}, u32[]{:S(2)}) collective-permute-start(bf16[256,512]{1,0:T(8,128)(2,1)S(1)} %collective-permute-done), channel_id=1, source_target_pairs={{0,8},{8,16},{16,24},{24,32},{32,40},{40,48},{48,56},{56,64},{64,7... | collective-permute-start | bytes 786440 | tf_op jit(solution)/shard_map/ppermute | solution.py:20
  60.4 16.0 %collective-permute-start.5 = (bf16[256,512]{0,1:T(8,128)(2,1)}, bf16[256,512]{0,1:T(8,128)(2,1)S(1)}, u32[]{:S(2)}, u32[]{:S(2)}) collective-permute-start(bf16[256,512]{0,1:T(8,128)(2,1)} %collective-permute-done.4), channel_id=1, source_target_pairs={{0,8},{8,16},{16,24},{24,32},{32,40},{40,48},{48,56},{56,64},{64,7... | collective-permute-start | bytes 786440 | tf_op jit(solution)/shard_map/ppermute | solution.py:20
  65.0 27.4 %all-to-all-start.1 = ((bf16[8,64,256]{2,0,1:T(8,128)(2,1)}), bf16[8,64,256]{2,0,1:T(8,128)(2,1)S(1)}, u32[]{:S(2)}, u32[]{:S(2)}) async-start(bf16[8,64,256]{2,0,1:T(8,128)(2,1)} %copy.31), calls=%async_computation.1 | async-start | bytes 524288 | tf_op jit(solution)/shard_map/all_to_all | solution.py:124
  74.1 13.4 %collective-permute-start.2 = (bf16[256,512]{1,0:T(8,128)(2,1)}, bf16[256,512]{1,0:T(8,128)(2,1)S(1)}, u32[]{:S(2)}, u32[]{:S(2)}) collective-permute-start(bf16[256,512]{1,0:T(8,128)(2,1)} %collective-permute-done.1), channel_id=1, source_target_pairs={{0,8},{8,16},{16,24},{24,32},{32,40},{40,48},{48,56},{56,64},{64,7... | collective-permute-start | bytes 786440 | tf_op jit(solution)/shard_map/ppermute | solution.py:20
  78.5 1.9 %copy-start.1 = (f32[4,1024,256]{2,1,0:T(8,128)}, f32[4,1024,256]{2,1,0:T(8,128)S(1)}, u32[]{:S(2)}) copy-start(f32[4,1024,256]{2,1,0:T(8,128)S(1)} %get-tuple-element.18) | copy-start | bytes 12582916
  78.5 9.0 %copy-start.4 = (bf16[256,512]{1,0:T(8,128)(2,1)S(1)}, bf16[256,512]{1,0:T(8,128)(2,1)}, u32[]{:S(2)}) copy-start(bf16[256,512]{1,0:T(8,128)(2,1)} %param.17) | copy-start | bytes 786436
  89.0 36.9 %copy-start.5 = (f32[512]{0:T(512)S(1)}, f32[512]{0:T(512)}, u32[]{:S(2)}) copy-start(f32[512]{0:T(512)} %param.19) | copy-start | bytes 6148
  89.0 36.9 %copy-start.6 = (f32[512]{0:T(512)S(1)}, f32[512]{0:T(512)}, u32[]{:S(2)}) copy-start(f32[512]{0:T(512)} %param.18) | copy-start | bytes 6148
where the time goes:
time: 128 us; the launch traced here: 127 us
  starting transfers between devices  39.2 us (31%)
  blocking collectives  33.3 us (26%)
  matrix products  25.8 us (20%)
  waiting for transfers between devices  12.2 us (10%)
  local copies, waits for them, and re-layouts  8.9 us (7%)
  other arithmetic  7.14 us (6%)
    psum x1, blocking collectives, on_device(): lax.psum((jnp.sum(attention_branch * attention_branch, axis=1), jnp.sum(m...  33.3 us
    ppermute x7, starting transfers between devices, shifted_2(): return lax.ppermute(block, axis, route)  18.5 us
    all_to_all x1, starting transfers between devices, on_device(): lax.all_to_all(jnp.transpose(ssm_input), 'seq', split_axis=0, concat_axis...  11.7 us
    all_to_all x1, starting transfers between devices, on_device(): lax.all_to_all(filtered, 'seq', split_axis=1, concat_axis=0, tiled=True)  9.04 us
    ppermute x7, waiting for transfers between devices, shifted_2(): return lax.ppermute(block, axis, route)  7.06 us
    all_to_all x1, waiting for transfers between devices, on_device(): lax.all_to_all(jnp.transpose(ssm_input), 'seq', split_axis=0, concat_axis...  5.09 us
    unnamed x19, local copies, waits for them, and re-layouts  4.63 us
    dot_general x1, matrix products, attend(): jnp.einsum('hqk,khd->qhd', weights, value_heads, preferred_element_type=j...  3.4 us
  transfers between devices with their start and end apart: 9, of which 2 were waited for; matrix products, arithmetic and copies ran while one was open for 30% of the time, Pallas kernels for 0%

commit v1 on v0

v1 whole, which is shorter than its diff:
```python
import math

import jax
import jax.numpy as jnp
import numpy as np
from jax import lax
from jax.experimental import pallas as pl
from jax.experimental.pallas import tpu as pltpu
from jax.sharding import PartitionSpec as P


D = 4096
HD = 128
TAPS = 8
SPAN = 3
RADIX = 128
F32 = jnp.float32
BF16 = jnp.bfloat16


def split_table(table):
    high = table.astype(np.float32).astype(jnp.bfloat16)
    low = (table - high.astype(np.float64)).astype(np.float32).astype(jnp.bfloat16)
    return high, low


def conv_tables(tokens):
    half = tokens // RADIX
    place = np.arange(RADIX)
    order = (place % (RADIX // half)) * half + place // (RADIX // half)
    freq = np.arange(RADIX) + 0.5
    one = 2.0 * np.pi * np.outer(freq, order) / (2 * RADIX)
    first = np.concatenate([np.cos(one), -np.sin(one)], 0)
    last = np.concatenate([np.cos(one), -np.sin(one)], 0).T * (1.0 / (RADIX * RADIX))
    first_natural = 2.0 * np.pi * np.outer(freq, place) / (2 * RADIX)
    first_natural = np.concatenate([np.cos(first_natural), -np.sin(first_natural)], 0)
    twist = 2.0 * np.pi * np.outer(freq, place) / (2 * RADIX * RADIX)
    two = 2.0 * np.pi * np.outer(place, place) / RADIX
    cos, sin = np.cos(two), np.sin(two)
    ahead = np.block([[cos, -sin], [sin, cos]])
    back = np.block([[cos, sin], [-sin, cos]])
    return dict(
        first=split_table(first),
        first_natural=split_table(first_natural),
        last=split_table(last),
        ahead=split_table(ahead),
        back=split_table(back),
        twist_cos=np.cos(twist).astype(np.float32),
        twist_sin=np.sin(twist).astype(np.float32),
    )


def halves(value):
    high = value.astype(BF16)
    return high, (value - high.astype(F32)).astype(BF16)


def mm(left, right):
    return lax.dot_general(left, right, (((1,), (0,)), ((), ())), preferred_element_type=F32)


def kernel_call(body, out_shape, scratch=(), vmem=None):
    def call(*args):
        return pl.pallas_call(
            body,
            out_shape=out_shape,
            scratch_shapes=list(scratch),
            compiler_params=pltpu.CompilerParams(vmem_limit_bytes=vmem or 48 * 2**20),
        )(*args)

    return call


def shift_body(before_ref, key_ref, value_ref, taps_ref, out_ref, ext_ref):
    count, _ = key_ref.shape
    ext_ref[0:8, :] = before_ref[...].astype(F32)
    ext_ref[8:, :] = key_ref[...].astype(F32)
    taps = taps_ref[...]
    total = taps[0:1, :] * ext_ref[8 : 8 + count, :]
    for j in range(1, TAPS):
        total = total + taps[j : j + 1, :] * ext_ref[8 - j : 8 - j + count, :]
    product = total * value_ref[...].astype(F32)
    out_ref[...] = product.T.astype(BF16).reshape(out_ref.shape)


def spectrum(first_step, twist_cos, twist_sin, ahead_hi, ahead_lo):
    real, imag = first_step[:RADIX], first_step[RADIX:]
    turned = jnp.concatenate(
        [real * twist_cos + imag * twist_sin, imag * twist_cos - real * twist_sin], 1
    )
    high, low = halves(turned)
    return mm(high, ahead_hi) + mm(low, ahead_hi) + mm(high, ahead_lo)


def kernel_spectrum_body(kernel_ref, fh_ref, fl_ref, tc_ref, ts_ref, ah_ref, al_ref, out_ref, rows_ref):
    channels = kernel_ref.shape[0]
    for a in range(RADIX):
        rows_ref[a * channels : (a + 1) * channels, :] = kernel_ref[:, a * RADIX : (a + 1) * RADIX]
    for c in range(channels):
        data = rows_ref[pl.ds(c, RADIX, stride=channels), :]
        high, low = halves(data)
        step = mm(fh_ref[...], high) + mm(fh_ref[...], low) + mm(fl_ref[...], high)
        out_ref[c] = spectrum(step, tc_ref[...], ts_ref[...], ah_ref[...], al_ref[...])


def filter_body(
    signal_ref, spec_ref, fh_ref, fl_ref, lh_ref, ll_ref, tc_ref, ts_ref, ah_ref, al_ref, bh_ref, bl_ref, out_ref, rows_ref, back_ref
):
    sources, channels, tokens = signal_ref.shape
    half = tokens // RADIX
    rows = sources * channels
    data = signal_ref[...].astype(F32).reshape(rows, tokens)
    for h in range(half):
        rows_ref[h * rows : (h + 1) * rows, :] = data[:, h * RADIX : (h + 1) * RADIX]
    tc, ts = tc_ref[...], ts_ref[...]
    for c in range(channels):
        data = rows_ref[pl.ds(c, RADIX, stride=channels), :].astype(BF16)
        step = mm(fh_ref[...], data) + mm(fl_ref[...], data)
        both = spectrum(step, tc, ts, ah_ref[...], al_ref[...])
        sig_r, sig_i = both[:, :RADIX], both[:, RADIX:]
        spec = spec_ref[c]
        ker_r, ker_i = spec[:, :RADIX], spec[:, RADIX:]
        high, low = halves(
            jnp.concatenate([sig_r * ker_r - sig_i * ker_i, sig_r * ker_i + sig_i * ker_r], 1)
        )
        back = mm(high, bh_ref[...]) + mm(low, bh_ref[...]) + mm(high, bl_ref[...])
        real, imag = back[:, :RADIX], back[:, RADIX:]
        high, low = halves(jnp.concatenate([real * tc - imag * ts, imag * tc + real * ts], 0))
        result = mm(lh_ref[...], high) + mm(lh_ref[...], low) + mm(ll_ref[...], high)
        back_ref[pl.ds(c, RADIX, stride=channels), :] = result
    joined = jnp.concatenate([back_ref[h * rows : (h + 1) * rows, :] for h in range(half)], 1)
    out_ref[...] = joined.astype(BF16).reshape(out_ref.shape)


def attention_body(block_ref, query_ref, key_ref, value_ref, one_ref, two_ref, three_ref, out_ref, sum_ref):
    count, width = query_ref.shape
    block = block_ref[0]
    earlier = (three_ref, two_ref, one_ref)
    row = lax.broadcasted_iota(jnp.int32, (count, count), 0)
    col = lax.broadcasted_iota(jnp.int32, (count, count), 1)
    causal = col <= row
    squares = jnp.zeros((count, HD), F32)
    for h in range(width // HD):
        lanes = slice(h * HD, (h + 1) * HD)
        query = query_ref[:, lanes]
        keys = jnp.concatenate([ref[0:count, lanes] for ref in earlier] + [key_ref[:, lanes]], 0)
        values = jnp.concatenate([ref[count:, lanes] for ref in earlier] + [value_ref[:, lanes]], 0)
        scores = lax.dot_general(query, keys, (((1,), (1,)), ((), ())), preferred_element_type=F32) * (
            1.0 / math.sqrt(HD)
        )
        parts = []
        for i in range(SPAN):
            seen = scores[:, i * count : (i + 1) * count]
            parts.append(jnp.where(block >= SPAN - i, seen, -1e30))
        parts.append(jnp.where(causal, scores[:, SPAN * count :], -1e30))
        scores = jnp.concatenate(parts, 1)
        top = jnp.max(scores, axis=1, keepdims=True)
        probs = jnp.exp(scores - top)
        total = jnp.sum(probs, axis=1, keepdims=True)
        numer = mm(probs.astype(BF16), values)
        branch = numer / total
        out_ref[:, lanes] = branch
        squares = squares + branch * branch
    sum_ref[...] = squares.T


def attend(block, query, key, value, one, two, three):
    count, width = query.shape
    vmem = pl.BlockSpec(memory_space=pltpu.VMEM)
    return pl.pallas_call(
        attention_body,
        out_shape=(jax.ShapeDtypeStruct((count, width), F32), jax.ShapeDtypeStruct((HD, count), F32)),
        in_specs=[pl.BlockSpec(memory_space=pltpu.SMEM)] + [vmem] * 6,
        out_specs=(vmem, vmem),
        compiler_params=pltpu.CompilerParams(vmem_limit_bytes=48 * 2**20),
        name="attention",
    )(block, query, key, value, one, two, three)


def sums_body(returned_ref, query_t_ref, att_ref, out_ref):
    mixed = returned_ref[...].astype(F32).reshape(query_t_ref.shape) * query_t_ref[...].astype(F32)
    mixer = jnp.sum(mixed * mixed, axis=0, keepdims=True)
    attention = jnp.sum(att_ref[...], axis=0, keepdims=True)
    rows = jnp.concatenate(
        [attention[:, :RADIX], attention[:, RADIX:], mixer[:, :RADIX], mixer[:, RADIX:], jnp.zeros((4, RADIX), F32)], 0
    )
    out_ref[...] = jnp.broadcast_to(rows[None], out_ref.shape)


def mixed_body(returned_ref, query_ref, beta_ref, out_ref):
    count, width = query_ref.shape
    returned = returned_ref[...].astype(F32).reshape(width, count).T
    out_ref[...] = query_ref[...].astype(F32) * returned * beta_ref[...]


def join_body(sums_ref, att_ref, mixed_ref, beta_ref, out_ref):
    count, _ = att_ref.shape
    total = sums_ref[0]
    for peer in range(1, sums_ref.shape[0]):
        total = total + sums_ref[peer]
    scale = lax.rsqrt(total * (1.0 / D) + 1e-05) * 0.5
    columns = jnp.concatenate([scale, jnp.zeros((RADIX - 8, RADIX), F32)], 0).T
    for h in range(count // RADIX):
        rows = slice(h * RADIX, (h + 1) * RADIX)
        attention_scale = columns[:, h : h + 1]
        mixer_scale = columns[:, 2 + h : 3 + h]
        out_ref[rows, :] = (
            beta_ref[...] * att_ref[rows, :] * attention_scale + mixed_ref[rows, :] * mixer_scale
        ).astype(BF16)


def transpose_body(in_ref, out_ref):
    out_ref[...] = in_ref[...].astype(F32).T.astype(BF16)


def mixer(
    mixer_query,
    mixer_key,
    mixer_value,
    shift_taps,
    conv_kernel,
    heads_query,
    heads_key,
    heads_value,
    beta_attention,
    beta_mixer,
):
    count, width = mixer_key.shape
    blocks = lax.axis_size("seq")
    peers = lax.axis_size("head")
    channels = width // blocks
    sds = jax.ShapeDtypeStruct
    tables = conv_tables(count)
    tables = {k: tuple(jnp.asarray(x) for x in v) if isinstance(v, tuple) else jnp.asarray(v) for k, v in tables.items()}
    onward = [(i, i + 1) for i in range(blocks - 1)]

    before = lax.ppermute(mixer_key[count - 8 :], "seq", onward)
    signal = kernel_call(
        shift_body, sds((blocks, channels, count), BF16), [pltpu.VMEM((count + 8, width), F32)]
    )(before, mixer_key, mixer_value, shift_taps)
    received = lax.all_to_all(signal, "seq", 0, 0, tiled=True)
    kernel_spectrum = kernel_call(
        kernel_spectrum_body, sds((channels, RADIX, 2 * RADIX), F32), [pltpu.VMEM((channels * RADIX, RADIX), F32)]
    )(conv_kernel, *tables["first_natural"], tables["twist_cos"], tables["twist_sin"], *tables["ahead"])
    filtered = kernel_call(
        filter_body, sds((blocks, channels, count), BF16), [pltpu.VMEM((channels * RADIX, RADIX), F32)] * 2
    )(
        received,
        kernel_spectrum,
        *tables["first"],
        *tables["last"],
        tables["twist_cos"],
        tables["twist_sin"],
        *tables["ahead"],
        *tables["back"],
    )
    returned = lax.all_to_all(filtered, "seq", 0, 0, tiled=True)

    carried = jnp.concatenate([heads_key, heads_value], 0)
    earlier = []
    for _ in range(SPAN):
        carried = lax.ppermute(carried, "seq", onward)
        earlier.append(carried)
    block = lax.axis_index("seq").astype(jnp.int32).reshape(1)
    attention_branch, attention_squares = attend(block, heads_query, heads_key, heads_value, *earlier)
    query_t = kernel_call(transpose_body, sds((width, count), BF16))(mixer_query)
    sums = kernel_call(sums_body, sds((peers, 8, RADIX), F32))(returned, query_t, attention_squares)
    gathered = lax.all_to_all(sums, "head", 0, 0, tiled=True)
    mixed = kernel_call(mixed_body, sds((count, width), F32))(
        returned, mixer_query, beta_mixer[None, :]
    )
    return kernel_call(join_body, sds((count, width), BF16))(gathered, attention_branch, mixed, beta_attention[None, :])


def solution(mesh):
    return jax.shard_map(
        mixer,
        mesh=mesh,
        in_specs=(
            P("seq", "head"),
            P("seq", "head"),
            P("seq", "head"),
            P(None, "head"),
            P(("head", "seq"), None),
            P("seq", "head"),
            P("seq", "head"),
            P("seq", "head"),
            P("head"),
            P("head"),
        ),
        out_specs=P("seq", "head"),
        check_vma=False,
    )
```

time: 128 us -> 105 us (0.82)
  waiting for transfers between devices: 12.2 us -> 46.5 us
  blocking collectives: 33.3 us -> 0 us
  matrix products: 25.8 us -> 0 us
  Pallas kernels: 0 us -> 13.1 us
  other arithmetic: 7.14 us -> 1.12 us
  starting transfers between devices: 39.2 us -> 35.4 us
  local copies, waits for them, and re-layouts: 8.9 us -> 6.99 us
    psum x1 -> x0, blocking collectives: 33.3 us -> none  [on_device(): lax.psum((jnp.sum(attention_branch * attention_branch, axis=1), jnp.sum(m...]
    dot_general x14 -> x0, matrix products: 25.8 us -> none  [the longest x1 3.4 us: attend(): jnp.einsum('hqk,khd->qhd', weights, value_heads, preferred_element_type=j...]
    all_to_all x2 -> x3, waiting for transfers between devices: 5.09 us -> 24 us  [the longest x1 10 us: mixer(): gathered = lax.all_to_all(sums, 'head', 0, 0, tiled=True)]
    ppermute x7 -> x4, waiting for transfers between devices: 7.06 us -> 22.5 us  [the longest x3 13.1 us: mixer(): carried = lax.ppermute(carried, 'seq', onward)]
    pallas_call x0 -> x8, Pallas kernels: none -> 13.1 us  [the longest x7 11 us: call(): pl.pallas_call(body, out_shape=out_shape, scratch_shapes=list(scratch), c...]
    ppermute x7 -> x4, starting transfers between devices: 18.5 us -> 7.78 us  [the longest x3 5.86 us: mixer(): carried = lax.ppermute(carried, 'seq', onward)]
    all_to_all x2 -> x3, starting transfers between devices: 20.7 us -> 27.7 us  [the longest x1 12.7 us: mixer(): gathered = lax.all_to_all(sums, 'head', 0, 0, tiled=True)]
    all_to_all x1 -> x0, other arithmetic: 2.36 us -> none  [on_device(): lax.all_to_all(jnp.transpose(ssm_input), 'seq', split_axis=0, concat_axis...]
  transfers between devices with their start and end apart: 9 -> 7, of which waited for: 2 -> 5; matrix products, arithmetic and copies ran while one was open for 30% -> 0% of each run, Pallas kernels for 0% -> 11%
where the time goes in v1:
time: 105 us; the launch traced here: 103 us
  waiting for transfers between devices  46.5 us (44%)
  starting transfers between devices  35.4 us (34%)
  Pallas kernels  13.1 us (12%)
  local copies, waits for them, and re-layouts  6.99 us (7%)
  other arithmetic  1.12 us (1%)
    ppermute x3, waiting for transfers between devices, mixer(): carried = lax.ppermute(carried, 'seq', onward)  13.1 us
    all_to_all x1, starting transfers between devices, mixer(): gathered = lax.all_to_all(sums, 'head', 0, 0, tiled=True)  12.7 us
    pallas_call x7, Pallas kernels, call(): pl.pallas_call(body, out_shape=out_shape, scratch_shapes=list(scratch), c...  11 us
    all_to_all x1, waiting for transfers between devices, mixer(): gathered = lax.all_to_all(sums, 'head', 0, 0, tiled=True)  10 us
    ppermute x1, waiting for transfers between devices, mixer(): before = lax.ppermute(mixer_key[count - 8:], 'seq', onward)  9.41 us
    all_to_all x1, starting transfers between devices, mixer(): received = lax.all_to_all(signal, 'seq', 0, 0, tiled=True)  8.47 us
    all_to_all x1, waiting for transfers between devices, mixer(): returned = lax.all_to_all(filtered, 'seq', 0, 0, tiled=True)  8.32 us
    unnamed x44, local copies, waits for them, and re-layouts  6.98 us
  transfers between devices with their start and end apart: 7, of which 5 were waited for; matrix products, arithmetic and copies ran while one was open for 0% of the time, Pallas kernels for 11%

profile of v1, /device:TPU:56, one launch (start us, length us, event | category | flops | bytes accessed | tf_op | source)
XLA Modules:
  0.0 103.4 jit_solution(3816760807132323360)
XLA Ops:
  0.0 1.1 %pad_maximum_fusion = bf16[512,512]{1,0:T(8,128)(2,1)S(1)} fusion(bf16[256,512]{1,0:T(8,128)(2,1)} %value_ref.3, bf16[256,512]{1,0:T(8,128)(2,1)} %key_ref.3), kind=kLoop, calls=%fused_computation | loop fusion | flops 1048576 | bytes 1048576 | tf_op jit(solution)/shard_map/concatenate | solution.py:259
  1.1 0.0 copy-start.19
  1.1 1.9 %collective-permute-start.1 = (bf16[512,512]{1,0:T(8,128)(2,1)S(1)}, bf16[512,512]{1,0:T(8,128)(2,1)S(1)}, u32[]{:S(2)}, u32[]{:S(2)}) collective-permute-start(bf16[512,512]{1,0:T(8,128)(2,1)S(1)} %pad_maximum_fusion), channel_id=1, source_target_pairs={{0,8},{8,16},{16,24},{24,32},{32,40},{40,48},{48,56},{56,64},{64,7... | collective-permute-start | bytes 1572872 | tf_op jit(solution)/shard_map/ppermute | solution.py:262
  3.1 13.1 %collective-permute-done.1.one_ref = bf16[512,512]{1,0:T(8,128)(2,1)S(1)} collective-permute-done((bf16[512,512]{1,0:T(8,128)(2,1)S(1)}, bf16[512,512]{1,0:T(8,128)(2,1)S(1)}, u32[]{:S(2)}, u32[]{:S(2)}) %collective-permute-start.1) | collective-permute-done | bytes 524320 | tf_op jit(solution)/shard_map/ppermute | solution.py:262
  16.1 1.9 %collective-permute-start.2 = (bf16[512,512]{1,0:T(8,128)(2,1)S(1)}, bf16[512,512]{1,0:T(8,128)(2,1)S(1)}, u32[]{:S(2)}, u32[]{:S(2)}) collective-permute-start(bf16[512,512]{1,0:T(8,128)(2,1)S(1)} %collective-permute-done.1.one_ref), channel_id=1, source_target_pairs={{0,8},{8,16},{16,24},{24,32},{32,40},{40,48},{48,56},{56,64},{64,7... | collective-permute-start | bytes 1572872 | tf_op jit(solution)/shard_map/ppermute | solution.py:262
  18.1 1.9 %collective-permute-start = (bf16[8,512]{1,0:T(8,128)(2,1)S(1)}, bf16[8,512]{1,0:T(8,128)(2,1)S(1)}, u32[]{:S(2)}, u32[]{:S(2)}) collective-permute-start(bf16[8,512]{1,0:T(8,128)(2,1)S(1)} %slice.3), channel_id=1, source_target_pairs={{0,8},{8,16},{16,24},{24,32},{32,40},{40,48},{48,56},{56,64},{64,7... | collective-permute-start | bytes 24584 | tf_op jit(solution)/shard_map/ppermute | solution.py:237
  20.0 9.4 %collective-permute-done.before_ref = bf16[8,512]{1,0:T(8,128)(2,1)S(1)} collective-permute-done((bf16[8,512]{1,0:T(8,128)(2,1)S(1)}, bf16[8,512]{1,0:T(8,128)(2,1)S(1)}, u32[]{:S(2)}, u32[]{:S(2)}) %collective-permute-start) | collective-permute-done | bytes 8224 | tf_op jit(solution)/shard_map/ppermute | solution.py:237
  29.4 1.5 %shard_map.208 = bf16[64,8,256]{2,1,0:T(8,128)(2,1)} custom-call(bf16[8,512]{1,0:T(8,128)(2,1)S(1)} %collective-permute-done.before_ref, bf16[256,512]{1,0:T(8,128)(2,1)S(1)} %copy-done.6, bf16[256,512]{1,0:T(8,128)(2,1)S(1)} %copy-done.7, f32[8,512]{1,0:T(8,128)S(1)} %copy-done.19), custom_call_target="tpu_custom_call" | custom-call | tf_op jit(solution)/shard_map/pallas_call | solution.py:64
  30.9 0.0 copy-start.11
  30.9 8.5 %all-to-all-start = ((bf16[64,8,256]{2,1,0:T(8,128)(2,1)}), bf16[64,8,256]{2,1,0:T(8,128)(2,1)S(1)}, u32[]{:S(2)}, u32[]{:S(2)}) async-start(bf16[64,8,256]{2,1,0:T(8,128)(2,1)} %shard_map.208), calls=%async_computation | async-start | bytes 524288 | tf_op jit(solution)/shard_map/all_to_all | solution.py:241
  39.4 2.0 %collective-permute-start.3 = (bf16[512,512]{1,0:T(8,128)(2,1)S(1)}, bf16[512,512]{1,0:T(8,128)(2,1)S(1)}, u32[]{:S(2)}, u32[]{:S(2)}) collective-permute-start(bf16[512,512]{1,0:T(8,128)(2,1)S(1)} %collective-permute-done.2.two_ref), channel_id=1, source_target_pairs={{0,8},{8,16},{16,24},{24,32},{32,40},{40,48},{48,56},{56,64},{64,7... | collective-permute-start | bytes 1572872 | tf_op jit(solution)/shard_map/ppermute | solution.py:262
  41.5 1.0 copy-done.5
  42.5 0.8 copy-done.13
  43.4 0.8 copy-done.18
  44.2 1.2 %shard_map.209.spec_ref = f32[8,128,256]{2,1,0:T(8,128)S(1)} custom-call(f32[8,16384]{1,0:T(8,128)S(1)} %copy-done.5, bf16[256,128]{1,0:T(8,128)(2,1)S(1)} %copy-done.13, bf16[256,128]{1,0:T(8,128)(2,1)S(1)} %copy-done.18, f32[128,128]{1,0:T(8,128)S(1)} %copy-done.9, f32[128,128]{1,0:T(8,128)S(1)} %copy-done.10, bf16[256,256]{1,0:T(8,128)(2,1)S(1)} %copy-done.3, ...), custom_call_target="tpu_custom_call" | custom-call | tf_op jit(solution)/shard_map/pallas_call | solution.py:64
  45.4 5.7 %all-to-all-done.signal_ref = bf16[64,8,256]{2,1,0:T(8,128)(2,1)S(1)} async-done(((bf16[64,8,256]{2,1,0:T(8,128)(2,1)}), bf16[64,8,256]{2,1,0:T(8,128)(2,1)S(1)}, u32[]{:S(2)}, u32[]{:S(2)}) %all-to-all-start) | async-done | bytes 262176 | tf_op jit(solution)/shard_map/all_to_all | solution.py:241
  51.1 0.8 copy-done.14
  52.0 0.8 copy-done.15
  52.8 0.8 copy-done.16
  53.6 0.8 copy-done.17
  54.5 6.3 %shard_map.210 = bf16[64,8,256]{2,1,0:T(8,128)(2,1)} custom-call(bf16[64,8,256]{2,1,0:T(8,128)(2,1)S(1)} %all-to-all-done.signal_ref, f32[8,128,256]{2,1,0:T(8,128)S(1)} %shard_map.209.spec_ref, bf16[256,128]{1,0:T(8,128)(2,1)S(1)} %copy-done.14, bf16[256,128]{1,0:T(8,128)(2,1)S(1)} %copy-done.15, bf16[128,256]{1,0:T(8,128)(2,1)S(1)} %copy-done.16, ...), custom_call_target="tpu_custom_call" | custom-call | tf_op jit(solution)/shard_map/pallas_call | solution.py:64
  60.8 6.4 %all-to-all-start.1 = ((bf16[64,8,256]{2,1,0:T(8,128)(2,1)}), bf16[64,8,256]{2,1,0:T(8,128)(2,1)S(1)}, u32[]{:S(2)}, u32[]{:S(2)}) async-start(bf16[64,8,256]{2,1,0:T(8,128)(2,1)} %shard_map.210), calls=%async_computation.1 | async-start | bytes 524288 | tf_op jit(solution)/shard_map/all_to_all | solution.py:257
  67.3 0.1 shard_map.211.query_t_ref
  67.5 0.8 copy-done
  68.2 0.1 copy-done.1
  68.3 2.2 %attention.1 = (f32[256,512]{1,0:T(8,128)S(1)}, f32[128,256]{1,0:T(8,128)S(1)}) custom-call(s32[1]{0:T(128)} %bitcast.block_ref, bf16[256,512]{1,0:T(8,128)(2,1)S(1)} %copy-done.8, bf16[256,512]{1,0:T(8,128)(2,1)S(1)} %copy-done, bf16[256,512]{1,0:T(8,128)(2,1)S(1)} %copy-done.1, bf16[512,512]{1,0:T(8,128)(2,1)S(1)} %collective-permute-done.1.one_ref, ...), custom_call_target="tpu_custom_call" | custom-call | tf_op jit(solution)/shard_map/attention/pallas_call | solution.py:170
  70.5 8.3 %all-to-all-done.1.returned_ref = bf16[64,8,256]{2,1,0:T(8,128)(2,1)S(1)} async-done(((bf16[64,8,256]{2,1,0:T(8,128)(2,1)}), bf16[64,8,256]{2,1,0:T(8,128)(2,1)S(1)}, u32[]{:S(2)}, u32[]{:S(2)}) %all-to-all-start.1) | async-done | bytes 262176 | tf_op jit(solution)/shard_map/all_to_all | solution.py:257
  78.8 0.7 shard_map.212
  79.5 12.7 %all-to-all-start.2 = ((f32[8,8,128]{2,1,0:T(8,128)}), f32[8,8,128]{2,1,0:T(8,128)S(1)}, u32[]{:S(2)}, u32[]{:S(2)}) async-start(f32[8,8,128]{2,1,0:T(8,128)} %shard_map.212), calls=%async_computation.2 | async-start | bytes 65536 | tf_op jit(solution)/shard_map/all_to_all | solution.py:268
  92.3 0.1 shard_map.213.mixed_ref
  92.4 10.0 %all-to-all-done.2.sums_ref = f32[8,8,128]{2,1,0:T(8,128)S(1)} async-done(((f32[8,8,128]{2,1,0:T(8,128)}), f32[8,8,128]{2,1,0:T(8,128)S(1)}, u32[]{:S(2)}, u32[]{:S(2)}) %all-to-all-start.2) | async-done | bytes 32800 | tf_op jit(solution)/shard_map/all_to_all | solution.py:268
  102.4 1.0 shard_map.214
  (36 shorter events, 0.1 us)
Async XLA Ops:
  0.0 18.0 %copy-start.6 = (bf16[256,512]{1,0:T(8,128)(2,1)S(1)}, bf16[256,512]{1,0:T(8,128)(2,1)}, u32[]{:S(2)}) copy-start(bf16[256,512]{1,0:T(8,128)(2,1)} %key_ref.2) | copy-start | bytes 786436
  0.0 29.4 %copy-start.7 = (bf16[256,512]{1,0:T(8,128)(2,1)S(1)}, bf16[256,512]{1,0:T(8,128)(2,1)}, u32[]{:S(2)}) copy-start(bf16[256,512]{1,0:T(8,128)(2,1)} %value_ref.2) | copy-start | bytes 786436
  1.1 28.3 %copy-start.19 = (f32[8,512]{1,0:T(8,128)S(1)}, f32[8,512]{1,0:T(8,128)}, u32[]{:S(2)}) copy-start(f32[8,512]{1,0:T(8,128)} %taps_ref.1) | copy-start | bytes 49156
  1.1 15.0 %collective-permute-start.1 = (bf16[512,512]{1,0:T(8,128)(2,1)S(1)}, bf16[512,512]{1,0:T(8,128)(2,1)S(1)}, u32[]{:S(2)}, u32[]{:S(2)}) collective-permute-start(bf16[512,512]{1,0:T(8,128)(2,1)S(1)} %pad_maximum_fusion), channel_id=1, source_target_pairs={{0,8},{8,16},{16,24},{24,32},{32,40},{40,48},{48,56},{56,64},{64,7... | collective-permute-start | bytes 1572872 | tf_op jit(solution)/shard_map/ppermute | solution.py:262
  16.1 23.3 %collective-permute-start.2 = (bf16[512,512]{1,0:T(8,128)(2,1)S(1)}, bf16[512,512]{1,0:T(8,128)(2,1)S(1)}, u32[]{:S(2)}, u32[]{:S(2)}) collective-permute-start(bf16[512,512]{1,0:T(8,128)(2,1)S(1)} %collective-permute-done.1.one_ref), channel_id=1, source_target_pairs={{0,8},{8,16},{16,24},{24,32},{32,40},{40,48},{48,56},{56,64},{64,7... | collective-permute-start | bytes 1572872 | tf_op jit(solution)/shard_map/ppermute | solution.py:262
  18.1 11.3 %collective-permute-start = (bf16[8,512]{1,0:T(8,128)(2,1)S(1)}, bf16[8,512]{1,0:T(8,128)(2,1)S(1)}, u32[]{:S(2)}, u32[]{:S(2)}) collective-permute-start(bf16[8,512]{1,0:T(8,128)(2,1)S(1)} %slice.3), channel_id=1, source_target_pairs={{0,8},{8,16},{16,24},{24,32},{32,40},{40,48},{48,56},{56,64},{64,7... | collective-permute-start | bytes 24584 | tf_op jit(solution)/shard_map/ppermute | solution.py:237
  30.9 10.6 %copy-start.3 = (bf16[256,256]{1,0:T(8,128)(2,1)S(1)}, bf16[256,256]{1,0:T(8,128)(2,1)}, u32[]{:S(2)}) copy-start(bf16[256,256]{1,0:T(8,128)(2,1)} %constant.36.clone.ah_ref) | copy-start | bytes 393220
  30.9 10.6 %copy-start.4 = (bf16[256,256]{1,0:T(8,128)(2,1)S(1)}, bf16[256,256]{1,0:T(8,128)(2,1)}, u32[]{:S(2)}) copy-start(bf16[256,256]{1,0:T(8,128)(2,1)} %constant.37.clone.al_ref) | copy-start | bytes 393220
  30.9 10.6 %copy-start.9 = (f32[128,128]{1,0:T(8,128)S(1)}, f32[128,128]{1,0:T(8,128)}, u32[]{:S(2)}) copy-start(f32[128,128]{1,0:T(8,128)} %constant.40.clone.tc_ref) | copy-start | bytes 196612
  30.9 10.6 %copy-start.10 = (f32[128,128]{1,0:T(8,128)S(1)}, f32[128,128]{1,0:T(8,128)}, u32[]{:S(2)}) copy-start(f32[128,128]{1,0:T(8,128)} %constant.41.clone.ts_ref) | copy-start | bytes 196612
  30.9 20.2 %copy-start.11 = (bf16[256,256]{1,0:T(8,128)(2,1)S(1)}, bf16[256,256]{1,0:T(8,128)(2,1)}, u32[]{:S(2)}) copy-start(bf16[256,256]{1,0:T(8,128)(2,1)} %constant.38.clone.bh_ref) | copy-start | bytes 393220
  30.9 20.2 %all-to-all-start = ((bf16[64,8,256]{2,1,0:T(8,128)(2,1)}), bf16[64,8,256]{2,1,0:T(8,128)(2,1)S(1)}, u32[]{:S(2)}, u32[]{:S(2)}) async-start(bf16[64,8,256]{2,1,0:T(8,128)(2,1)} %shard_map.208), calls=%async_computation | async-start | bytes 524288 | tf_op jit(solution)/shard_map/all_to_all | solution.py:241
  39.4 28.1 %collective-permute-start.3 = (bf16[512,512]{1,0:T(8,128)(2,1)S(1)}, bf16[512,512]{1,0:T(8,128)(2,1)S(1)}, u32[]{:S(2)}, u32[]{:S(2)}) collective-permute-start(bf16[512,512]{1,0:T(8,128)(2,1)S(1)} %collective-permute-done.2.two_ref), channel_id=1, source_target_pairs={{0,8},{8,16},{16,24},{24,32},{32,40},{40,48},{48,56},{56,64},{64,7... | collective-permute-start | bytes 1572872 | tf_op jit(solution)/shard_map/ppermute | solution.py:262
  41.5 1.0 %copy-start.5 = (f32[8,16384]{1,0:T(8,128)S(1)}, f32[8,16384]{1,0:T(8,128)}, u32[]{:S(2)}) copy-start(f32[8,16384]{1,0:T(8,128)} %kernel_ref.1) | copy-start | bytes 1572868
  42.5 0.8 copy-start.13
  43.4 0.8 copy-start.18
  44.2 6.9 %copy-start.12 = (bf16[256,256]{1,0:T(8,128)(2,1)S(1)}, bf16[256,256]{1,0:T(8,128)(2,1)}, u32[]{:S(2)}) copy-start(bf16[256,256]{1,0:T(8,128)(2,1)} %constant.39.clone.bl_ref) | copy-start | bytes 393220
  51.1 0.8 copy-start.14
  52.0 0.8 copy-start.15
  52.8 0.8 copy-start.16
  53.6 0.8 copy-start.17
  60.8 6.5 %copy-start.2 = (bf16[256,512]{1,0:T(8,128)(2,1)S(1)}, bf16[256,512]{1,0:T(8,128)(2,1)}, u32[]{:S(2)}) copy-start(bf16[256,512]{1,0:T(8,128)(2,1)} %query_ref.3) | copy-start | bytes 786436
  60.8 6.7 %copy-start.8 = (bf16[256,512]{1,0:T(8,128)(2,1)S(1)}, bf16[256,512]{1,0:T(8,128)(2,1)}, u32[]{:S(2)}) copy-start(bf16[256,512]{1,0:T(8,128)(2,1)} %query_ref.2) | copy-start | bytes 786436
  60.8 18.0 %all-to-all-start.1 = ((bf16[64,8,256]{2,1,0:T(8,128)(2,1)}), bf16[64,8,256]{2,1,0:T(8,128)(2,1)S(1)}, u32[]{:S(2)}, u32[]{:S(2)}) async-start(bf16[64,8,256]{2,1,0:T(8,128)(2,1)} %shard_map.210), calls=%async_computation.1 | async-start | bytes 524288 | tf_op jit(solution)/shard_map/all_to_all | solution.py:257
  67.3 1.0 copy-start
  67.3 1.0 copy-start.1
  78.8 13.5 %copy-start.20 = (f32[512]{0:T(512)S(1)}, f32[512]{0:T(512)}, u32[]{:S(2)}) copy-start(f32[512]{0:T(512)} %param.31) | copy-start | bytes 6148
  79.5 22.9 %all-to-all-start.2 = ((f32[8,8,128]{2,1,0:T(8,128)}), f32[8,8,128]{2,1,0:T(8,128)S(1)}, u32[]{:S(2)}, u32[]{:S(2)}) async-start(f32[8,8,128]{2,1,0:T(8,128)} %shard_map.212), calls=%async_computation.2 | async-start | bytes 65536 | tf_op jit(solution)/shard_map/all_to_all | solution.py:268
  92.4 10.0 %copy-start.21 = (f32[512]{0:T(512)S(1)}, f32[512]{0:T(512)}, u32[]{:S(2)}) copy-start(f32[512]{0:T(512)} %param.30) | copy-start | bytes 6148

commit v2 on v1

--- a/solution.py
+++ b/solution.py
@@ -1,3 +1,4 @@
+import functools
 import math
 
 import jax
@@ -31,22 +32,20 @@
     freq = np.arange(RADIX) + 0.5
     one = 2.0 * np.pi * np.outer(freq, order) / (2 * RADIX)
     first = np.concatenate([np.cos(one), -np.sin(one)], 0)
-    last = np.concatenate([np.cos(one), -np.sin(one)], 0).T * (1.0 / (RADIX * RADIX))
-    first_natural = 2.0 * np.pi * np.outer(freq, place) / (2 * RADIX)
-    first_natural = np.concatenate([np.cos(first_natural), -np.sin(first_natural)], 0)
+    last = first.T * (1.0 / (RADIX * RADIX))
     twist = 2.0 * np.pi * np.outer(freq, place) / (2 * RADIX * RADIX)
     two = 2.0 * np.pi * np.outer(place, place) / RADIX
     cos, sin = np.cos(two), np.sin(two)
     ahead = np.block([[cos, -sin], [sin, cos]])
     back = np.block([[cos, sin], [-sin, cos]])
-    return dict(
-        first=split_table(first),
-        first_natural=split_table(first_natural),
-        last=split_table(last),
-        ahead=split_table(ahead),
-        back=split_table(back),
-        twist_cos=np.cos(twist).astype(np.float32),
-        twist_sin=np.sin(twist).astype(np.float32),
+    products = [
+        np.concatenate(split_table(first), 1),
+        np.concatenate(split_table(last), 0),
+        *split_table(ahead),
+        *split_table(back),
+    ]
+    return jnp.asarray(np.stack(products)), jnp.asarray(
+        np.stack([np.cos(twist), np.sin(twist)]).astype(np.float32)
     )
 
 
@@ -71,65 +70,103 @@
     return call
 
 
-def shift_body(before_ref, key_ref, value_ref, taps_ref, out_ref, ext_ref):
-    count, _ = key_ref.shape
-    ext_ref[0:8, :] = before_ref[...].astype(F32)
-    ext_ref[8:, :] = key_ref[...].astype(F32)
+def shift_body(key_ref, value_ref, taps_ref, out_ref, ext_ref):
+    count, width = key_ref.shape
+    ext_ref[0:8, :] = jnp.zeros((8, width), F32)
+    ext_ref[8 : 8 + count, :] = key_ref[...].astype(F32)
     taps = taps_ref[...]
     total = taps[0:1, :] * ext_ref[8 : 8 + count, :]
     for j in range(1, TAPS):
         total = total + taps[j : j + 1, :] * ext_ref[8 - j : 8 - j + count, :]
     product = total * value_ref[...].astype(F32)
-    out_ref[...] = product.T.astype(BF16).reshape(out_ref.shape)
-
-
-def spectrum(first_step, twist_cos, twist_sin, ahead_hi, ahead_lo):
-    real, imag = first_step[:RADIX], first_step[RADIX:]
-    turned = jnp.concatenate(
-        [real * twist_cos + imag * twist_sin, imag * twist_cos - real * twist_sin], 1
-    )
-    high, low = halves(turned)
-    return mm(high, ahead_hi) + mm(low, ahead_hi) + mm(high, ahead_lo)
-
-
-def kernel_spectrum_body(kernel_ref, fh_ref, fl_ref, tc_ref, ts_ref, ah_ref, al_ref, out_ref, rows_ref):
+    edges = jnp.concatenate(
+        [
+            ext_ref[8:16, :],
+            ext_ref[count : 8 + count, :],
+            value_ref[0:16, :].astype(F32)[0:8],
+            jnp.zeros((RADIX - 24, width), F32),
+        ],
+        0,
+    )
+    shape = out_ref.shape[:2]
+    out_ref[:, :, 0:count] = product.T.astype(BF16).reshape(*shape, count)
+    out_ref[:, :, count:] = edges.T.astype(BF16).reshape(*shape, RADIX)
+
+
+def product3(value, table_hi, table_lo):
+    high, low = halves(value)
+    return mm(high, table_hi) + mm(low, table_hi) + mm(high, table_lo)
+
+
+def spectrum(step, tables_ref, twist_ref):
+    cos, sin = twist_ref[0], twist_ref[1]
+    turned = []
+    for c in range(step.shape[1] // RADIX):
+        lanes = slice(c * RADIX, (c + 1) * RADIX)
+        real, imag = step[:RADIX, lanes], step[RADIX:, lanes]
+        turned.append(jnp.concatenate([real * cos + imag * sin, imag * cos - real * sin], 1))
+    return product3(jnp.concatenate(turned, 0), tables_ref[2], tables_ref[3])
+
+
+def gather_rows(rows_ref, channels):
+    return jnp.concatenate([rows_ref[pl.ds(c, RADIX, stride=channels), :] for c in range(channels)], 1)
+
+
+def kernel_spectrum_body(half, kernel_ref, tables_ref, twist_ref, out_ref, rows_ref):
     channels = kernel_ref.shape[0]
     for a in range(RADIX):
-        rows_ref[a * channels : (a + 1) * channels, :] = kernel_ref[:, a * RADIX : (a + 1) * RADIX]
+        row = ((a % half) * (RADIX // half) + a // half) * channels
+        rows_ref[row : row + channels, :] = kernel_ref[:, a * RADIX : (a + 1) * RADIX]
+    high, low = halves(gather_rows(rows_ref, channels))
+    first_hi, first_lo = tables_ref[0, :, :RADIX], tables_ref[0, :, RADIX:]
+    step = mm(first_hi, high) + mm(first_hi, low) + mm(first_lo, high)
+    out_ref[...] = spectrum(step, tables_ref, twist_ref)
+
+
+def first_tokens(signal_ref, taps_ref, count):
+    own = signal_ref[:, :, count:].astype(F32)
+    head = signal_ref[:, :, :RADIX].astype(F32)
+    previous = jnp.concatenate([jnp.zeros_like(own[:1]), own[:-1]], 0)
+    sources, channels = own.shape[:2]
+    own, previous, head = (x.reshape(sources * channels, RADIX) for x in (own, previous, head))
+    lane = lax.broadcasted_iota(jnp.int32, own.shape, 1)
+    window = jnp.where(lane < 16, previous, pltpu.roll(own, 16, 1))
+    total = jnp.zeros_like(window)
+    for j in range(TAPS):
+        tap = jnp.broadcast_to(taps_ref[j][None], (sources, channels, RADIX)).reshape(window.shape)
+        total = total + tap * (pltpu.roll(window, j, 1) if j else window)
+    return jnp.where(lane < 8, pltpu.roll(total * own, RADIX - 16, 1), head)
+
+
+def filter_body(signal_ref, taps_ref, spec_ref, tables_ref, twist_ref, out_ref, rows_ref, back_ref):
+    sources, channels, count = out_ref.shape
+    half = count // RADIX
+    rows = sources * channels
+    rows_ref[:rows, :] = first_tokens(signal_ref, taps_ref, count)
+    for h in range(1, half):
+        part = signal_ref[:, :, h * RADIX : (h + 1) * RADIX].astype(F32)
+        rows_ref[h * rows : (h + 1) * rows, :] = part.reshape(rows, RADIX)
+    data = gather_rows(rows_ref, channels).astype(BF16)
+    step = mm(tables_ref[0], jnp.concatenate([data, data], 0))
+    both = spectrum(step, tables_ref, twist_ref)
+    sig_r, sig_i = both[:, :RADIX], both[:, RADIX:]
+    ker_r, ker_i = spec_ref[:, :RADIX], spec_ref[:, RADIX:]
+    both = jnp.concatenate([sig_r * ker_r - sig_i * ker_i, sig_r * ker_i + sig_i * ker_r], 1)
+    both = product3(both, tables_ref[4], tables_ref[5])
+    cos, sin = twist_ref[0], twist_ref[1]
+    turned = []
     for c in range(channels):
-        data = rows_ref[pl.ds(c, RADIX, stride=channels), :]
-        high, low = halves(data)
-        step = mm(fh_ref[...], high) + mm(fh_ref[...], low) + mm(fl_ref[...], high)
-        out_ref[c] = spectrum(step, tc_ref[...], ts_ref[...], ah_ref[...], al_ref[...])
-
-
-def filter_body(
-    signal_ref, spec_ref, fh_ref, fl_ref, lh_ref, ll_ref, tc_ref, ts_ref, ah_ref, al_ref, bh_ref, bl_ref, out_ref, rows_ref, back_ref
-):
-    sources, channels, tokens = signal_ref.shape
-    half = tokens // RADIX
-    rows = sources * channels
-    data = signal_ref[...].astype(F32).reshape(rows, tokens)
+        lines = slice(c * RADIX, (c + 1) * RADIX)
+        real, imag = both[lines, :RADIX], both[lines, RADIX:]
+        turned.append(jnp.concatenate([real * cos - imag * sin, imag * cos + real * sin], 0))
+    high, low = halves(jnp.concatenate(turned, 1))
+    last_hi, last_lo = tables_ref[1, :RADIX], tables_ref[1, RADIX:]
+    result = mm(last_hi, high) + mm(last_hi, low) + mm(last_lo, high)
+    for c in range(channels):
+        back_ref[pl.ds(c, RADIX, stride=channels), :] = result[:, c * RADIX : (c + 1) * RADIX]
     for h in range(half):
-        rows_ref[h * rows : (h + 1) * rows, :] = data[:, h * RADIX : (h + 1) * RADIX]
-    tc, ts = tc_ref[...], ts_ref[...]
-    for c in range(channels):
-        data = rows_ref[pl.ds(c, RADIX, stride=channels), :].astype(BF16)
-        step = mm(fh_ref[...], data) + mm(fl_ref[...], data)
-        both = spectrum(step, tc, ts, ah_ref[...], al_ref[...])
-        sig_r, sig_i = both[:, :RADIX], both[:, RADIX:]
-        spec = spec_ref[c]
-        ker_r, ker_i = spec[:, :RADIX], spec[:, RADIX:]
-        high, low = halves(
-            jnp.concatenate([sig_r * ker_r - sig_i * ker_i, sig_r * ker_i + sig_i * ker_r], 1)
-        )
-        back = mm(high, bh_ref[...]) + mm(low, bh_ref[...]) + mm(high, bl_ref[...])
-        real, imag = back[:, :RADIX], back[:, RADIX:]
-        high, low = halves(jnp.concatenate([real * tc - imag * ts, imag * tc + real * ts], 0))
-        result = mm(lh_ref[...], high) + mm(lh_ref[...], low) + mm(ll_ref[...], high)
-        back_ref[pl.ds(c, RADIX, stride=channels), :] = result
-    joined = jnp.concatenate([back_ref[h * rows : (h + 1) * rows, :] for h in range(half)], 1)
-    out_ref[...] = joined.astype(BF16).reshape(out_ref.shape)
+        part = back_ref[h * rows : (h + 1) * rows, :].astype(BF16)
+        out_ref[:, :, h * RADIX : (h + 1) * RADIX] = part.reshape(sources, channels, RADIX)
 
 
 def attention_body(block_ref, query_ref, key_ref, value_ref, one_ref, two_ref, three_ref, out_ref, sum_ref):
@@ -230,30 +267,23 @@
     peers = lax.axis_size("head")
     channels = width // blocks
     sds = jax.ShapeDtypeStruct
-    tables = conv_tables(count)
-    tables = {k: tuple(jnp.asarray(x) for x in v) if isinstance(v, tuple) else jnp.asarray(v) for k, v in tables.items()}
+    tables, twist = conv_tables(count)
     onward = [(i, i + 1) for i in range(blocks - 1)]
-
-    before = lax.ppermute(mixer_key[count - 8 :], "seq", onward)
+    seq = lax.axis_index("seq")
+
     signal = kernel_call(
-        shift_body, sds((blocks, channels, count), BF16), [pltpu.VMEM((count + 8, width), F32)]
-    )(before, mixer_key, mixer_value, shift_taps)
+        shift_body, sds((blocks, channels, count + RADIX), BF16), [pltpu.VMEM((count + 8, width), F32)]
+    )(mixer_key, mixer_value, shift_taps)
     received = lax.all_to_all(signal, "seq", 0, 0, tiled=True)
+    own_taps = lax.dynamic_slice(shift_taps, (0, seq * channels), (TAPS, channels))
+    own_taps = jnp.broadcast_to(own_taps[:, :, None], (TAPS, channels, RADIX))
+    rows = pltpu.VMEM((channels * RADIX, RADIX), F32)
     kernel_spectrum = kernel_call(
-        kernel_spectrum_body, sds((channels, RADIX, 2 * RADIX), F32), [pltpu.VMEM((channels * RADIX, RADIX), F32)]
-    )(conv_kernel, *tables["first_natural"], tables["twist_cos"], tables["twist_sin"], *tables["ahead"])
+        functools.partial(kernel_spectrum_body, count // RADIX), sds((channels * RADIX, 2 * RADIX), F32), [rows]
+    )(conv_kernel, tables, twist)
     filtered = kernel_call(
-        filter_body, sds((blocks, channels, count), BF16), [pltpu.VMEM((channels * RADIX, RADIX), F32)] * 2
-    )(
-        received,
-        kernel_spectrum,
-        *tables["first"],
-        *tables["last"],
-        tables["twist_cos"],
-        tables["twist_sin"],
-        *tables["ahead"],
-        *tables["back"],
-    )
+        filter_body, sds((blocks, channels, count), BF16), [rows, rows]
+    )(received, own_taps, kernel_spectrum, tables, twist)
     returned = lax.all_to_all(filtered, "seq", 0, 0, tiled=True)
 
     carried = jnp.concatenate([heads_key, heads_value], 0)
@@ -261,7 +291,7 @@
     for _ in range(SPAN):
         carried = lax.ppermute(carried, "seq", onward)
         earlier.append(carried)
-    block = lax.axis_index("seq").astype(jnp.int32).reshape(1)
+    block = seq.astype(jnp.int32).reshape(1)
     attention_branch, attention_squares = attend(block, heads_query, heads_key, heads_value, *earlier)
     query_t = kernel_call(transpose_body, sds((width, count), BF16))(mixer_query)
     sums = kernel_call(sums_body, sds((peers, 8, RADIX), F32))(returned, query_t, attention_squares)

time: 105 us -> 90.1 us (0.86)
  waiting for transfers between devices: 46.5 us -> 34.2 us
  local copies, waits for them, and re-layouts: 6.99 us -> 1.04 us
  starting transfers between devices: 35.4 us -> 40.6 us
  Pallas kernels: 13.1 us -> 11.4 us
    ppermute x1 -> x0, waiting for transfers between devices: 9.41 us -> none  [mixer(): before = lax.ppermute(mixer_key[count - 8:], 'seq', onward)]
    unnamed x44 -> x24, local copies, waits for them, and re-layouts: 6.98 us -> 0.9 us
    all_to_all x1, waiting for transfers between devices: 5.72 us -> 0.01 us  [mixer(): received = lax.all_to_all(signal, 'seq', 0, 0, tiled=True)]
    all_to_all x1, starting transfers between devices: 8.47 us -> 13.5 us  [mixer(): received = lax.all_to_all(signal, 'seq', 0, 0, tiled=True)]
    all_to_all x1, starting transfers between devices: 6.45 us -> 11 us  [mixer(): returned = lax.all_to_all(filtered, 'seq', 0, 0, tiled=True)]
    ppermute x3, waiting for transfers between devices: 13.1 us -> 17.1 us  [mixer(): carried = lax.ppermute(carried, 'seq', onward)]
    pallas_call x7, Pallas kernels: 11 us -> 8.05 us  [call(): pl.pallas_call(body, out_shape=out_shape, scratch_shapes=list(scratch), c...]
    all_to_all x1, starting transfers between devices: 12.7 us -> 10.1 us  [mixer(): gathered = lax.all_to_all(sums, 'head', 0, 0, tiled=True)]
  transfers between devices with their start and end apart: 7 -> 6, of which waited for: 5 -> 3; matrix products, arithmetic and copies ran while one was open for 0% -> 0% of each run, Pallas kernels for 11% -> 11%
where the time goes in v2:
time: 90.1 us; the launch traced here: 88.6 us
  starting transfers between devices  40.6 us (45%)
  waiting for transfers between devices  34.2 us (38%)
  Pallas kernels  11.4 us (13%)
  other arithmetic  1.13 us (1%)
  local copies, waits for them, and re-layouts  1.04 us (1%)
    ppermute x3, waiting for transfers between devices, mixer(): carried = lax.ppermute(carried, 'seq', onward)  17.1 us
    all_to_all x1, starting transfers between devices, mixer(): received = lax.all_to_all(signal, 'seq', 0, 0, tiled=True)  13.5 us
    all_to_all x1, starting transfers between devices, mixer(): returned = lax.all_to_all(filtered, 'seq', 0, 0, tiled=True)  11 us
    all_to_all x1, starting transfers between devices, mixer(): gathered = lax.all_to_all(sums, 'head', 0, 0, tiled=True)  10.1 us
    all_to_all x1, waiting for transfers between devices, mixer(): gathered = lax.all_to_all(sums, 'head', 0, 0, tiled=True)  10 us
    pallas_call x7, Pallas kernels, call(): pl.pallas_call(body, out_shape=out_shape, scratch_shapes=list(scratch), c...  8.05 us
    all_to_all x1, waiting for transfers between devices, mixer(): returned = lax.all_to_all(filtered, 'seq', 0, 0, tiled=True)  7.11 us
    ppermute x3, starting transfers between devices, mixer(): carried = lax.ppermute(carried, 'seq', onward)  5.99 us
  transfers between devices with their start and end apart: 6, of which 3 were waited for; matrix products, arithmetic and copies ran while one was open for 0% of the time, Pallas kernels for 11%

profile of v2, /device:TPU:56, one launch (start us, length us, event | category | flops | bytes accessed | tf_op | source)
XLA Modules:
  0.0 88.6 jit_solution(10964873913404549338)
XLA Ops:
  0.0 1.1 %pad_maximum_fusion = bf16[512,512]{1,0:T(8,128)(2,1)S(1)} fusion(bf16[256,512]{1,0:T(8,128)(2,1)} %value_ref.3, bf16[256,512]{1,0:T(8,128)(2,1)} %key_ref.3), kind=kLoop, calls=%fused_computation | loop fusion | flops 1048576 | bytes 1048576 | tf_op jit(solution)/shard_map/concatenate | solution.py:289
  1.1 0.0 copy-start
  1.2 2.1 %collective-permute-start = (bf16[512,512]{1,0:T(8,128)(2,1)S(1)}, bf16[512,512]{1,0:T(8,128)(2,1)S(1)}, u32[]{:S(2)}, u32[]{:S(2)}) collective-permute-start(bf16[512,512]{1,0:T(8,128)(2,1)S(1)} %pad_maximum_fusion), channel_id=1, source_target_pairs={{0,8},{8,16},{16,24},{24,32},{32,40},{40,48},{48,56},{56,64},{64,7... | collective-permute-start | bytes 1572872 | tf_op jit(solution)/shard_map/ppermute | solution.py:292
  3.2 0.0 copy-done.9
  3.2 0.0 copy-done.6
  3.2 1.6 %shard_map.118 = bf16[64,8,384]{2,1,0:T(8,128)(2,1)} custom-call(bf16[256,512]{1,0:T(8,128)(2,1)S(1)} %copy-done.6, bf16[256,512]{1,0:T(8,128)(2,1)S(1)} %copy-done.7, f32[8,512]{1,0:T(8,128)S(1)} %copy-done.9), custom_call_target="tpu_custom_call" | custom-call | tf_op jit(solution)/shard_map/pallas_call | solution.py:63
  4.8 13.5 %all-to-all-start = ((bf16[64,8,384]{2,1,0:T(8,128)(2,1)}), bf16[64,8,384]{2,1,0:T(8,128)(2,1)S(1)}, u32[]{:S(2)}, u32[]{:S(2)}) async-start(bf16[64,8,384]{2,1,0:T(8,128)(2,1)} %shard_map.118), calls=%async_computation | async-start | bytes 786432 | tf_op jit(solution)/shard_map/all_to_all | solution.py:277
  18.3 0.0 collective-permute-done.one_ref
  18.3 2.0 %collective-permute-start.1 = (bf16[512,512]{1,0:T(8,128)(2,1)S(1)}, bf16[512,512]{1,0:T(8,128)(2,1)}, u32[]{:S(2)}, u32[]{:S(2)}) collective-permute-start(bf16[512,512]{1,0:T(8,128)(2,1)S(1)} %collective-permute-done.one_ref), channel_id=1, source_target_pairs={{0,8},{8,16},{16,24},{24,32},{32,40},{40,48},{48,56},{56,64},{64,7... | collective-permute-start | bytes 1572872 | tf_op jit(solution)/shard_map/ppermute | solution.py:292
  20.4 17.1 %collective-permute-done.1.two_ref = bf16[512,512]{1,0:T(8,128)(2,1)} collective-permute-done((bf16[512,512]{1,0:T(8,128)(2,1)S(1)}, bf16[512,512]{1,0:T(8,128)(2,1)}, u32[]{:S(2)}, u32[]{:S(2)}) %collective-permute-start.1) | collective-permute-done | bytes 524320 | tf_op jit(solution)/shard_map/ppermute | solution.py:292
  37.4 1.9 %collective-permute-start.2 = (bf16[512,512]{1,0:T(8,128)(2,1)}, bf16[512,512]{1,0:T(8,128)(2,1)}, u32[]{:S(2)}, u32[]{:S(2)}) collective-permute-start(bf16[512,512]{1,0:T(8,128)(2,1)} %collective-permute-done.1.two_ref), channel_id=1, source_target_pairs={{0,8},{8,16},{16,24},{24,32},{32,40},{40,48},{48,56},{56,64},{64,7... | collective-permute-start | bytes 1572872 | tf_op jit(solution)/shard_map/ppermute | solution.py:292
  39.4 0.1 constant_dynamic-slice_fusion
  39.4 0.0 copy-done.5
  39.4 1.2 %shard_map.119.spec_ref = f32[1024,256]{1,0:T(8,128)S(1)} custom-call(f32[8,16384]{1,0:T(8,128)S(1)} %copy-done.4, bf16[6,256,256]{2,1,0:T(8,128)(2,1)S(1)} %copy-done, f32[2,128,128]{2,1,0:T(8,128)S(1)} %copy-done.5), custom_call_target="tpu_custom_call" | custom-call | tf_op jit(solution)/shard_map/pallas_call | solution.py:63
  40.6 0.0 all-to-all-done.signal_ref
  40.6 0.1 broadcast_in_dim.12.taps_ref
  40.7 3.4 %shard_map.120 = bf16[64,8,256]{2,1,0:T(8,128)(2,1)} custom-call(bf16[64,8,384]{2,1,0:T(8,128)(2,1)S(1)} %all-to-all-done.signal_ref, f32[8,8,128]{2,1,0:T(8,128)S(1)} %broadcast_in_dim.12.taps_ref, f32[1024,256]{1,0:T(8,128)S(1)} %shard_map.119.spec_ref, bf16[6,256,256]{2,1,0:T(8,128)(2,1)S(1)} %copy-done, f32[2,128,128]{2,1,0:T(8,128)S(1)} %copy-done.5), custom_call_target="tpu_custom_call" | custom-call | tf_op jit(solution)/shard_map/pallas_call | solution.py:63
  44.0 11.0 %all-to-all-start.1 = ((bf16[64,8,256]{2,1,0:T(8,128)(2,1)}), bf16[64,8,256]{2,1,0:T(8,128)(2,1)S(1)}, u32[]{:S(2)}, u32[]{:S(2)}) async-start(bf16[64,8,256]{2,1,0:T(8,128)(2,1)} %shard_map.120), calls=%async_computation.1 | async-start | bytes 524288 | tf_op jit(solution)/shard_map/all_to_all | solution.py:287
  55.1 0.0 copy-start.1
  55.1 0.0 copy-start.2
  55.1 0.1 shard_map.121.query_t_ref
  55.2 0.0 collective-permute-done.2.three_ref
  55.3 0.8 copy-done.1
  56.0 0.1 copy-done.2
  56.1 3.4 %attention.1 = (f32[256,512]{1,0:T(8,128)S(1)}, f32[128,256]{1,0:T(8,128)S(1)}) custom-call(s32[1]{0:T(128)} %bitcast.block_ref, bf16[256,512]{1,0:T(8,128)(2,1)S(1)} %copy-done.8, bf16[256,512]{1,0:T(8,128)(2,1)S(1)} %copy-done.1, bf16[256,512]{1,0:T(8,128)(2,1)S(1)} %copy-done.2, bf16[512,512]{1,0:T(8,128)(2,1)S(1)} %collective-permute-done.one_ref, ...), custom_call_target="tpu_custom_call" | custom-call | tf_op jit(solution)/shard_map/attention/pallas_call | solution.py:207
  59.5 7.1 %all-to-all-done.1.returned_ref = bf16[64,8,256]{2,1,0:T(8,128)(2,1)S(1)} async-done(((bf16[64,8,256]{2,1,0:T(8,128)(2,1)}), bf16[64,8,256]{2,1,0:T(8,128)(2,1)S(1)}, u32[]{:S(2)}, u32[]{:S(2)}) %all-to-all-start.1) | async-done | bytes 262176 | tf_op jit(solution)/shard_map/all_to_all | solution.py:287
  66.6 0.7 shard_map.122
  67.3 10.1 %all-to-all-start.2 = ((f32[8,8,128]{2,1,0:T(8,128)}), f32[8,8,128]{2,1,0:T(8,128)S(1)}, u32[]{:S(2)}, u32[]{:S(2)}) async-start(f32[8,8,128]{2,1,0:T(8,128)} %shard_map.122), calls=%async_computation.2 | async-start | bytes 65536 | tf_op jit(solution)/shard_map/all_to_all | solution.py:298
  77.4 0.1 shard_map.123.mixed_ref
  77.6 0.0 copy-start.11
  77.6 10.0 %all-to-all-done.2.sums_ref = f32[8,8,128]{2,1,0:T(8,128)S(1)} async-done(((f32[8,8,128]{2,1,0:T(8,128)}), f32[8,8,128]{2,1,0:T(8,128)S(1)}, u32[]{:S(2)}, u32[]{:S(2)}) %all-to-all-start.2) | async-done | bytes 32800 | tf_op jit(solution)/shard_map/all_to_all | solution.py:298
  87.6 1.0 %shard_map.124 = bf16[256,512]{1,0:T(8,128)(2,1)} custom-call(f32[8,8,128]{2,1,0:T(8,128)S(1)} %all-to-all-done.2.sums_ref, f32[256,512]{1,0:T(8,128)S(1)} %get-tuple-element.8.att_ref, f32[256,512]{1,0:T(8,128)S(1)} %shard_map.123.mixed_ref, f32[1,512]{1,0:T(1,128)S(1)} %bitcast.4), custom_call_target="tpu_custom_call" | custom-call | tf_op jit(solution)/shard_map/pallas_call | solution.py:63
  (15 shorter events, 0.0 us)
Async XLA Ops:
  0.0 3.2 %copy-start.9 = (f32[8,512]{1,0:T(8,128)S(1)}, f32[8,512]{1,0:T(8,128)}, u32[]{:S(2)}) copy-start(f32[8,512]{1,0:T(8,128)} %taps_ref.1) | copy-start | bytes 49156
  0.0 3.2 %copy-start.6 = (bf16[256,512]{1,0:T(8,128)(2,1)S(1)}, bf16[256,512]{1,0:T(8,128)(2,1)}, u32[]{:S(2)}) copy-start(bf16[256,512]{1,0:T(8,128)(2,1)} %key_ref.2) | copy-start | bytes 786436
  0.0 3.2 %copy-start.7 = (bf16[256,512]{1,0:T(8,128)(2,1)S(1)}, bf16[256,512]{1,0:T(8,128)(2,1)}, u32[]{:S(2)}) copy-start(bf16[256,512]{1,0:T(8,128)(2,1)} %value_ref.2) | copy-start | bytes 786436
  1.1 38.3 %copy-start = (bf16[6,256,256]{2,1,0:T(8,128)(2,1)S(1)}, bf16[6,256,256]{2,1,0:T(8,128)(2,1)}, u32[]{:S(2)}) copy-start(bf16[6,256,256]{2,1,0:T(8,128)(2,1)} %constant.16.clone.tables_ref) | copy-start | bytes 2359300
  1.2 17.2 %collective-permute-start = (bf16[512,512]{1,0:T(8,128)(2,1)S(1)}, bf16[512,512]{1,0:T(8,128)(2,1)S(1)}, u32[]{:S(2)}, u32[]{:S(2)}) collective-permute-start(bf16[512,512]{1,0:T(8,128)(2,1)S(1)} %pad_maximum_fusion), channel_id=1, source_target_pairs={{0,8},{8,16},{16,24},{24,32},{32,40},{40,48},{48,56},{56,64},{64,7... | collective-permute-start | bytes 1572872 | tf_op jit(solution)/shard_map/ppermute | solution.py:292
  4.8 34.6 %copy-start.4 = (f32[8,16384]{1,0:T(8,128)S(1)}, f32[8,16384]{1,0:T(8,128)}, u32[]{:S(2)}) copy-start(f32[8,16384]{1,0:T(8,128)} %kernel_ref.1) | copy-start | bytes 1572868
  4.8 34.6 %copy-start.5 = (f32[2,128,128]{2,1,0:T(8,128)S(1)}, f32[2,128,128]{2,1,0:T(8,128)}, u32[]{:S(2)}) copy-start(f32[2,128,128]{2,1,0:T(8,128)} %constant.17.clone.twist_ref) | copy-start | bytes 393220
  4.8 35.8 %all-to-all-start = ((bf16[64,8,384]{2,1,0:T(8,128)(2,1)}), bf16[64,8,384]{2,1,0:T(8,128)(2,1)S(1)}, u32[]{:S(2)}, u32[]{:S(2)}) async-start(bf16[64,8,384]{2,1,0:T(8,128)(2,1)} %shard_map.118), calls=%async_computation | async-start | bytes 786432 | tf_op jit(solution)/shard_map/all_to_all | solution.py:277
  18.3 19.1 %collective-permute-start.1 = (bf16[512,512]{1,0:T(8,128)(2,1)S(1)}, bf16[512,512]{1,0:T(8,128)(2,1)}, u32[]{:S(2)}, u32[]{:S(2)}) collective-permute-start(bf16[512,512]{1,0:T(8,128)(2,1)S(1)} %collective-permute-done.one_ref), channel_id=1, source_target_pairs={{0,8},{8,16},{16,24},{24,32},{32,40},{40,48},{48,56},{56,64},{64,7... | collective-permute-start | bytes 1572872 | tf_op jit(solution)/shard_map/ppermute | solution.py:292
  37.4 17.8 %collective-permute-start.2 = (bf16[512,512]{1,0:T(8,128)(2,1)}, bf16[512,512]{1,0:T(8,128)(2,1)}, u32[]{:S(2)}, u32[]{:S(2)}) collective-permute-start(bf16[512,512]{1,0:T(8,128)(2,1)} %collective-permute-done.1.two_ref), channel_id=1, source_target_pairs={{0,8},{8,16},{16,24},{24,32},{32,40},{40,48},{48,56},{56,64},{64,7... | collective-permute-start | bytes 1572872 | tf_op jit(solution)/shard_map/ppermute | solution.py:292
  44.0 11.0 %copy-start.3 = (bf16[256,512]{1,0:T(8,128)(2,1)S(1)}, bf16[256,512]{1,0:T(8,128)(2,1)}, u32[]{:S(2)}) copy-start(bf16[256,512]{1,0:T(8,128)(2,1)} %query_ref.3) | copy-start | bytes 786436
  44.0 11.2 %copy-start.8 = (bf16[256,512]{1,0:T(8,128)(2,1)S(1)}, bf16[256,512]{1,0:T(8,128)(2,1)}, u32[]{:S(2)}) copy-start(bf16[256,512]{1,0:T(8,128)(2,1)} %query_ref.2) | copy-start | bytes 786436
  44.0 22.6 %all-to-all-start.1 = ((bf16[64,8,256]{2,1,0:T(8,128)(2,1)}), bf16[64,8,256]{2,1,0:T(8,128)(2,1)S(1)}, u32[]{:S(2)}, u32[]{:S(2)}) async-start(bf16[64,8,256]{2,1,0:T(8,128)(2,1)} %shard_map.120), calls=%async_computation.1 | async-start | bytes 524288 | tf_op jit(solution)/shard_map/all_to_all | solution.py:287
  55.1 1.0 %copy-start.1 = (bf16[256,512]{1,0:T(8,128)(2,1)S(1)}, bf16[256,512]{1,0:T(8,128)(2,1)}, u32[]{:S(2)}) copy-start(bf16[256,512]{1,0:T(8,128)(2,1)} %key_ref.3) | copy-start | bytes 786436
  55.1 1.0 %copy-start.2 = (bf16[256,512]{1,0:T(8,128)(2,1)S(1)}, bf16[256,512]{1,0:T(8,128)(2,1)}, u32[]{:S(2)}) copy-start(bf16[256,512]{1,0:T(8,128)(2,1)} %value_ref.3) | copy-start | bytes 786436
  66.6 10.9 %copy-start.10 = (f32[512]{0:T(512)S(1)}, f32[512]{0:T(512)}, u32[]{:S(2)}) copy-start(f32[512]{0:T(512)} %param.21) | copy-start | bytes 6148
  67.3 20.3 %all-to-all-start.2 = ((f32[8,8,128]{2,1,0:T(8,128)}), f32[8,8,128]{2,1,0:T(8,128)S(1)}, u32[]{:S(2)}, u32[]{:S(2)}) async-start(f32[8,8,128]{2,1,0:T(8,128)} %shard_map.122), calls=%async_computation.2 | async-start | bytes 65536 | tf_op jit(solution)/shard_map/all_to_all | solution.py:298
  77.6 10.0 %copy-start.11 = (f32[512]{0:T(512)S(1)}, f32[512]{0:T(512)}, u32[]{:S(2)}) copy-start(f32[512]{0:T(512)} %param.20) | copy-start | bytes 6148

commit v3 on v2

--- a/solution.py
+++ b/solution.py
@@ -14,7 +14,9 @@
 HD = 128
 TAPS = 8
 SPAN = 3
+SIDE = 4
 RADIX = 128
+VMEM_LIMIT = 20 * 2**20
 F32 = jnp.float32
 BF16 = jnp.bfloat16
 
@@ -43,10 +45,9 @@
         np.concatenate(split_table(last), 0),
         *split_table(ahead),
         *split_table(back),
+        np.concatenate(split_table(np.concatenate([np.cos(twist), np.sin(twist)], 1)), 0),
     ]
-    return jnp.asarray(np.stack(products)), jnp.asarray(
-        np.stack([np.cos(twist), np.sin(twist)]).astype(np.float32)
-    )
+    return jnp.asarray(np.stack(products))
 
 
 def halves(value):
@@ -58,13 +59,13 @@
     return lax.dot_general(left, right, (((1,), (0,)), ((), ())), preferred_element_type=F32)
 
 
-def kernel_call(body, out_shape, scratch=(), vmem=None):
+def kernel_call(body, out_shape, scratch=()):
     def call(*args):
         return pl.pallas_call(
             body,
             out_shape=out_shape,
             scratch_shapes=list(scratch),
-            compiler_params=pltpu.CompilerParams(vmem_limit_bytes=vmem or 48 * 2**20),
+            compiler_params=pltpu.CompilerParams(vmem_limit_bytes=VMEM_LIMIT),
         )(*args)
 
     return call
@@ -88,9 +89,13 @@
         ],
         0,
     )
-    shape = out_ref.shape[:2]
-    out_ref[:, :, 0:count] = product.T.astype(BF16).reshape(*shape, count)
-    out_ref[:, :, count:] = edges.T.astype(BF16).reshape(*shape, RADIX)
+    blocks, lines = out_ref.shape[:2]
+    product = product.T.reshape(blocks, SIDE, lines, count)
+    edges = edges.T.reshape(blocks, SIDE, lines, RADIX)
+    for i in range(SIDE):
+        out_ref[:, :, i * count : (i + 1) * count] = product[:, i].astype(BF16)
+    joined = jnp.concatenate([edges[:, i, :, : RADIX // SIDE] for i in range(SIDE)], 2)
+    out_ref[:, :, SIDE * count :] = joined.astype(BF16)
 
 
 def product3(value, table_hi, table_lo):
@@ -98,8 +103,14 @@
     return mm(high, table_hi) + mm(low, table_hi) + mm(high, table_lo)
 
 
-def spectrum(step, tables_ref, twist_ref):
-    cos, sin = twist_ref[0], twist_ref[1]
+def twists(tables_ref):
+    table = tables_ref[6].astype(F32)
+    table = table[:RADIX] + table[RADIX:]
+    return table[:, :RADIX], table[:, RADIX:]
+
+
+def spectrum(step, tables_ref):
+    cos, sin = twists(tables_ref)
     turned = []
     for c in range(step.shape[1] // RADIX):
         lanes = slice(c * RADIX, (c + 1) * RADIX)
@@ -112,7 +123,7 @@
     return jnp.concatenate([rows_ref[pl.ds(c, RADIX, stride=channels), :] for c in range(channels)], 1)
 
 
-def kernel_spectrum_body(half, kernel_ref, tables_ref, twist_ref, out_ref, rows_ref):
+def kernel_spectrum_body(half, kernel_ref, tables_ref, out_ref, rows_ref):
     channels = kernel_ref.shape[0]
     for a in range(RADIX):
         row = ((a % half) * (RADIX // half) + a // half) * channels
@@ -120,12 +131,19 @@
     high, low = halves(gather_rows(rows_ref, channels))
     first_hi, first_lo = tables_ref[0, :, :RADIX], tables_ref[0, :, RADIX:]
     step = mm(first_hi, high) + mm(first_hi, low) + mm(first_lo, high)
-    out_ref[...] = spectrum(step, tables_ref, twist_ref)
+    out_ref[...] = spectrum(step, tables_ref)
+
+
+def channel_rows(signal_ref, count, h):
+    return jnp.concatenate(
+        [signal_ref[:, :, i * count + h * RADIX : i * count + (h + 1) * RADIX].astype(F32) for i in range(SIDE)], 1
+    )
 
 
 def first_tokens(signal_ref, taps_ref, count):
-    own = signal_ref[:, :, count:].astype(F32)
-    head = signal_ref[:, :, :RADIX].astype(F32)
+    own = signal_ref[:, :, SIDE * count :].astype(F32)
+    own = jnp.concatenate([own] + [jnp.roll(own, -i * (RADIX // SIDE), 2) for i in range(1, SIDE)], 1)
+    head = channel_rows(signal_ref, count, 0)
     previous = jnp.concatenate([jnp.zeros_like(own[:1]), own[:-1]], 0)
     sources, channels = own.shape[:2]
     own, previous, head = (x.reshape(sources * channels, RADIX) for x in (own, previous, head))
@@ -133,27 +151,28 @@
     window = jnp.where(lane < 16, previous, pltpu.roll(own, 16, 1))
     total = jnp.zeros_like(window)
     for j in range(TAPS):
-        tap = jnp.broadcast_to(taps_ref[j][None], (sources, channels, RADIX)).reshape(window.shape)
+        tap = jnp.broadcast_to(taps_ref[:, j : j + 1], (channels, RADIX))[None]
+        tap = jnp.broadcast_to(tap, (sources, channels, RADIX)).reshape(window.shape)
         total = total + tap * (pltpu.roll(window, j, 1) if j else window)
     return jnp.where(lane < 8, pltpu.roll(total * own, RADIX - 16, 1), head)
 
 
-def filter_body(signal_ref, taps_ref, spec_ref, tables_ref, twist_ref, out_ref, rows_ref, back_ref):
+def filter_body(signal_ref, taps_ref, spec_ref, tables_ref, out_ref, rows_ref, back_ref):
     sources, channels, count = out_ref.shape
     half = count // RADIX
     rows = sources * channels
     rows_ref[:rows, :] = first_tokens(signal_ref, taps_ref, count)
     for h in range(1, half):
-        part = signal_ref[:, :, h * RADIX : (h + 1) * RADIX].astype(F32)
+        part = channel_rows(signal_ref, count, h)
         rows_ref[h * rows : (h + 1) * rows, :] = part.reshape(rows, RADIX)
     data = gather_rows(rows_ref, channels).astype(BF16)
     step = mm(tables_ref[0], jnp.concatenate([data, data], 0))
-    both = spectrum(step, tables_ref, twist_ref)
+    both = spectrum(step, tables_ref)
     sig_r, sig_i = both[:, :RADIX], both[:, RADIX:]
     ker_r, ker_i = spec_ref[:, :RADIX], spec_ref[:, RADIX:]
     both = jnp.concatenate([sig_r * ker_r - sig_i * ker_i, sig_r * ker_i + sig_i * ker_r], 1)
     both = product3(both, tables_ref[4], tables_ref[5])
-    cos, sin = twist_ref[0], twist_ref[1]
+    cos, sin = twists(tables_ref)
     turned = []
     for c in range(channels):
         lines = slice(c * RADIX, (c + 1) * RADIX)
@@ -209,7 +228,7 @@
         out_shape=(jax.ShapeDtypeStruct((count, width), F32), jax.ShapeDtypeStruct((HD, count), F32)),
         in_specs=[pl.BlockSpec(memory_space=pltpu.SMEM)] + [vmem] * 6,
         out_specs=(vmem, vmem),
-        compiler_params=pltpu.CompilerParams(vmem_limit_bytes=48 * 2**20),
+        compiler_params=pltpu.CompilerParams(vmem_limit_bytes=VMEM_LIMIT),
         name="attention",
     )(block, query, key, value, one, two, three)
 
@@ -267,32 +286,32 @@
     peers = lax.axis_size("head")
     channels = width // blocks
     sds = jax.ShapeDtypeStruct
-    tables, twist = conv_tables(count)
+    tables = conv_tables(count)
     onward = [(i, i + 1) for i in range(blocks - 1)]
     seq = lax.axis_index("seq")
 
     signal = kernel_call(
-        shift_body, sds((blocks, channels, count + RADIX), BF16), [pltpu.VMEM((count + 8, width), F32)]
+        shift_body, sds((blocks, channels // SIDE, SIDE * count + RADIX), BF16), [pltpu.VMEM((count + 8, width), F32)]
     )(mixer_key, mixer_value, shift_taps)
     received = lax.all_to_all(signal, "seq", 0, 0, tiled=True)
-    own_taps = lax.dynamic_slice(shift_taps, (0, seq * channels), (TAPS, channels))
-    own_taps = jnp.broadcast_to(own_taps[:, :, None], (TAPS, channels, RADIX))
+    own_taps = lax.dynamic_slice(shift_taps, (0, seq * channels), (TAPS, channels)).T
     rows = pltpu.VMEM((channels * RADIX, RADIX), F32)
     kernel_spectrum = kernel_call(
         functools.partial(kernel_spectrum_body, count // RADIX), sds((channels * RADIX, 2 * RADIX), F32), [rows]
-    )(conv_kernel, tables, twist)
+    )(conv_kernel, tables)
     filtered = kernel_call(
         filter_body, sds((blocks, channels, count), BF16), [rows, rows]
-    )(received, own_taps, kernel_spectrum, tables, twist)
+    )(received, own_taps, kernel_spectrum, tables)
     returned = lax.all_to_all(filtered, "seq", 0, 0, tiled=True)
 
-    carried = jnp.concatenate([heads_key, heads_value], 0)
-    earlier = []
-    for _ in range(SPAN):
-        carried = lax.ppermute(carried, "seq", onward)
-        earlier.append(carried)
+    own = jnp.concatenate([heads_key, heads_value], 0)
+    two_back = lax.ppermute(own, "seq", [(i, i + 2) for i in range(blocks - 2)])
+    one_back = lax.ppermute(
+        jnp.where(seq % 2 == 1, two_back, own), "seq", [(i, i ^ 1) for i in range(blocks)]
+    )
+    three_back = lax.ppermute(two_back, "seq", onward)
     block = seq.astype(jnp.int32).reshape(1)
-    attention_branch, attention_squares = attend(block, heads_query, heads_key, heads_value, *earlier)
+    attention_branch, attention_squares = attend(block, heads_query, heads_key, heads_value, one_back, two_back, three_back)
     query_t = kernel_call(transpose_body, sds((width, count), BF16))(mixer_query)
     sums = kernel_call(sums_body, sds((peers, 8, RADIX), F32))(returned, query_t, attention_squares)
     gathered = lax.all_to_all(sums, "head", 0, 0, tiled=True)

time: 90.1 us -> 82.9 us (0.920)
  waiting for transfers between devices: 34.2 us -> 21.7 us
  starting transfers between devices: 40.6 us -> 43.6 us
  local copies, waits for them, and re-layouts: 1.04 us -> 3.13 us
    ppermute x3, waiting for transfers between devices: 17.1 us -> 3.44 us  [the longest x1 3.43 us: mixer(): two_back = lax.ppermute(own, 'seq', [(i, i + 2) for i in range(blocks - 2)])]
    all_to_all x1, starting transfers between devices: 10.1 us -> 14.3 us  [mixer(): gathered = lax.all_to_all(sums, 'head', 0, 0, tiled=True)]
    ppermute x3, starting transfers between devices: 5.99 us -> 8.73 us  [the longest x1 4.41 us: mixer(): two_back = lax.ppermute(own, 'seq', [(i, i + 2) for i in range(blocks - 2)])]
    all_to_all x1, starting transfers between devices: 13.5 us -> 11.3 us  [mixer(): received = lax.all_to_all(signal, 'seq', 0, 0, tiled=True)]
    unnamed x24, local copies, waits for them, and re-layouts: 0.9 us -> 3.03 us
    all_to_all x1, starting transfers between devices: 11 us -> 9.31 us  [mixer(): returned = lax.all_to_all(filtered, 'seq', 0, 0, tiled=True)]
    concatenate x1 -> x0, other arithmetic: 1.13 us -> none  [mixer(): carried = jnp.concatenate([heads_key, heads_value], 0)]
    all_to_all x1, waiting for transfers between devices: 0.01 us -> 1.11 us  [mixer(): received = lax.all_to_all(signal, 'seq', 0, 0, tiled=True)]
  transfers between devices with their start and end apart: 6 -> 6, of which waited for: 3 -> 4; matrix products, arithmetic and copies ran while one was open for 0% -> 1% of each run, Pallas kernels for 11% -> 13%
where the time goes in v3:
time: 82.9 us; the launch traced here: 81.4 us
  starting transfers between devices  43.6 us (53%)
  waiting for transfers between devices  21.7 us (26%)
  Pallas kernels  11.9 us (14%)
  local copies, waits for them, and re-layouts  3.13 us (4%)
  other arithmetic  0.87 us (1%)
    all_to_all x1, starting transfers between devices, mixer(): gathered = lax.all_to_all(sums, 'head', 0, 0, tiled=True)  14.3 us
    all_to_all x1, starting transfers between devices, mixer(): received = lax.all_to_all(signal, 'seq', 0, 0, tiled=True)  11.3 us
    all_to_all x1, waiting for transfers between devices, mixer(): gathered = lax.all_to_all(sums, 'head', 0, 0, tiled=True)  10 us
    all_to_all x1, starting transfers between devices, mixer(): returned = lax.all_to_all(filtered, 'seq', 0, 0, tiled=True)  9.31 us
    pallas_call x7, Pallas kernels, call(): pl.pallas_call(body, out_shape=out_shape, scratch_shapes=list(scratch), c...  8.56 us
    all_to_all x1, waiting for transfers between devices, mixer(): returned = lax.all_to_all(filtered, 'seq', 0, 0, tiled=True)  7.12 us
    ppermute x1, starting transfers between devices, mixer(): two_back = lax.ppermute(own, 'seq', [(i, i + 2) for i in range(blocks - 2)])  4.41 us
    ppermute x1, waiting for transfers between devices, mixer(): two_back = lax.ppermute(own, 'seq', [(i, i + 2) for i in range(blocks - 2)])  3.43 us
  transfers between devices with their start and end apart: 6, of which 4 were waited for; matrix products, arithmetic and copies ran while one was open for 1% of the time, Pallas kernels for 13%

profile of v3, /device:TPU:56, one launch (start us, length us, event | category | flops | bytes accessed | tf_op | source)
XLA Modules:
  0.0 81.4 jit_solution(2680184281094161760)
XLA Ops:
  0.0 1.0 %constant_dynamic-update-slice_fusion.1 = bf16[512,512]{1,0:T(8,128)(2,1)S(1)} fusion(bf16[256,512]{1,0:T(8,128)(2,1)} %key_ref.3), kind=kLoop, calls=%fused_computation.2 | loop fusion | bytes 524288
  1.0 0.0 copy-done.2
  1.0 0.0 copy-start.5
  1.0 0.0 copy-start.6
  1.1 4.4 %collective-permute-start = (bf16[512,512]{1,0:T(8,128)(2,1)S(1)}, bf16[512,512]{1,0:T(8,128)(2,1)S(1)}, u32[]{:S(2)}, u32[]{:S(2)}) collective-permute-start(bf16[512,512]{1,0:T(8,128)(2,1)S(1)} %constant_dynamic-update-slice_fusion), channel_id=1, source_target_pairs={{0,16},{8,24},{16,32},{24,40},{32,48},{40,56},{48,64},{56,72},{64,... | collective-permute-start | bytes 1572872 | tf_op jit(solution)/shard_map/ppermute | solution.py:308
  5.5 1.8 %shard_map.109 = bf16[64,2,1152]{2,1,0:T(2,128)(2,1)} custom-call(bf16[256,512]{1,0:T(8,128)(2,1)S(1)} %copy-done.5, bf16[256,512]{1,0:T(8,128)(2,1)S(1)} %copy-done.6, f32[8,512]{1,0:T(8,128)S(1)} %copy-done.8), custom_call_target="tpu_custom_call" | custom-call | tf_op jit(solution)/shard_map/pallas_call | solution.py:64
  7.3 11.3 %all-to-all-start = ((bf16[64,2,1152]{2,1,0:T(2,128)(2,1)}), bf16[64,2,1152]{2,1,0:T(2,128)(2,1)S(1)}, u32[]{:S(2)}, u32[]{:S(2)}) async-start(bf16[64,2,1152]{2,1,0:T(2,128)(2,1)} %shard_map.109), calls=%async_computation | async-start | bytes 589824 | tf_op jit(solution)/shard_map/all_to_all | solution.py:296
  18.6 0.0 copy-start
  18.6 3.4 %collective-permute-done.two_ref = bf16[512,512]{1,0:T(8,128)(2,1)S(1)} collective-permute-done((bf16[512,512]{1,0:T(8,128)(2,1)S(1)}, bf16[512,512]{1,0:T(8,128)(2,1)S(1)}, u32[]{:S(2)}, u32[]{:S(2)}) %collective-permute-start) | collective-permute-done | bytes 524320 | tf_op jit(solution)/shard_map/ppermute | solution.py:308
  22.1 0.9 %broadcast_select_fusion = bf16[512,512]{1,0:T(8,128)(2,1)} fusion(bf16[512,512]{1,0:T(8,128)(2,1)S(1)} %collective-permute-done.two_ref, bf16[512,512]{1,0:T(8,128)(2,1)S(1)} %constant_dynamic-update-slice_fusion, pred[]{:T(512)S(6)} %eq.5), kind=kLoop, calls=%fused_computation | loop fusion | flops 262144 | bytes 1572865 | tf_op jit(solution)/shard_map/jit(_where)/select_n | solution.py:310
  22.9 1.9 %collective-permute-start.1 = (bf16[512,512]{1,0:T(8,128)(2,1)}, bf16[512,512]{1,0:T(8,128)(2,1)}, u32[]{:S(2)}, u32[]{:S(2)}) collective-permute-start(bf16[512,512]{1,0:T(8,128)(2,1)} %broadcast_select_fusion), channel_id=1, source_target_pairs={{0,8},{8,0},{16,24},{24,16},{32,40},{40,32},{48,56},{56,48},{64,72... | collective-permute-start | bytes 1572872 | tf_op jit(solution)/shard_map/ppermute | solution.py:309
  24.8 2.4 %collective-permute-start.2 = (bf16[512,512]{1,0:T(8,128)(2,1)S(1)}, bf16[512,512]{1,0:T(8,128)(2,1)}, u32[]{:S(2)}, u32[]{:S(2)}) collective-permute-start(bf16[512,512]{1,0:T(8,128)(2,1)S(1)} %collective-permute-done.two_ref), channel_id=1, source_target_pairs={{0,8},{8,16},{16,24},{24,32},{32,40},{40,48},{48,56},{56,64},{64,7... | collective-permute-start | bytes 1572872 | tf_op jit(solution)/shard_map/ppermute | solution.py:312
  27.3 0.1 constant_dynamic-slice_fusion
  27.3 0.1 copy.13
  27.4 1.0 %copy-done.4 = f32[8,16384]{1,0:T(8,128)S(1)} copy-done((f32[8,16384]{1,0:T(8,128)S(1)}, f32[8,16384]{1,0:T(8,128)}, u32[]{:S(2)}) %copy-start.4) | copy-done | bytes 524312
  28.5 1.2 %shard_map.110.spec_ref = f32[1024,256]{1,0:T(8,128)S(1)} custom-call(f32[8,16384]{1,0:T(8,128)S(1)} %copy-done.4, bf16[7,256,256]{2,1,0:T(8,128)(2,1)S(1)} %copy-done), custom_call_target="tpu_custom_call" | custom-call | tf_op jit(solution)/shard_map/pallas_call | solution.py:64
  29.6 1.1 %all-to-all-done.signal_ref = bf16[64,2,1152]{2,1,0:T(2,128)(2,1)S(1)} async-done(((bf16[64,2,1152]{2,1,0:T(2,128)(2,1)}), bf16[64,2,1152]{2,1,0:T(2,128)(2,1)S(1)}, u32[]{:S(2)}, u32[]{:S(2)}) %all-to-all-start) | async-done | bytes 294944 | tf_op jit(solution)/shard_map/all_to_all | solution.py:296
  30.7 3.7 %shard_map.111 = bf16[64,8,256]{2,1,0:T(8,128)(2,1)} custom-call(bf16[64,2,1152]{2,1,0:T(2,128)(2,1)S(1)} %all-to-all-done.signal_ref, f32[8,8]{1,0:T(8,128)S(1)} %bitcast.4, f32[1024,256]{1,0:T(8,128)S(1)} %shard_map.110.spec_ref, bf16[7,256,256]{2,1,0:T(8,128)(2,1)S(1)} %copy-done), custom_call_target="tpu_custom_call" | custom-call | tf_op jit(solution)/shard_map/pallas_call | solution.py:64
  34.4 9.3 %all-to-all-start.1 = ((bf16[64,8,256]{2,1,0:T(8,128)(2,1)}), bf16[64,8,256]{2,1,0:T(8,128)(2,1)S(1)}, u32[]{:S(2)}, u32[]{:S(2)}) async-start(bf16[64,8,256]{2,1,0:T(8,128)(2,1)} %shard_map.111), calls=%async_computation.1 | async-start | bytes 524288 | tf_op jit(solution)/shard_map/all_to_all | solution.py:305
  43.7 0.0 copy-start.1
  43.7 0.0 copy-start.7
  43.8 0.1 shard_map.112.query_t_ref
  43.9 0.8 copy-done.1
  44.7 0.1 copy-done.7
  44.8 3.4 %attention.1 = (f32[256,512]{1,0:T(8,128)S(1)}, f32[128,256]{1,0:T(8,128)S(1)}) custom-call(s32[1]{0:T(128)} %bitcast.1.block_ref, bf16[256,512]{1,0:T(8,128)(2,1)S(1)} %copy-done.7, bf16[256,512]{1,0:T(8,128)(2,1)S(1)} %copy-done.1, bf16[256,512]{1,0:T(8,128)(2,1)S(1)} %copy-done.2, bf16[512,512]{1,0:T(8,128)(2,1)} %collective-permute-done.1.one_ref, ...), custom_call_target="tpu_custom_call" | custom-call | tf_op jit(solution)/shard_map/attention/pallas_call | solution.py:226
  48.1 7.1 %all-to-all-done.1.returned_ref = bf16[64,8,256]{2,1,0:T(8,128)(2,1)S(1)} async-done(((bf16[64,8,256]{2,1,0:T(8,128)(2,1)}), bf16[64,8,256]{2,1,0:T(8,128)(2,1)S(1)}, u32[]{:S(2)}, u32[]{:S(2)}) %all-to-all-start.1) | async-done | bytes 262176 | tf_op jit(solution)/shard_map/all_to_all | solution.py:305
  55.3 0.7 shard_map.113
  56.0 14.3 %all-to-all-start.2 = ((f32[8,8,128]{2,1,0:T(8,128)}), f32[8,8,128]{2,1,0:T(8,128)S(1)}, u32[]{:S(2)}, u32[]{:S(2)}) async-start(f32[8,8,128]{2,1,0:T(8,128)} %shard_map.113), calls=%async_computation.2 | async-start | bytes 65536 | tf_op jit(solution)/shard_map/all_to_all | solution.py:317
  70.3 0.1 shard_map.114.mixed_ref
  70.4 0.0 copy-start.10
  70.4 10.0 %all-to-all-done.2.sums_ref = f32[8,8,128]{2,1,0:T(8,128)S(1)} async-done(((f32[8,8,128]{2,1,0:T(8,128)}), f32[8,8,128]{2,1,0:T(8,128)S(1)}, u32[]{:S(2)}, u32[]{:S(2)}) %all-to-all-start.2) | async-done | bytes 32800 | tf_op jit(solution)/shard_map/all_to_all | solution.py:317
  80.4 1.0 %shard_map.115 = bf16[256,512]{1,0:T(8,128)(2,1)} custom-call(f32[8,8,128]{2,1,0:T(8,128)S(1)} %all-to-all-done.2.sums_ref, f32[256,512]{1,0:T(8,128)S(1)} %get-tuple-element.8.att_ref, f32[256,512]{1,0:T(8,128)S(1)} %shard_map.114.mixed_ref, f32[1,512]{1,0:T(1,128)S(1)} %bitcast.6), custom_call_target="tpu_custom_call" | custom-call | tf_op jit(solution)/shard_map/pallas_call | solution.py:64
  (15 shorter events, 0.0 us)
Async XLA Ops:
  0.0 1.0 %copy-start.2 = (bf16[256,512]{1,0:T(8,128)(2,1)S(1)}, bf16[256,512]{1,0:T(8,128)(2,1)}, u32[]{:S(2)}) copy-start(bf16[256,512]{1,0:T(8,128)(2,1)} %value_ref.3) | copy-start | bytes 786436
  0.0 5.5 %copy-start.8 = (f32[8,512]{1,0:T(8,128)S(1)}, f32[8,512]{1,0:T(8,128)}, u32[]{:S(2)}) copy-start(f32[8,512]{1,0:T(8,128)} %taps_ref.1) | copy-start | bytes 49156
  1.0 4.5 %copy-start.5 = (bf16[256,512]{1,0:T(8,128)(2,1)S(1)}, bf16[256,512]{1,0:T(8,128)(2,1)}, u32[]{:S(2)}) copy-start(bf16[256,512]{1,0:T(8,128)(2,1)} %key_ref.2) | copy-start | bytes 786436
  1.0 4.5 %copy-start.6 = (bf16[256,512]{1,0:T(8,128)(2,1)S(1)}, bf16[256,512]{1,0:T(8,128)(2,1)}, u32[]{:S(2)}) copy-start(bf16[256,512]{1,0:T(8,128)(2,1)} %value_ref.2) | copy-start | bytes 786436
  1.1 21.0 %collective-permute-start = (bf16[512,512]{1,0:T(8,128)(2,1)S(1)}, bf16[512,512]{1,0:T(8,128)(2,1)S(1)}, u32[]{:S(2)}, u32[]{:S(2)}) collective-permute-start(bf16[512,512]{1,0:T(8,128)(2,1)S(1)} %constant_dynamic-update-slice_fusion), channel_id=1, source_target_pairs={{0,16},{8,24},{16,32},{24,40},{32,48},{40,56},{48,64},{56,72},{64,... | collective-permute-start | bytes 1572872 | tf_op jit(solution)/shard_map/ppermute | solution.py:308
  7.3 23.4 %all-to-all-start = ((bf16[64,2,1152]{2,1,0:T(2,128)(2,1)}), bf16[64,2,1152]{2,1,0:T(2,128)(2,1)S(1)}, u32[]{:S(2)}, u32[]{:S(2)}) async-start(bf16[64,2,1152]{2,1,0:T(2,128)(2,1)} %shard_map.109), calls=%async_computation | async-start | bytes 589824 | tf_op jit(solution)/shard_map/all_to_all | solution.py:296
  18.6 8.8 %copy-start = (bf16[7,256,256]{2,1,0:T(8,128)(2,1)S(1)}, bf16[7,256,256]{2,1,0:T(8,128)(2,1)}, u32[]{:S(2)}) copy-start(bf16[7,256,256]{2,1,0:T(8,128)(2,1)} %constant.27.clone.tables_ref) | copy-start | bytes 2752516
  22.9 21.0 %collective-permute-start.1 = (bf16[512,512]{1,0:T(8,128)(2,1)}, bf16[512,512]{1,0:T(8,128)(2,1)}, u32[]{:S(2)}, u32[]{:S(2)}) collective-permute-start(bf16[512,512]{1,0:T(8,128)(2,1)} %broadcast_select_fusion), channel_id=1, source_target_pairs={{0,8},{8,0},{16,24},{24,16},{32,40},{40,32},{48,56},{56,48},{64,72... | collective-permute-start | bytes 1572872 | tf_op jit(solution)/shard_map/ppermute | solution.py:309
  24.8 19.1 %collective-permute-start.2 = (bf16[512,512]{1,0:T(8,128)(2,1)S(1)}, bf16[512,512]{1,0:T(8,128)(2,1)}, u32[]{:S(2)}, u32[]{:S(2)}) collective-permute-start(bf16[512,512]{1,0:T(8,128)(2,1)S(1)} %collective-permute-done.two_ref), channel_id=1, source_target_pairs={{0,8},{8,16},{16,24},{24,32},{32,40},{40,48},{48,56},{56,64},{64,7... | collective-permute-start | bytes 1572872 | tf_op jit(solution)/shard_map/ppermute | solution.py:312
  27.4 1.0 %copy-start.4 = (f32[8,16384]{1,0:T(8,128)S(1)}, f32[8,16384]{1,0:T(8,128)}, u32[]{:S(2)}) copy-start(f32[8,16384]{1,0:T(8,128)} %kernel_ref.1) | copy-start | bytes 1572868
  34.4 9.3 %copy-start.3 = (bf16[256,512]{1,0:T(8,128)(2,1)S(1)}, bf16[256,512]{1,0:T(8,128)(2,1)}, u32[]{:S(2)}) copy-start(bf16[256,512]{1,0:T(8,128)(2,1)} %query_ref.3) | copy-start | bytes 786436
  34.4 20.8 %all-to-all-start.1 = ((bf16[64,8,256]{2,1,0:T(8,128)(2,1)}), bf16[64,8,256]{2,1,0:T(8,128)(2,1)S(1)}, u32[]{:S(2)}, u32[]{:S(2)}) async-start(bf16[64,8,256]{2,1,0:T(8,128)(2,1)} %shard_map.111), calls=%async_computation.1 | async-start | bytes 524288 | tf_op jit(solution)/shard_map/all_to_all | solution.py:305
  43.7 1.0 %copy-start.1 = (bf16[256,512]{1,0:T(8,128)(2,1)S(1)}, bf16[256,512]{1,0:T(8,128)(2,1)}, u32[]{:S(2)}) copy-start(bf16[256,512]{1,0:T(8,128)(2,1)} %key_ref.3) | copy-start | bytes 786436
  43.7 1.0 %copy-start.7 = (bf16[256,512]{1,0:T(8,128)(2,1)S(1)}, bf16[256,512]{1,0:T(8,128)(2,1)}, u32[]{:S(2)}) copy-start(bf16[256,512]{1,0:T(8,128)(2,1)} %query_ref.2) | copy-start | bytes 786436
  55.3 15.0 %copy-start.9 = (f32[512]{0:T(512)S(1)}, f32[512]{0:T(512)}, u32[]{:S(2)}) copy-start(f32[512]{0:T(512)} %param.20) | copy-start | bytes 6148
  56.0 24.4 %all-to-all-start.2 = ((f32[8,8,128]{2,1,0:T(8,128)}), f32[8,8,128]{2,1,0:T(8,128)S(1)}, u32[]{:S(2)}, u32[]{:S(2)}) async-start(f32[8,8,128]{2,1,0:T(8,128)} %shard_map.113), calls=%async_computation.2 | async-start | bytes 65536 | tf_op jit(solution)/shard_map/all_to_all | solution.py:317
  70.4 10.0 %copy-start.10 = (f32[512]{0:T(512)S(1)}, f32[512]{0:T(512)}, u32[]{:S(2)}) copy-start(f32[512]{0:T(512)} %param.19) | copy-start | bytes 6148

commit v4 on v3

--- a/solution.py
+++ b/solution.py
@@ -129,8 +129,7 @@
         row = ((a % half) * (RADIX // half) + a // half) * channels
         rows_ref[row : row + channels, :] = kernel_ref[:, a * RADIX : (a + 1) * RADIX]
     high, low = halves(gather_rows(rows_ref, channels))
-    first_hi, first_lo = tables_ref[0, :, :RADIX], tables_ref[0, :, RADIX:]
-    step = mm(first_hi, high) + mm(first_hi, low) + mm(first_lo, high)
+    step = mm(tables_ref[0], jnp.concatenate([high, high], 0)) + mm(tables_ref[0, :, :RADIX], low)
     out_ref[...] = spectrum(step, tables_ref)
 
 
@@ -179,8 +178,8 @@
         real, imag = both[lines, :RADIX], both[lines, RADIX:]
         turned.append(jnp.concatenate([real * cos - imag * sin, imag * cos + real * sin], 0))
     high, low = halves(jnp.concatenate(turned, 1))
-    last_hi, last_lo = tables_ref[1, :RADIX], tables_ref[1, RADIX:]
-    result = mm(last_hi, high) + mm(last_hi, low) + mm(last_lo, high)
+    both = mm(tables_ref[1], high)
+    result = both[:RADIX] + both[RADIX:] + mm(tables_ref[1, :RADIX], low)
     for c in range(channels):
         back_ref[pl.ds(c, RADIX, stride=channels), :] = result[:, c * RADIX : (c + 1) * RADIX]
     for h in range(half):
@@ -306,10 +305,13 @@
 
     own = jnp.concatenate([heads_key, heads_value], 0)
     two_back = lax.ppermute(own, "seq", [(i, i + 2) for i in range(blocks - 2)])
-    one_back = lax.ppermute(
-        jnp.where(seq % 2 == 1, two_back, own), "seq", [(i, i ^ 1) for i in range(blocks)]
-    )
     three_back = lax.ppermute(two_back, "seq", onward)
+    two_back, three_back = lax.optimization_barrier((two_back, three_back))
+    odd = seq % 2 == 1
+    exchanged = jnp.concatenate(
+        [jnp.where(odd, two_back[:count], heads_key), jnp.where(odd, two_back[count:], heads_value)], 0
+    )
+    one_back = lax.ppermute(exchanged, "seq", [(i, i ^ 1) for i in range(blocks)])
     block = seq.astype(jnp.int32).reshape(1)
     attention_branch, attention_squares = attend(block, heads_query, heads_key, heads_value, one_back, two_back, three_back)
     query_t = kernel_call(transpose_body, sds((width, count), BF16))(mixer_query)

time: 82.9 us -> 95 us (1.15)
  waiting for transfers between devices: 21.7 us -> 39.8 us
  starting transfers between devices: 43.6 us -> 37 us
  other arithmetic: 0.87 us -> 2 us
  Pallas kernels: 11.9 us -> 10.9 us
    ppermute x1, waiting for transfers between devices: 3.43 us -> 16.3 us  [mixer(): two_back = lax.ppermute(own, 'seq', [(i, i + 2) for i in range(blocks - 2)])]
    all_to_all x1, waiting for transfers between devices: 1.11 us -> 6.15 us  [mixer(): received = lax.all_to_all(signal, 'seq', 0, 0, tiled=True)]
    all_to_all x1, starting transfers between devices: 9.31 us -> 6.35 us  [mixer(): returned = lax.all_to_all(filtered, 'seq', 0, 0, tiled=True)]
    all_to_all x1, starting transfers between devices: 14.3 us -> 11.5 us  [mixer(): gathered = lax.all_to_all(sums, 'head', 0, 0, tiled=True)]
    concatenate x0 -> x2, other arithmetic: none -> 1.95 us  [the longest x1 1.13 us: mixer(): own = jnp.concatenate([heads_key, heads_value], 0)]
    unnamed x24 -> x29, local copies, waits for them, and re-layouts: 3.03 us -> 3.44 us
  transfers between devices with their start and end apart: 6 -> 6, of which waited for: 4 -> 4; matrix products, arithmetic and copies ran while one was open for 1% -> 1% of each run, Pallas kernels for 13% -> 10%
where the time goes in v4:
time: 95 us; the launch traced here: 93.4 us
  waiting for transfers between devices  39.8 us (42%)
  starting transfers between devices  37 us (39%)
  Pallas kernels  10.9 us (11%)
  local copies, waits for them, and re-layouts  3.52 us (4%)
  other arithmetic  2 us (2%)
    ppermute x1, waiting for transfers between devices, mixer(): two_back = lax.ppermute(own, 'seq', [(i, i + 2) for i in range(blocks - 2)])  16.3 us
    all_to_all x1, starting transfers between devices, mixer(): gathered = lax.all_to_all(sums, 'head', 0, 0, tiled=True)  11.5 us
    all_to_all x1, starting transfers between devices, mixer(): received = lax.all_to_all(signal, 'seq', 0, 0, tiled=True)  10.9 us
    all_to_all x1, waiting for transfers between devices, mixer(): gathered = lax.all_to_all(sums, 'head', 0, 0, tiled=True)  10 us
    pallas_call x7, Pallas kernels, call(): pl.pallas_call(body, out_shape=out_shape, scratch_shapes=list(scratch), c...  7.68 us
    all_to_all x1, waiting for transfers between devices, mixer(): returned = lax.all_to_all(filtered, 'seq', 0, 0, tiled=True)  7.36 us
    all_to_all x1, starting transfers between devices, mixer(): returned = lax.all_to_all(filtered, 'seq', 0, 0, tiled=True)  6.35 us
    all_to_all x1, waiting for transfers between devices, mixer(): received = lax.all_to_all(signal, 'seq', 0, 0, tiled=True)  6.15 us
  transfers between devices with their start and end apart: 6, of which 4 were waited for; matrix products, arithmetic and copies ran while one was open for 1% of the time, Pallas kernels for 10%

profile of v4, /device:TPU:56, one launch (start us, length us, event | category | flops | bytes accessed | tf_op | source)
XLA Modules:
  0.0 93.4 jit_solution(4268459267225406972)
XLA Ops:
  0.0 1.1 %pad_maximum_fusion = bf16[512,512]{1,0:T(8,128)(2,1)S(1)} fusion(bf16[256,512]{1,0:T(8,128)(2,1)} %value_ref.3, bf16[256,512]{1,0:T(8,128)(2,1)} %key_ref.3), kind=kLoop, calls=%fused_computation | loop fusion | flops 1048576 | bytes 1048576 | tf_op jit(solution)/shard_map/concatenate | solution.py:306
  1.1 4.3 %collective-permute-start = (bf16[512,512]{1,0:T(8,128)(2,1)S(1)}, bf16[512,512]{1,0:T(8,128)(2,1)S(1)}, u32[]{:S(2)}, u32[]{:S(2)}) collective-permute-start(bf16[512,512]{1,0:T(8,128)(2,1)S(1)} %pad_maximum_fusion), channel_id=1, source_target_pairs={{0,16},{8,24},{16,32},{24,40},{32,48},{40,56},{48,64},{56,72},{64,... | collective-permute-start | bytes 1572872 | tf_op jit(solution)/shard_map/ppermute | solution.py:307
  5.4 16.3 %collective-permute-done.two_ref = bf16[512,512]{1,0:T(8,128)(2,1)S(1)} collective-permute-done((bf16[512,512]{1,0:T(8,128)(2,1)S(1)}, bf16[512,512]{1,0:T(8,128)(2,1)S(1)}, u32[]{:S(2)}, u32[]{:S(2)}) %collective-permute-start) | collective-permute-done | bytes 524320 | tf_op jit(solution)/shard_map/ppermute | solution.py:307
  21.7 1.9 %collective-permute-start.1 = (bf16[512,512]{1,0:T(8,128)(2,1)S(1)}, bf16[512,512]{1,0:T(8,128)(2,1)S(1)}, u32[]{:S(2)}, u32[]{:S(2)}) collective-permute-start(bf16[512,512]{1,0:T(8,128)(2,1)S(1)} %collective-permute-done.two_ref), channel_id=1, source_target_pairs={{0,8},{8,16},{16,24},{24,32},{32,40},{40,48},{48,56},{56,64},{64,7... | collective-permute-start | bytes 1572872 | tf_op jit(solution)/shard_map/ppermute | solution.py:308
  23.7 1.8 %shard_map.109 = bf16[64,2,1152]{2,1,0:T(2,128)(2,1)} custom-call(bf16[256,512]{1,0:T(8,128)(2,1)S(1)} %copy-done.8, bf16[256,512]{1,0:T(8,128)(2,1)S(1)} %copy-done.9, f32[8,512]{1,0:T(8,128)S(1)} %copy-done.11), custom_call_target="tpu_custom_call" | custom-call | tf_op jit(solution)/shard_map/pallas_call | solution.py:64
  25.5 10.9 %all-to-all-start = ((bf16[64,2,1152]{2,1,0:T(2,128)(2,1)}), bf16[64,2,1152]{2,1,0:T(2,128)(2,1)S(1)}, u32[]{:S(2)}, u32[]{:S(2)}) async-start(bf16[64,2,1152]{2,1,0:T(2,128)(2,1)} %shard_map.109), calls=%async_computation | async-start | bytes 589824 | tf_op jit(solution)/shard_map/all_to_all | solution.py:295
  36.4 0.0 collective-permute-done.1.three_ref
  36.4 0.8 copy-done.6
  37.2 0.1 slice_select_fusion.1
  37.3 0.0 copy-start
  37.3 0.8 pad_maximum_fusion.1
  38.1 2.0 %collective-permute-start.2 = (bf16[512,512]{1,0:T(8,128)(2,1)}, bf16[512,512]{1,0:T(8,128)(2,1)}, u32[]{:S(2)}, u32[]{:S(2)}) collective-permute-start(bf16[512,512]{1,0:T(8,128)(2,1)} %pad_maximum_fusion.1), channel_id=1, source_target_pairs={{0,8},{8,0},{16,24},{24,16},{32,40},{40,32},{48,56},{56,48},{64,72... | collective-permute-start | bytes 1572872 | tf_op jit(solution)/shard_map/ppermute | solution.py:314
  40.1 0.1 constant_dynamic-slice_fusion
  40.2 0.1 copy.13
  40.3 1.0 %copy-done.5 = f32[8,16384]{1,0:T(8,128)S(1)} copy-done((f32[8,16384]{1,0:T(8,128)S(1)}, f32[8,16384]{1,0:T(8,128)}, u32[]{:S(2)}) %copy-start.5) | copy-done | bytes 524312
  41.3 1.0 %shard_map.110.spec_ref = f32[1024,256]{1,0:T(8,128)S(1)} custom-call(f32[8,16384]{1,0:T(8,128)S(1)} %copy-done.5, bf16[7,256,256]{2,1,0:T(8,128)(2,1)S(1)} %copy-done), custom_call_target="tpu_custom_call" | custom-call | tf_op jit(solution)/shard_map/pallas_call | solution.py:64
  42.3 6.1 %all-to-all-done.signal_ref = bf16[64,2,1152]{2,1,0:T(2,128)(2,1)S(1)} async-done(((bf16[64,2,1152]{2,1,0:T(2,128)(2,1)}), bf16[64,2,1152]{2,1,0:T(2,128)(2,1)S(1)}, u32[]{:S(2)}, u32[]{:S(2)}) %all-to-all-start) | async-done | bytes 294944 | tf_op jit(solution)/shard_map/all_to_all | solution.py:295
  48.5 2.9 %shard_map.111 = bf16[64,8,256]{2,1,0:T(8,128)(2,1)S(1)} custom-call(bf16[64,2,1152]{2,1,0:T(2,128)(2,1)S(1)} %all-to-all-done.signal_ref, f32[8,8]{1,0:T(8,128)S(1)} %bitcast.4, f32[1024,256]{1,0:T(8,128)S(1)} %shard_map.110.spec_ref, bf16[7,256,256]{2,1,0:T(8,128)(2,1)S(1)} %copy-done), custom_call_target="tpu_custom_call" | custom-call | tf_op jit(solution)/shard_map/pallas_call | solution.py:64
  51.4 0.0 copy-start.3
  51.4 0.7 copy-done.3
  52.1 6.4 %all-to-all-start.1 = ((bf16[64,8,256]{2,1,0:T(8,128)(2,1)}), bf16[64,8,256]{2,1,0:T(8,128)(2,1)S(1)}, u32[]{:S(2)}, u32[]{:S(2)}) async-start(bf16[64,8,256]{2,1,0:T(8,128)(2,1)} %copy-done.3), calls=%async_computation.1 | async-start | bytes 524288 | tf_op jit(solution)/shard_map/all_to_all | solution.py:304
  58.5 0.0 copy-start.10
  58.5 0.1 shard_map.112.query_t_ref
  58.7 0.8 copy-done.10
  59.4 3.2 %attention.1 = (f32[256,512]{1,0:T(8,128)S(1)}, f32[128,256]{1,0:T(8,128)S(1)}) custom-call(s32[1]{0:T(128)} %bitcast.1.block_ref, bf16[256,512]{1,0:T(8,128)(2,1)S(1)} %copy-done.10, bf16[256,512]{1,0:T(8,128)(2,1)S(1)} %copy-done.1, bf16[256,512]{1,0:T(8,128)(2,1)S(1)} %copy-done.2, bf16[512,512]{1,0:T(8,128)(2,1)} %collective-permute-done.2.one_ref, ...), custom_call_target="tpu_custom_call" | custom-call | tf_op jit(solution)/shard_map/attention/pallas_call | solution.py:225
  62.7 7.4 %all-to-all-done.1.returned_ref = bf16[64,8,256]{2,1,0:T(8,128)(2,1)S(1)} async-done(((bf16[64,8,256]{2,1,0:T(8,128)(2,1)}), bf16[64,8,256]{2,1,0:T(8,128)(2,1)S(1)}, u32[]{:S(2)}, u32[]{:S(2)}) %all-to-all-start.1) | async-done | bytes 262176 | tf_op jit(solution)/shard_map/all_to_all | solution.py:304
  70.0 0.7 shard_map.113
  70.8 11.5 %all-to-all-start.2 = ((f32[8,8,128]{2,1,0:T(8,128)}), f32[8,8,128]{2,1,0:T(8,128)S(1)}, u32[]{:S(2)}, u32[]{:S(2)}) async-start(f32[8,8,128]{2,1,0:T(8,128)} %shard_map.113), calls=%async_computation.2 | async-start | bytes 65536 | tf_op jit(solution)/shard_map/all_to_all | solution.py:319
  82.3 0.1 shard_map.114.mixed_ref
  82.4 0.0 copy-start.13
  82.4 10.0 %all-to-all-done.2.sums_ref = f32[8,8,128]{2,1,0:T(8,128)S(1)} async-done(((f32[8,8,128]{2,1,0:T(8,128)}), f32[8,8,128]{2,1,0:T(8,128)S(1)}, u32[]{:S(2)}, u32[]{:S(2)}) %all-to-all-start.2) | async-done | bytes 32800 | tf_op jit(solution)/shard_map/all_to_all | solution.py:319
  92.4 1.0 %shard_map.115 = bf16[256,512]{1,0:T(8,128)(2,1)} custom-call(f32[8,8,128]{2,1,0:T(8,128)S(1)} %all-to-all-done.2.sums_ref, f32[256,512]{1,0:T(8,128)S(1)} %get-tuple-element.12.att_ref, f32[256,512]{1,0:T(8,128)S(1)} %shard_map.114.mixed_ref, f32[1,512]{1,0:T(1,128)S(1)} %bitcast.6), custom_call_target="tpu_custom_call" | custom-call | tf_op jit(solution)/shard_map/pallas_call | solution.py:64
  (21 shorter events, 0.0 us)
Async XLA Ops:
  0.0 23.7 %copy-start.11 = (f32[8,512]{1,0:T(8,128)S(1)}, f32[8,512]{1,0:T(8,128)}, u32[]{:S(2)}) copy-start(f32[8,512]{1,0:T(8,128)} %taps_ref.1) | copy-start | bytes 49156
  0.0 23.7 %copy-start.8 = (bf16[256,512]{1,0:T(8,128)(2,1)S(1)}, bf16[256,512]{1,0:T(8,128)(2,1)}, u32[]{:S(2)}) copy-start(bf16[256,512]{1,0:T(8,128)(2,1)} %key_ref.2) | copy-start | bytes 786436
  0.0 23.7 %copy-start.9 = (bf16[256,512]{1,0:T(8,128)(2,1)S(1)}, bf16[256,512]{1,0:T(8,128)(2,1)}, u32[]{:S(2)}) copy-start(bf16[256,512]{1,0:T(8,128)(2,1)} %value_ref.2) | copy-start | bytes 786436
  1.1 20.6 %collective-permute-start = (bf16[512,512]{1,0:T(8,128)(2,1)S(1)}, bf16[512,512]{1,0:T(8,128)(2,1)S(1)}, u32[]{:S(2)}, u32[]{:S(2)}) collective-permute-start(bf16[512,512]{1,0:T(8,128)(2,1)S(1)} %pad_maximum_fusion), channel_id=1, source_target_pairs={{0,16},{8,24},{16,32},{24,40},{32,48},{40,56},{48,64},{56,72},{64,... | collective-permute-start | bytes 1572872 | tf_op jit(solution)/shard_map/ppermute | solution.py:307
  21.7 14.6 %collective-permute-start.1 = (bf16[512,512]{1,0:T(8,128)(2,1)S(1)}, bf16[512,512]{1,0:T(8,128)(2,1)S(1)}, u32[]{:S(2)}, u32[]{:S(2)}) collective-permute-start(bf16[512,512]{1,0:T(8,128)(2,1)S(1)} %collective-permute-done.two_ref), channel_id=1, source_target_pairs={{0,8},{8,16},{16,24},{24,32},{32,40},{40,48},{48,56},{56,64},{64,7... | collective-permute-start | bytes 1572872 | tf_op jit(solution)/shard_map/ppermute | solution.py:308
  25.4 11.8 %copy-start.1 = (bf16[256,512]{1,0:T(8,128)(2,1)S(1)}, bf16[256,512]{1,0:T(8,128)(2,1)}, u32[]{:S(2)}) copy-start(bf16[256,512]{1,0:T(8,128)(2,1)} %key_ref.3) | copy-start | bytes 786436
  25.5 11.8 %copy-start.2 = (bf16[256,512]{1,0:T(8,128)(2,1)S(1)}, bf16[256,512]{1,0:T(8,128)(2,1)}, u32[]{:S(2)}) copy-start(bf16[256,512]{1,0:T(8,128)(2,1)} %value_ref.3) | copy-start | bytes 786436
  25.5 23.0 %all-to-all-start = ((bf16[64,2,1152]{2,1,0:T(2,128)(2,1)}), bf16[64,2,1152]{2,1,0:T(2,128)(2,1)S(1)}, u32[]{:S(2)}, u32[]{:S(2)}) async-start(bf16[64,2,1152]{2,1,0:T(2,128)(2,1)} %shard_map.109), calls=%async_computation | async-start | bytes 589824 | tf_op jit(solution)/shard_map/all_to_all | solution.py:295
  36.4 0.8 copy-start.6
  37.3 3.0 %copy-start = (bf16[7,256,256]{2,1,0:T(8,128)(2,1)S(1)}, bf16[7,256,256]{2,1,0:T(8,128)(2,1)}, u32[]{:S(2)}) copy-start(bf16[7,256,256]{2,1,0:T(8,128)(2,1)} %constant.27.clone.tables_ref) | copy-start | bytes 2752516
  38.1 20.6 %collective-permute-start.2 = (bf16[512,512]{1,0:T(8,128)(2,1)}, bf16[512,512]{1,0:T(8,128)(2,1)}, u32[]{:S(2)}, u32[]{:S(2)}) collective-permute-start(bf16[512,512]{1,0:T(8,128)(2,1)} %pad_maximum_fusion.1), channel_id=1, source_target_pairs={{0,8},{8,0},{16,24},{24,16},{32,40},{40,32},{48,56},{56,48},{64,72... | collective-permute-start | bytes 1572872 | tf_op jit(solution)/shard_map/ppermute | solution.py:314
  40.3 1.0 %copy-start.5 = (f32[8,16384]{1,0:T(8,128)S(1)}, f32[8,16384]{1,0:T(8,128)}, u32[]{:S(2)}) copy-start(f32[8,16384]{1,0:T(8,128)} %kernel_ref.1) | copy-start | bytes 1572868
  51.4 0.7 copy-start.3
  52.1 6.4 %copy-start.4 = (bf16[256,512]{1,0:T(8,128)(2,1)S(1)}, bf16[256,512]{1,0:T(8,128)(2,1)}, u32[]{:S(2)}) copy-start(bf16[256,512]{1,0:T(8,128)(2,1)} %query_ref.3) | copy-start | bytes 786436
  52.1 6.5 %copy-start.7 = (bf16[512,512]{1,0:T(8,128)(2,1)S(1)}, bf16[512,512]{1,0:T(8,128)(2,1)}, u32[]{:S(2)}) copy-start(bf16[512,512]{1,0:T(8,128)(2,1)} %copy-done.6) | copy-start | bytes 1572868
  52.1 17.9 %all-to-all-start.1 = ((bf16[64,8,256]{2,1,0:T(8,128)(2,1)}), bf16[64,8,256]{2,1,0:T(8,128)(2,1)S(1)}, u32[]{:S(2)}, u32[]{:S(2)}) async-start(bf16[64,8,256]{2,1,0:T(8,128)(2,1)} %copy-done.3), calls=%async_computation.1 | async-start | bytes 524288 | tf_op jit(solution)/shard_map/all_to_all | solution.py:304
  58.5 1.0 %copy-start.10 = (bf16[256,512]{1,0:T(8,128)(2,1)S(1)}, bf16[256,512]{1,0:T(8,128)(2,1)}, u32[]{:S(2)}) copy-start(bf16[256,512]{1,0:T(8,128)(2,1)} %query_ref.2) | copy-start | bytes 786436
  70.0 12.2 %copy-start.12 = (f32[512]{0:T(512)S(1)}, f32[512]{0:T(512)}, u32[]{:S(2)}) copy-start(f32[512]{0:T(512)} %param.20) | copy-start | bytes 6148
  70.8 21.7 %all-to-all-start.2 = ((f32[8,8,128]{2,1,0:T(8,128)}), f32[8,8,128]{2,1,0:T(8,128)S(1)}, u32[]{:S(2)}, u32[]{:S(2)}) async-start(f32[8,8,128]{2,1,0:T(8,128)} %shard_map.113), calls=%async_computation.2 | async-start | bytes 65536 | tf_op jit(solution)/shard_map/all_to_all | solution.py:319
  82.4 10.0 %copy-start.13 = (f32[512]{0:T(512)S(1)}, f32[512]{0:T(512)}, u32[]{:S(2)}) copy-start(f32[512]{0:T(512)} %param.19) | copy-start | bytes 6148

commit v5 on v4

--- a/solution.py
+++ b/solution.py
@@ -123,8 +123,11 @@
     return jnp.concatenate([rows_ref[pl.ds(c, RADIX, stride=channels), :] for c in range(channels)], 1)
 
 
-def kernel_spectrum_body(half, kernel_ref, tables_ref, out_ref, rows_ref):
+def kernel_spectrum_body(half, kernel_in, tables_ref, out_ref, rows_ref, kernel_ref, sem):
     channels = kernel_ref.shape[0]
+    copy = pltpu.make_async_copy(kernel_in, kernel_ref, sem)
+    copy.start()
+    copy.wait()
     for a in range(RADIX):
         row = ((a % half) * (RADIX // half) + a // half) * channels
         rows_ref[row : row + channels, :] = kernel_ref[:, a * RADIX : (a + 1) * RADIX]
@@ -295,9 +298,14 @@
     received = lax.all_to_all(signal, "seq", 0, 0, tiled=True)
     own_taps = lax.dynamic_slice(shift_taps, (0, seq * channels), (TAPS, channels)).T
     rows = pltpu.VMEM((channels * RADIX, RADIX), F32)
-    kernel_spectrum = kernel_call(
-        functools.partial(kernel_spectrum_body, count // RADIX), sds((channels * RADIX, 2 * RADIX), F32), [rows]
-    )(conv_kernel, tables)
+    kernel_spectrum = pl.pallas_call(
+        functools.partial(kernel_spectrum_body, count // RADIX),
+        out_shape=sds((channels * RADIX, 2 * RADIX), F32),
+        in_specs=[pl.BlockSpec(memory_space=pltpu.HBM), pl.BlockSpec(memory_space=pltpu.VMEM)],
+        scratch_shapes=[rows, pltpu.VMEM(conv_kernel.shape, F32), pltpu.SemaphoreType.DMA],
+        compiler_params=pltpu.CompilerParams(vmem_limit_bytes=VMEM_LIMIT),
+        name="kernel_spectrum",
+    )(pltpu.with_memory_space_constraint(conv_kernel, pltpu.HBM), tables)
     filtered = kernel_call(
         filter_body, sds((blocks, channels, count), BF16), [rows, rows]
     )(received, own_taps, kernel_spectrum, tables)

time: 95 us -> 95 us (level)
  local copies, waits for them, and re-layouts: 3.52 us -> 2.46 us
  Pallas kernels: 10.9 us -> 11.9 us
    pallas_call x0 -> x1, Pallas kernels: none -> 2.07 us  [mixer(): pl.pallas_call(functools.partial(kernel_spectrum_body, count // RADIX), o...]
    unnamed x29 -> x27, local copies, waits for them, and re-layouts: 3.44 us -> 2.38 us
    pallas_call x7 -> x6, Pallas kernels: 7.68 us -> 6.64 us  [call(): pl.pallas_call(body, out_shape=out_shape, scratch_shapes=list(scratch), c...]
  transfers between devices with their start and end apart: 6 -> 6, of which waited for: 4 -> 4; matrix products, arithmetic and copies ran while one was open for 1% -> 1% of each run, Pallas kernels for 10% -> 11%
where the time goes in v5:
time: 95 us; the launch traced here: 93.4 us
  waiting for transfers between devices  39.8 us (42%)
  starting transfers between devices  37 us (39%)
  Pallas kernels  11.9 us (13%)
  local copies, waits for them, and re-layouts  2.46 us (3%)
  other arithmetic  2.02 us (2%)
    ppermute x1, waiting for transfers between devices, mixer(): two_back = lax.ppermute(own, 'seq', [(i, i + 2) for i in range(blocks - 2)])  16.3 us
    all_to_all x1, starting transfers between devices, mixer(): gathered = lax.all_to_all(sums, 'head', 0, 0, tiled=True)  11.5 us
    all_to_all x1, starting transfers between devices, mixer(): received = lax.all_to_all(signal, 'seq', 0, 0, tiled=True)  10.9 us
    all_to_all x1, waiting for transfers between devices, mixer(): gathered = lax.all_to_all(sums, 'head', 0, 0, tiled=True)  10 us
    all_to_all x1, waiting for transfers between devices, mixer(): returned = lax.all_to_all(filtered, 'seq', 0, 0, tiled=True)  7.36 us
    pallas_call x6, Pallas kernels, call(): pl.pallas_call(body, out_shape=out_shape, scratch_shapes=list(scratch), c...  6.64 us
    all_to_all x1, starting transfers between devices, mixer(): returned = lax.all_to_all(filtered, 'seq', 0, 0, tiled=True)  6.36 us
    all_to_all x1, waiting for transfers between devices, mixer(): received = lax.all_to_all(signal, 'seq', 0, 0, tiled=True)  6.14 us
  transfers between devices with their start and end apart: 6, of which 4 were waited for; matrix products, arithmetic and copies ran while one was open for 1% of the time, Pallas kernels for 11%

profile of v5, /device:TPU:56, one launch (start us, length us, event | category | flops | bytes accessed | tf_op | source)
XLA Modules:
  0.0 93.4 jit_solution(11386101961142833026)
XLA Ops:
  0.0 1.1 %pad_maximum_fusion = bf16[512,512]{1,0:T(8,128)(2,1)S(1)} fusion(bf16[256,512]{1,0:T(8,128)(2,1)} %value_ref.3, bf16[256,512]{1,0:T(8,128)(2,1)} %key_ref.3), kind=kLoop, calls=%fused_computation | loop fusion | flops 1048576 | bytes 1048576 | tf_op jit(solution)/shard_map/concatenate | solution.py:314
  1.1 4.3 %collective-permute-start = (bf16[512,512]{1,0:T(8,128)(2,1)S(1)}, bf16[512,512]{1,0:T(8,128)(2,1)S(1)}, u32[]{:S(2)}, u32[]{:S(2)}) collective-permute-start(bf16[512,512]{1,0:T(8,128)(2,1)S(1)} %pad_maximum_fusion), channel_id=1, source_target_pairs={{0,16},{8,24},{16,32},{24,40},{32,48},{40,56},{48,64},{56,72},{64,... | collective-permute-start | bytes 1572872 | tf_op jit(solution)/shard_map/ppermute | solution.py:315
  5.4 16.3 %collective-permute-done.two_ref = bf16[512,512]{1,0:T(8,128)(2,1)S(1)} collective-permute-done((bf16[512,512]{1,0:T(8,128)(2,1)S(1)}, bf16[512,512]{1,0:T(8,128)(2,1)S(1)}, u32[]{:S(2)}, u32[]{:S(2)}) %collective-permute-start) | collective-permute-done | bytes 524320 | tf_op jit(solution)/shard_map/ppermute | solution.py:315
  21.7 1.9 %collective-permute-start.1 = (bf16[512,512]{1,0:T(8,128)(2,1)S(1)}, bf16[512,512]{1,0:T(8,128)(2,1)S(1)}, u32[]{:S(2)}, u32[]{:S(2)}) collective-permute-start(bf16[512,512]{1,0:T(8,128)(2,1)S(1)} %collective-permute-done.two_ref), channel_id=1, source_target_pairs={{0,8},{8,16},{16,24},{24,32},{32,40},{40,48},{48,56},{56,64},{64,7... | collective-permute-start | bytes 1572872 | tf_op jit(solution)/shard_map/ppermute | solution.py:316
  23.7 1.8 %shard_map.109 = bf16[64,2,1152]{2,1,0:T(2,128)(2,1)} custom-call(bf16[256,512]{1,0:T(8,128)(2,1)S(1)} %copy-done.7, bf16[256,512]{1,0:T(8,128)(2,1)S(1)} %copy-done.8, f32[8,512]{1,0:T(8,128)S(1)} %copy-done.10), custom_call_target="tpu_custom_call" | custom-call | tf_op jit(solution)/shard_map/pallas_call | solution.py:64
  25.4 10.9 %all-to-all-start = ((bf16[64,2,1152]{2,1,0:T(2,128)(2,1)}), bf16[64,2,1152]{2,1,0:T(2,128)(2,1)S(1)}, u32[]{:S(2)}, u32[]{:S(2)}) async-start(bf16[64,2,1152]{2,1,0:T(2,128)(2,1)} %shard_map.109), calls=%async_computation | async-start | bytes 589824 | tf_op jit(solution)/shard_map/all_to_all | solution.py:298
  36.4 0.0 collective-permute-done.1.three_ref
  36.4 0.8 copy-done.5
  37.2 0.1 slice_select_fusion.1
  37.2 0.0 copy-start
  37.2 0.8 pad_maximum_fusion.1
  38.1 2.0 %collective-permute-start.2 = (bf16[512,512]{1,0:T(8,128)(2,1)}, bf16[512,512]{1,0:T(8,128)(2,1)}, u32[]{:S(2)}, u32[]{:S(2)}) collective-permute-start(bf16[512,512]{1,0:T(8,128)(2,1)} %pad_maximum_fusion.1), channel_id=1, source_target_pairs={{0,8},{8,0},{16,24},{24,16},{32,40},{40,32},{48,56},{56,48},{64,72... | collective-permute-start | bytes 1572872 | tf_op jit(solution)/shard_map/ppermute | solution.py:322
  40.1 0.1 constant_dynamic-slice_fusion
  40.2 0.1 copy.13
  40.3 2.1 %kernel_spectrum.1.spec_ref = f32[1024,256]{1,0:T(8,128)S(1)} custom-call(f32[8,16384]{1,0:T(8,128)} %kernel_in.1, bf16[7,256,256]{2,1,0:T(8,128)(2,1)S(1)} %copy-done), custom_call_target="tpu_custom_call" | custom-call | tf_op jit(solution)/shard_map/kernel_spectrum/pallas_call | solution.py:301
  42.3 6.1 %all-to-all-done.signal_ref = bf16[64,2,1152]{2,1,0:T(2,128)(2,1)S(1)} async-done(((bf16[64,2,1152]{2,1,0:T(2,128)(2,1)}), bf16[64,2,1152]{2,1,0:T(2,128)(2,1)S(1)}, u32[]{:S(2)}, u32[]{:S(2)}) %all-to-all-start) | async-done | bytes 294944 | tf_op jit(solution)/shard_map/all_to_all | solution.py:298
  48.5 2.9 %shard_map.110 = bf16[64,8,256]{2,1,0:T(8,128)(2,1)S(1)} custom-call(bf16[64,2,1152]{2,1,0:T(2,128)(2,1)S(1)} %all-to-all-done.signal_ref, f32[8,8]{1,0:T(8,128)S(1)} %bitcast.4, f32[1024,256]{1,0:T(8,128)S(1)} %kernel_spectrum.1.spec_ref, bf16[7,256,256]{2,1,0:T(8,128)(2,1)S(1)} %copy-done), custom_call_target="tpu_custom_call" | custom-call | tf_op jit(solution)/shard_map/pallas_call | solution.py:64
  51.4 0.0 copy-start.3
  51.4 0.7 copy-done.3
  52.1 6.4 %all-to-all-start.1 = ((bf16[64,8,256]{2,1,0:T(8,128)(2,1)}), bf16[64,8,256]{2,1,0:T(8,128)(2,1)S(1)}, u32[]{:S(2)}, u32[]{:S(2)}) async-start(bf16[64,8,256]{2,1,0:T(8,128)(2,1)} %copy-done.3), calls=%async_computation.1 | async-start | bytes 524288 | tf_op jit(solution)/shard_map/all_to_all | solution.py:312
  58.5 0.0 copy-start.9
  58.5 0.1 shard_map.111.query_t_ref
  58.6 0.0 collective-permute-done.2.one_ref
  58.7 0.8 copy-done.9
  59.4 3.2 %attention.1 = (f32[256,512]{1,0:T(8,128)S(1)}, f32[128,256]{1,0:T(8,128)S(1)}) custom-call(s32[1]{0:T(128)} %bitcast.1.block_ref, bf16[256,512]{1,0:T(8,128)(2,1)S(1)} %copy-done.9, bf16[256,512]{1,0:T(8,128)(2,1)S(1)} %copy-done.1, bf16[256,512]{1,0:T(8,128)(2,1)S(1)} %copy-done.2, bf16[512,512]{1,0:T(8,128)(2,1)} %collective-permute-done.2.one_ref, ...), custom_call_target="tpu_custom_call" | custom-call | tf_op jit(solution)/shard_map/attention/pallas_call | solution.py:228
  62.7 7.4 %all-to-all-done.1.returned_ref = bf16[64,8,256]{2,1,0:T(8,128)(2,1)S(1)} async-done(((bf16[64,8,256]{2,1,0:T(8,128)(2,1)}), bf16[64,8,256]{2,1,0:T(8,128)(2,1)S(1)}, u32[]{:S(2)}, u32[]{:S(2)}) %all-to-all-start.1) | async-done | bytes 262176 | tf_op jit(solution)/shard_map/all_to_all | solution.py:312
  70.0 0.7 shard_map.112
  70.7 11.5 %all-to-all-start.2 = ((f32[8,8,128]{2,1,0:T(8,128)}), f32[8,8,128]{2,1,0:T(8,128)S(1)}, u32[]{:S(2)}, u32[]{:S(2)}) async-start(f32[8,8,128]{2,1,0:T(8,128)} %shard_map.112), calls=%async_computation.2 | async-start | bytes 65536 | tf_op jit(solution)/shard_map/all_to_all | solution.py:327
  82.2 0.1 shard_map.113.mixed_ref
  82.4 0.0 copy-start.12
  82.4 10.0 %all-to-all-done.2.sums_ref = f32[8,8,128]{2,1,0:T(8,128)S(1)} async-done(((f32[8,8,128]{2,1,0:T(8,128)}), f32[8,8,128]{2,1,0:T(8,128)S(1)}, u32[]{:S(2)}, u32[]{:S(2)}) %all-to-all-start.2) | async-done | bytes 32800 | tf_op jit(solution)/shard_map/all_to_all | solution.py:327
  92.4 1.0 %shard_map.114 = bf16[256,512]{1,0:T(8,128)(2,1)} custom-call(f32[8,8,128]{2,1,0:T(8,128)S(1)} %all-to-all-done.2.sums_ref, f32[256,512]{1,0:T(8,128)S(1)} %get-tuple-element.12.att_ref, f32[256,512]{1,0:T(8,128)S(1)} %shard_map.113.mixed_ref, f32[1,512]{1,0:T(1,128)S(1)} %bitcast.6), custom_call_target="tpu_custom_call" | custom-call | tf_op jit(solution)/shard_map/pallas_call | solution.py:64
  (19 shorter events, 0.0 us)
Async XLA Ops:
  0.0 23.7 %copy-start.10 = (f32[8,512]{1,0:T(8,128)S(1)}, f32[8,512]{1,0:T(8,128)}, u32[]{:S(2)}) copy-start(f32[8,512]{1,0:T(8,128)} %taps_ref.1) | copy-start | bytes 49156
  0.0 23.7 %copy-start.7 = (bf16[256,512]{1,0:T(8,128)(2,1)S(1)}, bf16[256,512]{1,0:T(8,128)(2,1)}, u32[]{:S(2)}) copy-start(bf16[256,512]{1,0:T(8,128)(2,1)} %key_ref.2) | copy-start | bytes 786436
  0.0 23.7 %copy-start.8 = (bf16[256,512]{1,0:T(8,128)(2,1)S(1)}, bf16[256,512]{1,0:T(8,128)(2,1)}, u32[]{:S(2)}) copy-start(bf16[256,512]{1,0:T(8,128)(2,1)} %value_ref.2) | copy-start | bytes 786436
  1.1 20.6 %collective-permute-start = (bf16[512,512]{1,0:T(8,128)(2,1)S(1)}, bf16[512,512]{1,0:T(8,128)(2,1)S(1)}, u32[]{:S(2)}, u32[]{:S(2)}) collective-permute-start(bf16[512,512]{1,0:T(8,128)(2,1)S(1)} %pad_maximum_fusion), channel_id=1, source_target_pairs={{0,16},{8,24},{16,32},{24,40},{32,48},{40,56},{48,64},{56,72},{64,... | collective-permute-start | bytes 1572872 | tf_op jit(solution)/shard_map/ppermute | solution.py:315
  21.7 14.6 %collective-permute-start.1 = (bf16[512,512]{1,0:T(8,128)(2,1)S(1)}, bf16[512,512]{1,0:T(8,128)(2,1)S(1)}, u32[]{:S(2)}, u32[]{:S(2)}) collective-permute-start(bf16[512,512]{1,0:T(8,128)(2,1)S(1)} %collective-permute-done.two_ref), channel_id=1, source_target_pairs={{0,8},{8,16},{16,24},{24,32},{32,40},{40,48},{48,56},{56,64},{64,7... | collective-permute-start | bytes 1572872 | tf_op jit(solution)/shard_map/ppermute | solution.py:316
  25.4 11.7 %copy-start.1 = (bf16[256,512]{1,0:T(8,128)(2,1)S(1)}, bf16[256,512]{1,0:T(8,128)(2,1)}, u32[]{:S(2)}) copy-start(bf16[256,512]{1,0:T(8,128)(2,1)} %key_ref.3) | copy-start | bytes 786436
  25.4 11.7 %copy-start.2 = (bf16[256,512]{1,0:T(8,128)(2,1)S(1)}, bf16[256,512]{1,0:T(8,128)(2,1)}, u32[]{:S(2)}) copy-start(bf16[256,512]{1,0:T(8,128)(2,1)} %value_ref.3) | copy-start | bytes 786436
  25.4 23.0 %all-to-all-start = ((bf16[64,2,1152]{2,1,0:T(2,128)(2,1)}), bf16[64,2,1152]{2,1,0:T(2,128)(2,1)S(1)}, u32[]{:S(2)}, u32[]{:S(2)}) async-start(bf16[64,2,1152]{2,1,0:T(2,128)(2,1)} %shard_map.109), calls=%async_computation | async-start | bytes 589824 | tf_op jit(solution)/shard_map/all_to_all | solution.py:298
  36.4 0.8 copy-start.5
  37.2 3.0 %copy-start = (bf16[7,256,256]{2,1,0:T(8,128)(2,1)S(1)}, bf16[7,256,256]{2,1,0:T(8,128)(2,1)}, u32[]{:S(2)}) copy-start(bf16[7,256,256]{2,1,0:T(8,128)(2,1)} %constant.27.clone.tables_ref) | copy-start | bytes 2752516
  38.1 20.6 %collective-permute-start.2 = (bf16[512,512]{1,0:T(8,128)(2,1)}, bf16[512,512]{1,0:T(8,128)(2,1)}, u32[]{:S(2)}, u32[]{:S(2)}) collective-permute-start(bf16[512,512]{1,0:T(8,128)(2,1)} %pad_maximum_fusion.1), channel_id=1, source_target_pairs={{0,8},{8,0},{16,24},{24,16},{32,40},{40,32},{48,56},{56,48},{64,72... | collective-permute-start | bytes 1572872 | tf_op jit(solution)/shard_map/ppermute | solution.py:322
  51.4 0.7 copy-start.3
  52.1 6.4 %copy-start.4 = (bf16[256,512]{1,0:T(8,128)(2,1)S(1)}, bf16[256,512]{1,0:T(8,128)(2,1)}, u32[]{:S(2)}) copy-start(bf16[256,512]{1,0:T(8,128)(2,1)} %query_ref.3) | copy-start | bytes 786436
  52.1 6.5 %copy-start.6 = (bf16[512,512]{1,0:T(8,128)(2,1)S(1)}, bf16[512,512]{1,0:T(8,128)(2,1)}, u32[]{:S(2)}) copy-start(bf16[512,512]{1,0:T(8,128)(2,1)} %copy-done.5) | copy-start | bytes 1572868
  52.1 17.9 %all-to-all-start.1 = ((bf16[64,8,256]{2,1,0:T(8,128)(2,1)}), bf16[64,8,256]{2,1,0:T(8,128)(2,1)S(1)}, u32[]{:S(2)}, u32[]{:S(2)}) async-start(bf16[64,8,256]{2,1,0:T(8,128)(2,1)} %copy-done.3), calls=%async_computation.1 | async-start | bytes 524288 | tf_op jit(solution)/shard_map/all_to_all | solution.py:312
  58.5 1.0 %copy-start.9 = (bf16[256,512]{1,0:T(8,128)(2,1)S(1)}, bf16[256,512]{1,0:T(8,128)(2,1)}, u32[]{:S(2)}) copy-start(bf16[256,512]{1,0:T(8,128)(2,1)} %query_ref.2) | copy-start | bytes 786436
  70.0 12.2 %copy-start.11 = (f32[512]{0:T(512)S(1)}, f32[512]{0:T(512)}, u32[]{:S(2)}) copy-start(f32[512]{0:T(512)} %param.20) | copy-start | bytes 6148
  70.7 21.7 %all-to-all-start.2 = ((f32[8,8,128]{2,1,0:T(8,128)}), f32[8,8,128]{2,1,0:T(8,128)S(1)}, u32[]{:S(2)}, u32[]{:S(2)}) async-start(f32[8,8,128]{2,1,0:T(8,128)} %shard_map.112), calls=%async_computation.2 | async-start | bytes 65536 | tf_op jit(solution)/shard_map/all_to_all | solution.py:327
  82.4 10.0 %copy-start.12 = (f32[512]{0:T(512)S(1)}, f32[512]{0:T(512)}, u32[]{:S(2)}) copy-start(f32[512]{0:T(512)} %param.19) | copy-start | bytes 6148

commit v6 on v5

--- a/solution.py
+++ b/solution.py
@@ -96,6 +96,31 @@
         out_ref[:, :, i * count : (i + 1) * count] = product[:, i].astype(BF16)
     joined = jnp.concatenate([edges[:, i, :, : RADIX // SIDE] for i in range(SIDE)], 2)
     out_ref[:, :, SIDE * count :] = joined.astype(BF16)
+
+
+def pack_body(key_in, value_in, out_ref, sems):
+    count = key_in.shape[0]
+    copies = [
+        pltpu.make_async_copy(source, out_ref.at[pl.ds(i * count, count)], sems.at[i])
+        for i, source in enumerate((key_in, value_in))
+    ]
+    for copy in copies:
+        copy.start()
+    for copy in copies:
+        copy.wait()
+
+
+def pack(key, value):
+    count, width = key.shape
+    return pl.pallas_call(
+        pack_body,
+        out_shape=jax.ShapeDtypeStruct((2 * count, width), key.dtype),
+        in_specs=[pl.BlockSpec(memory_space=pltpu.HBM)] * 2,
+        out_specs=pl.BlockSpec(memory_space=pltpu.VMEM),
+        scratch_shapes=[pltpu.SemaphoreType.DMA((2,))],
+        compiler_params=pltpu.CompilerParams(vmem_limit_bytes=VMEM_LIMIT),
+        name="pack",
+    )(*(pltpu.with_memory_space_constraint(x, pltpu.HBM) for x in (key, value)))
 
 
 def product3(value, table_hi, table_lo):
@@ -311,7 +336,7 @@
     )(received, own_taps, kernel_spectrum, tables)
     returned = lax.all_to_all(filtered, "seq", 0, 0, tiled=True)
 
-    own = jnp.concatenate([heads_key, heads_value], 0)
+    own = pack(heads_key, heads_value)
     two_back = lax.ppermute(own, "seq", [(i, i + 2) for i in range(blocks - 2)])
     three_back = lax.ppermute(two_back, "seq", onward)
     two_back, three_back = lax.optimization_barrier((two_back, three_back))

time: 95 us -> 94.9 us (level)
  other arithmetic: 2.02 us -> 0.89 us
  Pallas kernels: 11.9 us -> 13 us
    concatenate x1 -> x0, other arithmetic: 1.13 us -> none  [mixer(): own = jnp.concatenate([heads_key, heads_value], 0)]
    pallas_call x0 -> x1, Pallas kernels: none -> 1.11 us  [pack(): pl.pallas_call(pack_body, out_shape=jax.ShapeDtypeStruct((2 * count, widt...]
where the time goes in v6:
time: 94.9 us; the launch traced here: 93.4 us
  waiting for transfers between devices  39.8 us (42%)
  starting transfers between devices  37 us (39%)
  Pallas kernels  13 us (14%)
  local copies, waits for them, and re-layouts  2.46 us (3%)
    ppermute x1, waiting for transfers between devices, mixer(): two_back = lax.ppermute(own, 'seq', [(i, i + 2) for i in range(blocks - 2)])  16.3 us
    all_to_all x1, starting transfers between devices, mixer(): gathered = lax.all_to_all(sums, 'head', 0, 0, tiled=True)  11.5 us
    all_to_all x1, starting transfers between devices, mixer(): received = lax.all_to_all(signal, 'seq', 0, 0, tiled=True)  10.9 us
    all_to_all x1, waiting for transfers between devices, mixer(): gathered = lax.all_to_all(sums, 'head', 0, 0, tiled=True)  10 us
    all_to_all x1, waiting for transfers between devices, mixer(): returned = lax.all_to_all(filtered, 'seq', 0, 0, tiled=True)  7.36 us
    pallas_call x6, Pallas kernels, call(): pl.pallas_call(body, out_shape=out_shape, scratch_shapes=list(scratch), c...  6.65 us
    all_to_all x1, starting transfers between devices, mixer(): returned = lax.all_to_all(filtered, 'seq', 0, 0, tiled=True)  6.35 us
    all_to_all x1, waiting for transfers between devices, mixer(): received = lax.all_to_all(signal, 'seq', 0, 0, tiled=True)  6.15 us
  transfers between devices with their start and end apart: 6, of which 4 were waited for; matrix products, arithmetic and copies ran while one was open for 1% of the time, Pallas kernels for 11%

profile of v6, /device:TPU:56, one launch (start us, length us, event | category | flops | bytes accessed | tf_op | source)
XLA Modules:
  0.0 93.4 jit_solution(11782089376570830830)
XLA Ops:
  0.0 1.1 %pack.1 = bf16[512,512]{1,0:T(8,128)(2,1)S(1)} custom-call(bf16[256,512]{1,0:T(8,128)(2,1)} %key_ref.3, bf16[256,512]{1,0:T(8,128)(2,1)} %value_ref.3), custom_call_target="tpu_custom_call" | custom-call | tf_op jit(solution)/shard_map/pack/pallas_call | solution.py:115
  1.1 4.3 %collective-permute-start = (bf16[512,512]{1,0:T(8,128)(2,1)S(1)}, bf16[512,512]{1,0:T(8,128)(2,1)S(1)}, u32[]{:S(2)}, u32[]{:S(2)}) collective-permute-start(bf16[512,512]{1,0:T(8,128)(2,1)S(1)} %pack.1), channel_id=1, source_target_pairs={{0,16},{8,24},{16,32},{24,40},{32,48},{40,56},{48,64},{56,72},{64,... | collective-permute-start | bytes 1572872 | tf_op jit(solution)/shard_map/ppermute | solution.py:340
  5.4 16.3 %collective-permute-done.two_ref = bf16[512,512]{1,0:T(8,128)(2,1)S(1)} collective-permute-done((bf16[512,512]{1,0:T(8,128)(2,1)S(1)}, bf16[512,512]{1,0:T(8,128)(2,1)S(1)}, u32[]{:S(2)}, u32[]{:S(2)}) %collective-permute-start) | collective-permute-done | bytes 524320 | tf_op jit(solution)/shard_map/ppermute | solution.py:340
  21.7 1.9 %collective-permute-start.1 = (bf16[512,512]{1,0:T(8,128)(2,1)S(1)}, bf16[512,512]{1,0:T(8,128)(2,1)S(1)}, u32[]{:S(2)}, u32[]{:S(2)}) collective-permute-start(bf16[512,512]{1,0:T(8,128)(2,1)S(1)} %collective-permute-done.two_ref), channel_id=1, source_target_pairs={{0,8},{8,16},{16,24},{24,32},{32,40},{40,48},{48,56},{56,64},{64,7... | collective-permute-start | bytes 1572872 | tf_op jit(solution)/shard_map/ppermute | solution.py:341
  23.7 1.8 %shard_map.109 = bf16[64,2,1152]{2,1,0:T(2,128)(2,1)} custom-call(bf16[256,512]{1,0:T(8,128)(2,1)S(1)} %copy-done.7, bf16[256,512]{1,0:T(8,128)(2,1)S(1)} %copy-done.8, f32[8,512]{1,0:T(8,128)S(1)} %copy-done.10), custom_call_target="tpu_custom_call" | custom-call | tf_op jit(solution)/shard_map/pallas_call | solution.py:64
  25.4 10.9 %all-to-all-start = ((bf16[64,2,1152]{2,1,0:T(2,128)(2,1)}), bf16[64,2,1152]{2,1,0:T(2,128)(2,1)S(1)}, u32[]{:S(2)}, u32[]{:S(2)}) async-start(bf16[64,2,1152]{2,1,0:T(2,128)(2,1)} %shard_map.109), calls=%async_computation | async-start | bytes 589824 | tf_op jit(solution)/shard_map/all_to_all | solution.py:323
  36.3 0.0 collective-permute-done.1.three_ref
  36.4 0.8 copy-done.5
  37.2 0.1 slice_select_fusion.1
  37.2 0.0 copy-start
  37.2 0.8 pad_maximum_fusion
  38.1 2.0 %collective-permute-start.2 = (bf16[512,512]{1,0:T(8,128)(2,1)}, bf16[512,512]{1,0:T(8,128)(2,1)}, u32[]{:S(2)}, u32[]{:S(2)}) collective-permute-start(bf16[512,512]{1,0:T(8,128)(2,1)} %pad_maximum_fusion), channel_id=1, source_target_pairs={{0,8},{8,0},{16,24},{24,16},{32,40},{40,32},{48,56},{56,48},{64,72... | collective-permute-start | bytes 1572872 | tf_op jit(solution)/shard_map/ppermute | solution.py:347
  40.1 0.1 constant_dynamic-slice_fusion
  40.2 0.1 copy.13
  40.2 2.1 %kernel_spectrum.1.spec_ref = f32[1024,256]{1,0:T(8,128)S(1)} custom-call(f32[8,16384]{1,0:T(8,128)} %kernel_in.1, bf16[7,256,256]{2,1,0:T(8,128)(2,1)S(1)} %copy-done), custom_call_target="tpu_custom_call" | custom-call | tf_op jit(solution)/shard_map/kernel_spectrum/pallas_call | solution.py:326
  42.3 6.1 %all-to-all-done.signal_ref = bf16[64,2,1152]{2,1,0:T(2,128)(2,1)S(1)} async-done(((bf16[64,2,1152]{2,1,0:T(2,128)(2,1)}), bf16[64,2,1152]{2,1,0:T(2,128)(2,1)S(1)}, u32[]{:S(2)}, u32[]{:S(2)}) %all-to-all-start) | async-done | bytes 294944 | tf_op jit(solution)/shard_map/all_to_all | solution.py:323
  48.5 2.9 %shard_map.110 = bf16[64,8,256]{2,1,0:T(8,128)(2,1)S(1)} custom-call(bf16[64,2,1152]{2,1,0:T(2,128)(2,1)S(1)} %all-to-all-done.signal_ref, f32[8,8]{1,0:T(8,128)S(1)} %bitcast.4, f32[1024,256]{1,0:T(8,128)S(1)} %kernel_spectrum.1.spec_ref, bf16[7,256,256]{2,1,0:T(8,128)(2,1)S(1)} %copy-done), custom_call_target="tpu_custom_call" | custom-call | tf_op jit(solution)/shard_map/pallas_call | solution.py:64
  51.4 0.0 copy-start.3
  51.4 0.7 copy-done.3
  52.1 6.3 %all-to-all-start.1 = ((bf16[64,8,256]{2,1,0:T(8,128)(2,1)}), bf16[64,8,256]{2,1,0:T(8,128)(2,1)S(1)}, u32[]{:S(2)}, u32[]{:S(2)}) async-start(bf16[64,8,256]{2,1,0:T(8,128)(2,1)} %copy-done.3), calls=%async_computation.1 | async-start | bytes 524288 | tf_op jit(solution)/shard_map/all_to_all | solution.py:337
  58.5 0.0 copy-start.9
  58.5 0.1 shard_map.111.query_t_ref
  58.6 0.0 collective-permute-done.2.one_ref
  58.6 0.8 copy-done.9
  59.4 3.2 %attention.1 = (f32[256,512]{1,0:T(8,128)S(1)}, f32[128,256]{1,0:T(8,128)S(1)}) custom-call(s32[1]{0:T(128)} %bitcast.1.block_ref, bf16[256,512]{1,0:T(8,128)(2,1)S(1)} %copy-done.9, bf16[256,512]{1,0:T(8,128)(2,1)S(1)} %copy-done.1, bf16[256,512]{1,0:T(8,128)(2,1)S(1)} %copy-done.2, bf16[512,512]{1,0:T(8,128)(2,1)} %collective-permute-done.2.one_ref, ...), custom_call_target="tpu_custom_call" | custom-call | tf_op jit(solution)/shard_map/attention/pallas_call | solution.py:253
  62.6 7.4 %all-to-all-done.1.returned_ref = bf16[64,8,256]{2,1,0:T(8,128)(2,1)S(1)} async-done(((bf16[64,8,256]{2,1,0:T(8,128)(2,1)}), bf16[64,8,256]{2,1,0:T(8,128)(2,1)S(1)}, u32[]{:S(2)}, u32[]{:S(2)}) %all-to-all-start.1) | async-done | bytes 262176 | tf_op jit(solution)/shard_map/all_to_all | solution.py:337
  70.0 0.7 shard_map.112
  70.7 11.5 %all-to-all-start.2 = ((f32[8,8,128]{2,1,0:T(8,128)}), f32[8,8,128]{2,1,0:T(8,128)S(1)}, u32[]{:S(2)}, u32[]{:S(2)}) async-start(f32[8,8,128]{2,1,0:T(8,128)} %shard_map.112), calls=%async_computation.2 | async-start | bytes 65536 | tf_op jit(solution)/shard_map/all_to_all | solution.py:352
  82.2 0.1 shard_map.113.mixed_ref
  82.4 0.0 copy-start.12
  82.4 10.0 %all-to-all-done.2.sums_ref = f32[8,8,128]{2,1,0:T(8,128)S(1)} async-done(((f32[8,8,128]{2,1,0:T(8,128)}), f32[8,8,128]{2,1,0:T(8,128)S(1)}, u32[]{:S(2)}, u32[]{:S(2)}) %all-to-all-start.2) | async-done | bytes 32800 | tf_op jit(solution)/shard_map/all_to_all | solution.py:352
  92.4 1.0 %shard_map.114 = bf16[256,512]{1,0:T(8,128)(2,1)} custom-call(f32[8,8,128]{2,1,0:T(8,128)S(1)} %all-to-all-done.2.sums_ref, f32[256,512]{1,0:T(8,128)S(1)} %get-tuple-element.12.att_ref, f32[256,512]{1,0:T(8,128)S(1)} %shard_map.113.mixed_ref, f32[1,512]{1,0:T(1,128)S(1)} %bitcast.6), custom_call_target="tpu_custom_call" | custom-call | tf_op jit(solution)/shard_map/pallas_call | solution.py:64
  (19 shorter events, 0.0 us)
Async XLA Ops:
  0.0 23.6 %copy-start.10 = (f32[8,512]{1,0:T(8,128)S(1)}, f32[8,512]{1,0:T(8,128)}, u32[]{:S(2)}) copy-start(f32[8,512]{1,0:T(8,128)} %taps_ref.1) | copy-start | bytes 49156
  0.0 23.6 %copy-start.7 = (bf16[256,512]{1,0:T(8,128)(2,1)S(1)}, bf16[256,512]{1,0:T(8,128)(2,1)}, u32[]{:S(2)}) copy-start(bf16[256,512]{1,0:T(8,128)(2,1)} %key_ref.2) | copy-start | bytes 786436
  0.0 23.7 %copy-start.8 = (bf16[256,512]{1,0:T(8,128)(2,1)S(1)}, bf16[256,512]{1,0:T(8,128)(2,1)}, u32[]{:S(2)}) copy-start(bf16[256,512]{1,0:T(8,128)(2,1)} %value_ref.2) | copy-start | bytes 786436
  1.1 20.6 %collective-permute-start = (bf16[512,512]{1,0:T(8,128)(2,1)S(1)}, bf16[512,512]{1,0:T(8,128)(2,1)S(1)}, u32[]{:S(2)}, u32[]{:S(2)}) collective-permute-start(bf16[512,512]{1,0:T(8,128)(2,1)S(1)} %pack.1), channel_id=1, source_target_pairs={{0,16},{8,24},{16,32},{24,40},{32,48},{40,56},{48,64},{56,72},{64,... | collective-permute-start | bytes 1572872 | tf_op jit(solution)/shard_map/ppermute | solution.py:340
  21.7 14.6 %collective-permute-start.1 = (bf16[512,512]{1,0:T(8,128)(2,1)S(1)}, bf16[512,512]{1,0:T(8,128)(2,1)S(1)}, u32[]{:S(2)}, u32[]{:S(2)}) collective-permute-start(bf16[512,512]{1,0:T(8,128)(2,1)S(1)} %collective-permute-done.two_ref), channel_id=1, source_target_pairs={{0,8},{8,16},{16,24},{24,32},{32,40},{40,48},{48,56},{56,64},{64,7... | collective-permute-start | bytes 1572872 | tf_op jit(solution)/shard_map/ppermute | solution.py:341
  25.4 11.7 %copy-start.1 = (bf16[256,512]{1,0:T(8,128)(2,1)S(1)}, bf16[256,512]{1,0:T(8,128)(2,1)}, u32[]{:S(2)}) copy-start(bf16[256,512]{1,0:T(8,128)(2,1)} %key_ref.3) | copy-start | bytes 786436
  25.4 11.7 %copy-start.2 = (bf16[256,512]{1,0:T(8,128)(2,1)S(1)}, bf16[256,512]{1,0:T(8,128)(2,1)}, u32[]{:S(2)}) copy-start(bf16[256,512]{1,0:T(8,128)(2,1)} %value_ref.3) | copy-start | bytes 786436
  25.4 23.0 %all-to-all-start = ((bf16[64,2,1152]{2,1,0:T(2,128)(2,1)}), bf16[64,2,1152]{2,1,0:T(2,128)(2,1)S(1)}, u32[]{:S(2)}, u32[]{:S(2)}) async-start(bf16[64,2,1152]{2,1,0:T(2,128)(2,1)} %shard_map.109), calls=%async_computation | async-start | bytes 589824 | tf_op jit(solution)/shard_map/all_to_all | solution.py:323
  36.4 0.8 copy-start.5
  37.2 3.0 %copy-start = (bf16[7,256,256]{2,1,0:T(8,128)(2,1)S(1)}, bf16[7,256,256]{2,1,0:T(8,128)(2,1)}, u32[]{:S(2)}) copy-start(bf16[7,256,256]{2,1,0:T(8,128)(2,1)} %constant.27.clone.tables_ref) | copy-start | bytes 2752516
  38.1 20.6 %collective-permute-start.2 = (bf16[512,512]{1,0:T(8,128)(2,1)}, bf16[512,512]{1,0:T(8,128)(2,1)}, u32[]{:S(2)}, u32[]{:S(2)}) collective-permute-start(bf16[512,512]{1,0:T(8,128)(2,1)} %pad_maximum_fusion), channel_id=1, source_target_pairs={{0,8},{8,0},{16,24},{24,16},{32,40},{40,32},{48,56},{56,48},{64,72... | collective-permute-start | bytes 1572872 | tf_op jit(solution)/shard_map/ppermute | solution.py:347
  51.4 0.7 copy-start.3
  52.1 6.4 %copy-start.4 = (bf16[256,512]{1,0:T(8,128)(2,1)S(1)}, bf16[256,512]{1,0:T(8,128)(2,1)}, u32[]{:S(2)}) copy-start(bf16[256,512]{1,0:T(8,128)(2,1)} %query_ref.3) | copy-start | bytes 786436
  52.1 6.5 %copy-start.6 = (bf16[512,512]{1,0:T(8,128)(2,1)S(1)}, bf16[512,512]{1,0:T(8,128)(2,1)}, u32[]{:S(2)}) copy-start(bf16[512,512]{1,0:T(8,128)(2,1)} %copy-done.5) | copy-start | bytes 1572868
  52.1 17.9 %all-to-all-start.1 = ((bf16[64,8,256]{2,1,0:T(8,128)(2,1)}), bf16[64,8,256]{2,1,0:T(8,128)(2,1)S(1)}, u32[]{:S(2)}, u32[]{:S(2)}) async-start(bf16[64,8,256]{2,1,0:T(8,128)(2,1)} %copy-done.3), calls=%async_computation.1 | async-start | bytes 524288 | tf_op jit(solution)/shard_map/all_to_all | solution.py:337
  58.5 1.0 %copy-start.9 = (bf16[256,512]{1,0:T(8,128)(2,1)S(1)}, bf16[256,512]{1,0:T(8,128)(2,1)}, u32[]{:S(2)}) copy-start(bf16[256,512]{1,0:T(8,128)(2,1)} %query_ref.2) | copy-start | bytes 786436
  70.0 12.2 %copy-start.11 = (f32[512]{0:T(512)S(1)}, f32[512]{0:T(512)}, u32[]{:S(2)}) copy-start(f32[512]{0:T(512)} %param.20) | copy-start | bytes 6148
  70.7 21.7 %all-to-all-start.2 = ((f32[8,8,128]{2,1,0:T(8,128)}), f32[8,8,128]{2,1,0:T(8,128)S(1)}, u32[]{:S(2)}, u32[]{:S(2)}) async-start(f32[8,8,128]{2,1,0:T(8,128)} %shard_map.112), calls=%async_computation.2 | async-start | bytes 65536 | tf_op jit(solution)/shard_map/all_to_all | solution.py:352
  82.4 10.0 %copy-start.12 = (f32[512]{0:T(512)S(1)}, f32[512]{0:T(512)}, u32[]{:S(2)}) copy-start(f32[512]{0:T(512)} %param.19) | copy-start | bytes 6148

commit v7 on v6

--- a/solution.py
+++ b/solution.py
@@ -265,7 +265,7 @@
     mixer = jnp.sum(mixed * mixed, axis=0, keepdims=True)
     attention = jnp.sum(att_ref[...], axis=0, keepdims=True)
     rows = jnp.concatenate(
-        [attention[:, :RADIX], attention[:, RADIX:], mixer[:, :RADIX], mixer[:, RADIX:], jnp.zeros((4, RADIX), F32)], 0
+        [attention[:, :RADIX], attention[:, RADIX:], mixer[:, :RADIX], mixer[:, RADIX:]], 0
     )
     out_ref[...] = jnp.broadcast_to(rows[None], out_ref.shape)
 
@@ -282,7 +282,7 @@
     for peer in range(1, sums_ref.shape[0]):
         total = total + sums_ref[peer]
     scale = lax.rsqrt(total * (1.0 / D) + 1e-05) * 0.5
-    columns = jnp.concatenate([scale, jnp.zeros((RADIX - 8, RADIX), F32)], 0).T
+    columns = jnp.concatenate([scale, jnp.zeros((RADIX - 4, RADIX), F32)], 0).T
     for h in range(count // RADIX):
         rows = slice(h * RADIX, (h + 1) * RADIX)
         attention_scale = columns[:, h : h + 1]
@@ -348,7 +348,7 @@
     block = seq.astype(jnp.int32).reshape(1)
     attention_branch, attention_squares = attend(block, heads_query, heads_key, heads_value, one_back, two_back, three_back)
     query_t = kernel_call(transpose_body, sds((width, count), BF16))(mixer_query)
-    sums = kernel_call(sums_body, sds((peers, 8, RADIX), F32))(returned, query_t, attention_squares)
+    sums = kernel_call(sums_body, sds((peers, 4, RADIX), F32))(returned, query_t, attention_squares)
     gathered = lax.all_to_all(sums, "head", 0, 0, tiled=True)
     mixed = kernel_call(mixed_body, sds((count, width), F32))(
         returned, mixer_query, beta_mixer[None, :]

time: 94.9 us -> 94.9 us (level)
  no operation moved by 1% of the time
where the time goes in v7:
time: 94.9 us; the launch traced here: 93.3 us
  waiting for transfers between devices  39.8 us (42%)
  starting transfers between devices  37 us (39%)
  Pallas kernels  13 us (14%)
  local copies, waits for them, and re-layouts  2.46 us (3%)
    ppermute x1, waiting for transfers between devices, mixer(): two_back = lax.ppermute(own, 'seq', [(i, i + 2) for i in range(blocks - 2)])  16.3 us
    all_to_all x1, starting transfers between devices, mixer(): gathered = lax.all_to_all(sums, 'head', 0, 0, tiled=True)  11.5 us
    all_to_all x1, starting transfers between devices, mixer(): received = lax.all_to_all(signal, 'seq', 0, 0, tiled=True)  10.9 us
    all_to_all x1, waiting for transfers between devices, mixer(): gathered = lax.all_to_all(sums, 'head', 0, 0, tiled=True)  9.96 us
    all_to_all x1, waiting for transfers between devices, mixer(): returned = lax.all_to_all(filtered, 'seq', 0, 0, tiled=True)  7.36 us
    pallas_call x6, Pallas kernels, call(): pl.pallas_call(body, out_shape=out_shape, scratch_shapes=list(scratch), c...  6.64 us
    all_to_all x1, starting transfers between devices, mixer(): returned = lax.all_to_all(filtered, 'seq', 0, 0, tiled=True)  6.35 us
    all_to_all x1, waiting for transfers between devices, mixer(): received = lax.all_to_all(signal, 'seq', 0, 0, tiled=True)  6.15 us
  transfers between devices with their start and end apart: 6, of which 4 were waited for; matrix products, arithmetic and copies ran while one was open for 1% of the time, Pallas kernels for 11%

profile of v7, /device:TPU:56, one launch (start us, length us, event | category | flops | bytes accessed | tf_op | source)
XLA Modules:
  0.0 93.3 jit_solution(9200920577583333929)
XLA Ops:
  0.0 1.1 %pack.1 = bf16[512,512]{1,0:T(8,128)(2,1)S(1)} custom-call(bf16[256,512]{1,0:T(8,128)(2,1)} %key_ref.3, bf16[256,512]{1,0:T(8,128)(2,1)} %value_ref.3), custom_call_target="tpu_custom_call" | custom-call | tf_op jit(solution)/shard_map/pack/pallas_call | solution.py:115
  1.1 4.3 %collective-permute-start = (bf16[512,512]{1,0:T(8,128)(2,1)S(1)}, bf16[512,512]{1,0:T(8,128)(2,1)S(1)}, u32[]{:S(2)}, u32[]{:S(2)}) collective-permute-start(bf16[512,512]{1,0:T(8,128)(2,1)S(1)} %pack.1), channel_id=1, source_target_pairs={{0,16},{8,24},{16,32},{24,40},{32,48},{40,56},{48,64},{56,72},{64,... | collective-permute-start | bytes 1572872 | tf_op jit(solution)/shard_map/ppermute | solution.py:340
  5.4 16.3 %collective-permute-done.two_ref = bf16[512,512]{1,0:T(8,128)(2,1)S(1)} collective-permute-done((bf16[512,512]{1,0:T(8,128)(2,1)S(1)}, bf16[512,512]{1,0:T(8,128)(2,1)S(1)}, u32[]{:S(2)}, u32[]{:S(2)}) %collective-permute-start) | collective-permute-done | bytes 524320 | tf_op jit(solution)/shard_map/ppermute | solution.py:340
  21.7 1.9 %collective-permute-start.1 = (bf16[512,512]{1,0:T(8,128)(2,1)S(1)}, bf16[512,512]{1,0:T(8,128)(2,1)S(1)}, u32[]{:S(2)}, u32[]{:S(2)}) collective-permute-start(bf16[512,512]{1,0:T(8,128)(2,1)S(1)} %collective-permute-done.two_ref), channel_id=1, source_target_pairs={{0,8},{8,16},{16,24},{24,32},{32,40},{40,48},{48,56},{56,64},{64,7... | collective-permute-start | bytes 1572872 | tf_op jit(solution)/shard_map/ppermute | solution.py:341
  23.7 1.8 %shard_map.109 = bf16[64,2,1152]{2,1,0:T(2,128)(2,1)} custom-call(bf16[256,512]{1,0:T(8,128)(2,1)S(1)} %copy-done.7, bf16[256,512]{1,0:T(8,128)(2,1)S(1)} %copy-done.8, f32[8,512]{1,0:T(8,128)S(1)} %copy-done.10), custom_call_target="tpu_custom_call" | custom-call | tf_op jit(solution)/shard_map/pallas_call | solution.py:64
  25.4 10.9 %all-to-all-start = ((bf16[64,2,1152]{2,1,0:T(2,128)(2,1)}), bf16[64,2,1152]{2,1,0:T(2,128)(2,1)S(1)}, u32[]{:S(2)}, u32[]{:S(2)}) async-start(bf16[64,2,1152]{2,1,0:T(2,128)(2,1)} %shard_map.109), calls=%async_computation | async-start | bytes 589824 | tf_op jit(solution)/shard_map/all_to_all | solution.py:323
  36.3 0.0 collective-permute-done.1.three_ref
  36.4 0.8 copy-done.5
  37.2 0.1 slice_select_fusion.1
  37.2 0.0 copy-start
  37.2 0.8 pad_maximum_fusion
  38.1 2.0 %collective-permute-start.2 = (bf16[512,512]{1,0:T(8,128)(2,1)}, bf16[512,512]{1,0:T(8,128)(2,1)}, u32[]{:S(2)}, u32[]{:S(2)}) collective-permute-start(bf16[512,512]{1,0:T(8,128)(2,1)} %pad_maximum_fusion), channel_id=1, source_target_pairs={{0,8},{8,0},{16,24},{24,16},{32,40},{40,32},{48,56},{56,48},{64,72... | collective-permute-start | bytes 1572872 | tf_op jit(solution)/shard_map/ppermute | solution.py:347
  40.1 0.1 constant_dynamic-slice_fusion
  40.2 0.1 copy.13
  40.2 2.1 %kernel_spectrum.1.spec_ref = f32[1024,256]{1,0:T(8,128)S(1)} custom-call(f32[8,16384]{1,0:T(8,128)} %kernel_in.1, bf16[7,256,256]{2,1,0:T(8,128)(2,1)S(1)} %copy-done), custom_call_target="tpu_custom_call" | custom-call | tf_op jit(solution)/shard_map/kernel_spectrum/pallas_call | solution.py:326
  42.3 6.1 %all-to-all-done.signal_ref = bf16[64,2,1152]{2,1,0:T(2,128)(2,1)S(1)} async-done(((bf16[64,2,1152]{2,1,0:T(2,128)(2,1)}), bf16[64,2,1152]{2,1,0:T(2,128)(2,1)S(1)}, u32[]{:S(2)}, u32[]{:S(2)}) %all-to-all-start) | async-done | bytes 294944 | tf_op jit(solution)/shard_map/all_to_all | solution.py:323
  48.5 2.9 %shard_map.110 = bf16[64,8,256]{2,1,0:T(8,128)(2,1)S(1)} custom-call(bf16[64,2,1152]{2,1,0:T(2,128)(2,1)S(1)} %all-to-all-done.signal_ref, f32[8,8]{1,0:T(8,128)S(1)} %bitcast.4, f32[1024,256]{1,0:T(8,128)S(1)} %kernel_spectrum.1.spec_ref, bf16[7,256,256]{2,1,0:T(8,128)(2,1)S(1)} %copy-done), custom_call_target="tpu_custom_call" | custom-call | tf_op jit(solution)/shard_map/pallas_call | solution.py:64
  51.4 0.0 copy-start.3
  51.4 0.7 copy-done.3
  52.1 6.3 %all-to-all-start.1 = ((bf16[64,8,256]{2,1,0:T(8,128)(2,1)}), bf16[64,8,256]{2,1,0:T(8,128)(2,1)S(1)}, u32[]{:S(2)}, u32[]{:S(2)}) async-start(bf16[64,8,256]{2,1,0:T(8,128)(2,1)} %copy-done.3), calls=%async_computation.1 | async-start | bytes 524288 | tf_op jit(solution)/shard_map/all_to_all | solution.py:337
  58.5 0.0 copy-start.9
  58.5 0.1 shard_map.111.query_t_ref
  58.6 0.0 collective-permute-done.2.one_ref
  58.6 0.8 copy-done.9
  59.4 3.2 %attention.1 = (f32[256,512]{1,0:T(8,128)S(1)}, f32[128,256]{1,0:T(8,128)S(1)}) custom-call(s32[1]{0:T(128)} %bitcast.1.block_ref, bf16[256,512]{1,0:T(8,128)(2,1)S(1)} %copy-done.9, bf16[256,512]{1,0:T(8,128)(2,1)S(1)} %copy-done.1, bf16[256,512]{1,0:T(8,128)(2,1)S(1)} %copy-done.2, bf16[512,512]{1,0:T(8,128)(2,1)} %collective-permute-done.2.one_ref, ...), custom_call_target="tpu_custom_call" | custom-call | tf_op jit(solution)/shard_map/attention/pallas_call | solution.py:253
  62.6 7.4 %all-to-all-done.1.returned_ref = bf16[64,8,256]{2,1,0:T(8,128)(2,1)S(1)} async-done(((bf16[64,8,256]{2,1,0:T(8,128)(2,1)}), bf16[64,8,256]{2,1,0:T(8,128)(2,1)S(1)}, u32[]{:S(2)}, u32[]{:S(2)}) %all-to-all-start.1) | async-done | bytes 262176 | tf_op jit(solution)/shard_map/all_to_all | solution.py:337
  70.0 0.7 shard_map.112
  70.7 11.5 %all-to-all-start.2 = ((f32[8,4,128]{2,1,0:T(4,128)}), f32[8,4,128]{2,1,0:T(4,128)S(1)}, u32[]{:S(2)}, u32[]{:S(2)}) async-start(f32[8,4,128]{2,1,0:T(4,128)} %shard_map.112), calls=%async_computation.2 | async-start | bytes 32768 | tf_op jit(solution)/shard_map/all_to_all | solution.py:352
  82.2 0.1 shard_map.113.mixed_ref
  82.4 0.0 copy-start.12
  82.4 10.0 %all-to-all-done.2.sums_ref = f32[8,4,128]{2,1,0:T(4,128)S(1)} async-done(((f32[8,4,128]{2,1,0:T(4,128)}), f32[8,4,128]{2,1,0:T(4,128)S(1)}, u32[]{:S(2)}, u32[]{:S(2)}) %all-to-all-start.2) | async-done | bytes 16416 | tf_op jit(solution)/shard_map/all_to_all | solution.py:352
  92.3 1.0 %shard_map.114 = bf16[256,512]{1,0:T(8,128)(2,1)} custom-call(f32[8,4,128]{2,1,0:T(4,128)S(1)} %all-to-all-done.2.sums_ref, f32[256,512]{1,0:T(8,128)S(1)} %get-tuple-element.12.att_ref, f32[256,512]{1,0:T(8,128)S(1)} %shard_map.113.mixed_ref, f32[1,512]{1,0:T(1,128)S(1)} %bitcast.6), custom_call_target="tpu_custom_call" | custom-call | tf_op jit(solution)/shard_map/pallas_call | solution.py:64
  (19 shorter events, 0.0 us)
Async XLA Ops:
  0.0 23.6 %copy-start.10 = (f32[8,512]{1,0:T(8,128)S(1)}, f32[8,512]{1,0:T(8,128)}, u32[]{:S(2)}) copy-start(f32[8,512]{1,0:T(8,128)} %taps_ref.1) | copy-start | bytes 49156
  0.0 23.6 %copy-start.7 = (bf16[256,512]{1,0:T(8,128)(2,1)S(1)}, bf16[256,512]{1,0:T(8,128)(2,1)}, u32[]{:S(2)}) copy-start(bf16[256,512]{1,0:T(8,128)(2,1)} %key_ref.2) | copy-start | bytes 786436
  0.0 23.7 %copy-start.8 = (bf16[256,512]{1,0:T(8,128)(2,1)S(1)}, bf16[256,512]{1,0:T(8,128)(2,1)}, u32[]{:S(2)}) copy-start(bf16[256,512]{1,0:T(8,128)(2,1)} %value_ref.2) | copy-start | bytes 786436
  1.1 20.6 %collective-permute-start = (bf16[512,512]{1,0:T(8,128)(2,1)S(1)}, bf16[512,512]{1,0:T(8,128)(2,1)S(1)}, u32[]{:S(2)}, u32[]{:S(2)}) collective-permute-start(bf16[512,512]{1,0:T(8,128)(2,1)S(1)} %pack.1), channel_id=1, source_target_pairs={{0,16},{8,24},{16,32},{24,40},{32,48},{40,56},{48,64},{56,72},{64,... | collective-permute-start | bytes 1572872 | tf_op jit(solution)/shard_map/ppermute | solution.py:340
  21.7 14.6 %collective-permute-start.1 = (bf16[512,512]{1,0:T(8,128)(2,1)S(1)}, bf16[512,512]{1,0:T(8,128)(2,1)S(1)}, u32[]{:S(2)}, u32[]{:S(2)}) collective-permute-start(bf16[512,512]{1,0:T(8,128)(2,1)S(1)} %collective-permute-done.two_ref), channel_id=1, source_target_pairs={{0,8},{8,16},{16,24},{24,32},{32,40},{40,48},{48,56},{56,64},{64,7... | collective-permute-start | bytes 1572872 | tf_op jit(solution)/shard_map/ppermute | solution.py:341
  25.4 11.7 %copy-start.1 = (bf16[256,512]{1,0:T(8,128)(2,1)S(1)}, bf16[256,512]{1,0:T(8,128)(2,1)}, u32[]{:S(2)}) copy-start(bf16[256,512]{1,0:T(8,128)(2,1)} %key_ref.3) | copy-start | bytes 786436
  25.4 11.7 %copy-start.2 = (bf16[256,512]{1,0:T(8,128)(2,1)S(1)}, bf16[256,512]{1,0:T(8,128)(2,1)}, u32[]{:S(2)}) copy-start(bf16[256,512]{1,0:T(8,128)(2,1)} %value_ref.3) | copy-start | bytes 786436
  25.4 23.0 %all-to-all-start = ((bf16[64,2,1152]{2,1,0:T(2,128)(2,1)}), bf16[64,2,1152]{2,1,0:T(2,128)(2,1)S(1)}, u32[]{:S(2)}, u32[]{:S(2)}) async-start(bf16[64,2,1152]{2,1,0:T(2,128)(2,1)} %shard_map.109), calls=%async_computation | async-start | bytes 589824 | tf_op jit(solution)/shard_map/all_to_all | solution.py:323
  36.4 0.8 copy-start.5
  37.2 3.0 %copy-start = (bf16[7,256,256]{2,1,0:T(8,128)(2,1)S(1)}, bf16[7,256,256]{2,1,0:T(8,128)(2,1)}, u32[]{:S(2)}) copy-start(bf16[7,256,256]{2,1,0:T(8,128)(2,1)} %constant.27.clone.tables_ref) | copy-start | bytes 2752516
  38.1 20.6 %collective-permute-start.2 = (bf16[512,512]{1,0:T(8,128)(2,1)}, bf16[512,512]{1,0:T(8,128)(2,1)}, u32[]{:S(2)}, u32[]{:S(2)}) collective-permute-start(bf16[512,512]{1,0:T(8,128)(2,1)} %pad_maximum_fusion), channel_id=1, source_target_pairs={{0,8},{8,0},{16,24},{24,16},{32,40},{40,32},{48,56},{56,48},{64,72... | collective-permute-start | bytes 1572872 | tf_op jit(solution)/shard_map/ppermute | solution.py:347
  51.4 0.7 copy-start.3
  52.1 6.4 %copy-start.4 = (bf16[256,512]{1,0:T(8,128)(2,1)S(1)}, bf16[256,512]{1,0:T(8,128)(2,1)}, u32[]{:S(2)}) copy-start(bf16[256,512]{1,0:T(8,128)(2,1)} %query_ref.3) | copy-start | bytes 786436
  52.1 6.5 %copy-start.6 = (bf16[512,512]{1,0:T(8,128)(2,1)S(1)}, bf16[512,512]{1,0:T(8,128)(2,1)}, u32[]{:S(2)}) copy-start(bf16[512,512]{1,0:T(8,128)(2,1)} %copy-done.5) | copy-start | bytes 1572868
  52.1 17.9 %all-to-all-start.1 = ((bf16[64,8,256]{2,1,0:T(8,128)(2,1)}), bf16[64,8,256]{2,1,0:T(8,128)(2,1)S(1)}, u32[]{:S(2)}, u32[]{:S(2)}) async-start(bf16[64,8,256]{2,1,0:T(8,128)(2,1)} %copy-done.3), calls=%async_computation.1 | async-start | bytes 524288 | tf_op jit(solution)/shard_map/all_to_all | solution.py:337
  58.5 1.0 %copy-start.9 = (bf16[256,512]{1,0:T(8,128)(2,1)S(1)}, bf16[256,512]{1,0:T(8,128)(2,1)}, u32[]{:S(2)}) copy-start(bf16[256,512]{1,0:T(8,128)(2,1)} %query_ref.2) | copy-start | bytes 786436
  70.0 12.2 %copy-start.11 = (f32[512]{0:T(512)S(1)}, f32[512]{0:T(512)}, u32[]{:S(2)}) copy-start(f32[512]{0:T(512)} %param.20) | copy-start | bytes 6148
  70.7 21.6 %all-to-all-start.2 = ((f32[8,4,128]{2,1,0:T(4,128)}), f32[8,4,128]{2,1,0:T(4,128)S(1)}, u32[]{:S(2)}, u32[]{:S(2)}) async-start(f32[8,4,128]{2,1,0:T(4,128)} %shard_map.112), calls=%async_computation.2 | async-start | bytes 32768 | tf_op jit(solution)/shard_map/all_to_all | solution.py:352
  82.4 10.0 %copy-start.12 = (f32[512]{0:T(512)S(1)}, f32[512]{0:T(512)}, u32[]{:S(2)}) copy-start(f32[512]{0:T(512)} %param.19) | copy-start | bytes 6148
